TPU v7x, 512 devices: a whole 4x4x16 slice. The times are simulated.
512 devices in a mesh: tm: 4 (over y_hi, core), space: 128 (over x, z, y_lo).
Axes of the slice: x: 4, y: 4 (y_hi: 2, y_lo: 2; y = y_hi * 2 + y_lo), z: 16, core: 2. Of those that a mesh axis runs over, the one named last changes fastest.
Arguments:
- sources: bfloat16 [4, 2, 4, 3, 12, 128, 128], P('tm', None, None, None, None, 'space'), may hold values from -6 to 6
- gauge_links: bfloat16 [4, 4, 2, 3, 3, 128, 128], P(None, 'tm', None, None, None, 'space'), may hold values from -2.5 to 2.5
- eigenvectors: bfloat16 [4, 128, 2, 3, 128, 128], P('tm', None, None, None, 'space'), may hold values from -0.078125 to 0.078125
- elementals: float32 [4, 2, 128, 128], P('tm', None, 'space'), may hold values from -0.375 to 0.375
Outputs:
- projected: float32 [4, 2, 4, 12, 128], P('tm', None, None, None, 'space')
- contracted: float32 [4, 2, 4, 12, 128], P('tm', None, None, None, 'space')
All inputs are finite; a program needn't handle non-finite values.
Results may differ from a plain program's by a relative error of at most 0.0075.
Values may be sent and summed in bfloat16 or wider, within the bound.
No kernel may reach another device: no remote copies, remote signals or barrier semaphores. Data moves between devices by JAX's collectives and lax.ppermute only.
A program may use at most 64 MiB of HBM per device.

v0:
```python
import jax
import jax.numpy as jnp
from jax import lax
from jax.sharding import PartitionSpec as P

LX = 8


highest = lax.Precision.HIGHEST
hopping = 0.125


def from_behind(value, axis, steps):
    count = lax.axis_size(axis)
    pairs = [(source, (source + steps) % count) for source in range(count)]
    return lax.ppermute(value, axis, pairs)


def with_halo(array, sides, width):
    for axis, dim in sides:
        peers, length = (lax.axis_size(axis), array.shape[dim])
        up = [(i, (i + 1) % peers) for i in range(peers)]
        down = [(j, i) for i, j in up]
        last = lax.slice_in_dim(array, length - width, length, axis=dim)
        leading = lax.slice_in_dim(array, 0, width, axis=dim)
        before = lax.ppermute(last, axis, up)
        after = lax.ppermute(leading, axis, down)
        array = jnp.concatenate([before, array, after], axis=dim)
    return array


def times_unit(value, sign):
    return (-sign * value[1], sign * value[0])


def mult_block(direction, first, second):
    if direction == 0:
        return (times_unit(second, -1.0), times_unit(first, -1.0))
    if direction == 1:
        return ((-second[0], -second[1]), first)
    if direction == 2:
        return (times_unit(first, -1.0), times_unit(second, 1.0))
    return (first, second)


def half_spinor(direction, pair, sign):
    upper_a = (pair[0][:, 0], pair[1][:, 0])
    upper_b = (pair[0][:, 1], pair[1][:, 1])
    lower_a = (pair[0][:, 2], pair[1][:, 2])
    lower_b = (pair[0][:, 3], pair[1][:, 3])
    moved_a, moved_b = mult_block(direction, lower_a, lower_b)
    real_part = jnp.stack([upper_a[0] + sign * moved_a[0], upper_b[0] + sign * moved_b[0]], 1)
    imag_part = jnp.stack([upper_a[1] + sign * moved_a[1], upper_b[1] + sign * moved_b[1]], 1)
    return (real_part, imag_part)


def rebuild(direction, pair, sign):
    first = (pair[0][:, 0], pair[1][:, 0])
    second = (pair[0][:, 1], pair[1][:, 1])
    if direction == 3:
        lower_a = (sign * first[0], sign * first[1])
        lower_b = (sign * second[0], sign * second[1])
    else:
        moved_a, moved_b = mult_block(direction, first, second)
        lower_a = (-sign * moved_a[0], -sign * moved_a[1])
        lower_b = (-sign * moved_b[0], -sign * moved_b[1])
    real_part = jnp.stack([first[0], second[0], lower_a[0], lower_b[0]], 1)
    imag_part = jnp.stack([first[1], second[1], lower_a[1], lower_b[1]], 1)
    return (real_part, imag_part)


def color_apply(link_re, link_im, field_re, field_im, dagger):
    out_re = []
    out_im = []
    for row in range(3):
        acc_re = 0.0
        acc_im = 0.0
        for col in range(3):
            if dagger:
                entry_re = link_re[:, col, row][:, None, None]
                entry_im = -link_im[:, col, row][:, None, None]
            else:
                entry_re = link_re[:, row, col][:, None, None]
                entry_im = link_im[:, row, col][:, None, None]
            vec_re = field_re[:, :, col]
            vec_im = field_im[:, :, col]
            acc_re = acc_re + entry_re * vec_re - entry_im * vec_im
            acc_im = acc_im + entry_re * vec_im + entry_im * vec_re
        out_re.append(acc_re)
        out_im.append(acc_im)
    return (jnp.stack(out_re, 2), jnp.stack(out_im, 2))


def plane_shift(values, direction, stride, row_len):
    if direction == 1:
        return jnp.roll(values, -stride * row_len, axis=-1)
    column = jnp.arange(values.shape[-1]) % row_len
    if stride == 1:
        return jnp.where(
            column == row_len - 1, jnp.roll(values, row_len - 1, -1), jnp.roll(values, -1, -1)
        )
    return jnp.where(column == 0, jnp.roll(values, -(row_len - 1), -1), jnp.roll(values, 1, -1))


def split_parts(values):
    widened = values.astype(jnp.float32)
    return (widened[:, 0], widened[:, 1])


def stored(pair):
    return jnp.stack([pair[0], pair[1]], 1).astype(jnp.bfloat16)


def minus_chi(direction, pair):
    return stored(half_spinor(direction, pair, -1.0))


def plus_chi(direction, pair, link_pair):
    half = half_spinor(direction, pair, 1.0)
    return stored(color_apply(link_pair[0], link_pair[1], half[0], half[1], True))


def direction_term(direction, ahead, behind, link_pair):
    ahead_pair = split_parts(ahead)
    behind_pair = split_parts(behind)
    moved = color_apply(link_pair[0], link_pair[1], ahead_pair[0], ahead_pair[1], False)
    forward = rebuild(direction, moved, -1.0)
    backward = rebuild(direction, behind_pair, 1.0)
    return (forward[0] + backward[0], forward[1] + backward[1])


def contract(matrices, values):

    def product(left, right):
        return jnp.einsum("tkl,tasl->task", left, right, precision=highest)

    real_part = product(matrices[:, 0], values[:, 0]) - product(matrices[:, 1], values[:, 1])
    imag_part = product(matrices[:, 0], values[:, 1]) + product(matrices[:, 1], values[:, 0])
    return jnp.stack([real_part, imag_part], 1)


def local(sources, gauge_links, eigenvectors, elementals):
    tm_last = lax.axis_size("tm") - 1
    tm_index = lax.axis_index("tm")
    local_t = sources.shape[0]
    link_here = [split_parts(gauge_links[direction]) for direction in range(4)]
    below_t = from_behind(gauge_links[3], "tm", 1)
    below_z = from_behind(gauge_links[2], "space", 1)
    link_t_back = split_parts(jnp.concatenate([below_t, gauge_links[3][:-1]], 0))
    link_z_back = split_parts(jnp.concatenate([below_z, gauge_links[2][:, :, :, :, :-1, :]], 4))
    tpos = jnp.arange(local_t).reshape(-1, 1, 1, 1, 1, 1, 1)
    ahead_sign = jnp.where((tpos == local_t - 1) & (tm_index == tm_last), -1.0, 1.0)
    behind_sign = jnp.where((tpos == 0) & (tm_index == 0), -1.0, 1.0)
    current = sources
    for sweep in range(3):
        pair = split_parts(current)
        ahead = {}
        behind = {}
        for apply_direction in range(2):
            ahead[apply_direction] = plane_shift(
                minus_chi(apply_direction, pair), apply_direction, 1, LX
            )
            behind[apply_direction] = plane_shift(
                plus_chi(apply_direction, pair, link_here[apply_direction]), apply_direction, -1, LX
            )
        padded = with_halo(current, (("tm", 0), ("space", 5)), 1)
        along_t = padded[:, :, :, :, :, 1:-1, :].astype(jnp.float32)
        along_z = padded[1:-1]
        ahead[3] = minus_chi(3, split_parts(ahead_sign * along_t[2:]))
        behind[3] = plus_chi(3, split_parts(behind_sign * along_t[:-2]), link_t_back)
        ahead[2] = minus_chi(2, split_parts(along_z[:, :, :, :, :, 2:, :]))
        behind[2] = plus_chi(2, split_parts(along_z[:, :, :, :, :, :-2, :]), link_z_back)
        result_re = 0.0
        result_im = 0.0
        for apply_direction in range(4):
            term_re, term_im = direction_term(
                apply_direction,
                ahead[apply_direction],
                behind[apply_direction],
                link_here[apply_direction],
            )
            result_re = result_re + term_re
            result_im = result_im + term_im
        current = (
            sources.astype(jnp.float32) + hopping * jnp.stack([result_re, result_im], 1)
        ).astype(jnp.bfloat16)
    flipped = jnp.stack([current[:, 1], -current[:, 0]], 1)
    stacked = jnp.stack([current, flipped], 1)
    partial_value = jnp.einsum(
        "tkrczp,toracszp->toask", eigenvectors, stacked, preferred_element_type=jnp.float32
    )
    modes_dev = elementals.shape[2]
    totals = lax.psum(partial_value, "space")
    projected = lax.dynamic_slice_in_dim(totals, lax.axis_index("space") * modes_dev, modes_dev, 4)
    contracted = contract(elementals, totals)
    return (projected, contracted)


def solution(mesh):
    placed = (
        P("tm", None, None, None, None, "space", None),
        P(None, "tm", None, None, None, "space", None),
        P("tm", None, None, None, "space", None),
        P("tm", None, "space", None),
    )
    return jax.shard_map(
        local,
        mesh=mesh,
        in_specs=placed,
        out_specs=(P("tm", None, None, None, "space"), P("tm", None, None, None, "space")),
        check_vma=False,
    )
```

profile of v0, /device:TPU:16, one launch (start us, length us, event | category | flops | bytes accessed | tf_op | source)
XLA Modules:
  0.0 718.3 jit_solution(9376545102428188039)
XLA Ops:
  0.7 0.9 copy.6
  1.6 1.9 collective-permute-start
  3.5 5.1 collective-permute-start.1
  8.7 4.5 collective-permute-start.5
  13.2 1.9 collective-permute-start.3
  15.4 11.2 %collective-permute-done.3 = bf16[1,2,3,3,1,128]{5,1,3,2,4,0:T(2,128)(2,1)S(1)} collective-permute-done((bf16[1,2,3,3,1,128]{5,1,3,2,4,0:T(2,128)(2,1)S(1)}, bf16[1,2,3,3,1,128]{5,1,3,2,4,0:T(2,128)(2,1)S(1)}, u32[]{:S(2)}, u32[]{:S(2)}) %collective-permute-start.3) | collective-permute-done | bytes 4640 | tf_op jit(solution)/shard_map/ppermute | solution.py:16
  26.7 0.8 copy-done.1
  27.6 1.9 collective-permute-start.4
  29.6 8.1 %collective-permute-start.2 = (bf16[3,2,4,3,12,1,128]{6,4,3,2,5,1,0:T(8,128)(2,1)S(1)}, bf16[3,2,4,3,12,1,128]{6,4,3,2,5,1,0:T(8,128)(2,1)S(1)}, u32[]{:S(2)}, u32[]{:S(2)}) collective-permute-start(bf16[3,2,4,3,12,1,128]{6,4,3,2,5,1,0:T(8,128)(2,1)S(1)} %constant_dynamic-update-slice_fusion), channel_id=1, source_target_pairs={{1,0},{2,1},{3,2},{4,3},{5,4},{6,5},{7,6},{8,7},{9,8},{10,9},{11,1... | collective-permute-start | bytes 663560 | tf_op jit(solution)/shard_map/ppermute | solution.py:27
  40.2 3.1 collective-permute-done.4
  43.5 3.7 collective-permute-done.2
  47.6 1.9 collective-permute-start.6
  49.6 5.1 collective-permute-start.7
  57.4 1.9 collective-permute-start.9
  59.4 8.1 %collective-permute-start.8 = (bf16[3,2,4,3,12,1,128]{6,4,3,2,5,1,0:T(8,128)(2,1)S(1)}, bf16[3,2,4,3,12,1,128]{6,4,3,2,5,1,0:T(8,128)(2,1)S(1)}, u32[]{:S(2)}, u32[]{:S(2)}) collective-permute-start(bf16[3,2,4,3,12,1,128]{6,4,3,2,5,1,0:T(8,128)(2,1)S(1)} %get-tuple-element.83), channel_id=1, source_target_pairs={{1,0},{2,1},{3,2},{4,3},{5,4},{6,5},{7,6},{8,7},{9,8},{10,9},{11,1... | collective-permute-start | bytes 663560 | tf_op jit(solution)/shard_map/ppermute | solution.py:27
  67.7 5.7 collective-permute-done.9
  73.5 3.8 collective-permute-done.8
  77.9 1.9 collective-permute-start.10
  79.8 5.1 collective-permute-start.11
  87.7 1.9 collective-permute-start.13
  89.6 8.1 %collective-permute-start.12 = (bf16[3,2,4,3,12,1,128]{6,4,3,2,5,1,0:T(8,128)(2,1)S(1)}, bf16[3,2,4,3,12,1,128]{6,4,3,2,5,1,0:T(8,128)(2,1)S(1)}, u32[]{:S(2)}, u32[]{:S(2)}) collective-permute-start(bf16[3,2,4,3,12,1,128]{6,4,3,2,5,1,0:T(8,128)(2,1)S(1)} %copy.354), channel_id=1, source_target_pairs={{1,0},{2,1},{3,2},{4,3},{5,4},{6,5},{7,6},{8,7},{9,8},{10,9},{11,1... | collective-permute-start | bytes 663560 | tf_op jit(solution)/shard_map/ppermute | solution.py:27
  97.9 4.9 collective-permute-done.13
  103.0 3.8 collective-permute-done.12
  107.6 607.9 %psum.7 = f32[1,2,4,12,128]{4,3,2,1,0:T(8,128)S(1)} all-reduce(f32[1,2,4,12,128]{4,3,2,1,0:T(8,128)S(1)} %convolution_bitcast_fusion), channel_id=1, replica_groups=mesh['tm'=4,'space'=128] {'space'}, use_global_device_ids=true, to_apply=%region_0.1 | all-reduce | flops 12288 | bytes 98304 | tf_op jit(solution)/shard_map/psum | solution.py:193
  (389 shorter events, 11.5 us)
Async XLA Ops:
  0.6 106.8 %copy-start = (bf16[1,128,2,3,1,128]{5,2,4,3,1,0:T(2,128)(2,1)S(1)}, bf16[1,128,2,3,1,128]{5,2,4,3,1,0:T(2,128)(2,1)}, u32[]{:S(2)}) copy-start(bf16[1,128,2,3,1,128]{5,2,4,3,1,0:T(2,128)(2,1)} %param.6) | copy-start | bytes 589828
  0.6 8.0 %copy-start.2 = (bf16[4,1,2,3,3,1,128]{6,2,5,4,3,1,0:T(2,128)(2,1)S(1)}, bf16[4,1,2,3,3,1,128]{6,2,5,4,3,1,0:T(2,128)(2,1)}, u32[]{:S(2)}) copy-start(bf16[4,1,2,3,3,1,128]{6,2,5,4,3,1,0:T(2,128)(2,1)} %param.5) | copy-start | bytes 55300
  1.6 25.0 %collective-permute-start = (bf16[1,2,4,3,12,1,128]{6,4,3,2,5,1,0:T(8,128)(2,1)S(1)}, bf16[1,2,4,3,12,1,128]{6,4,3,2,5,1,0:T(8,128)(2,1)S(1)}, u32[]{:S(2)}, u32[]{:S(2)}) collective-permute-start(bf16[1,2,4,3,12,1,128]{6,4,3,2,5,1,0:T(8,128)(2,1)S(1)} %copy.6), channel_id=1, source_target_pairs={{0,128},{128,256},{256,384},{384,0},{1,129},{129,257},{257,385},{3... | collective-permute-start | bytes 221192 | tf_op jit(solution)/shard_map/ppermute | solution.py:26
  3.5 24.0 %collective-permute-start.1 = (bf16[1,2,4,3,12,1,128]{6,4,3,2,5,1,0:T(8,128)(2,1)S(1)}, bf16[1,2,4,3,12,1,128]{6,4,3,2,5,1,0:T(8,128)(2,1)S(1)}, u32[]{:S(2)}, u32[]{:S(2)}) collective-permute-start(bf16[1,2,4,3,12,1,128]{6,4,3,2,5,1,0:T(8,128)(2,1)S(1)} %copy.6), channel_id=1, source_target_pairs={{128,0},{256,128},{384,256},{0,384},{129,1},{257,129},{385,257},{1... | collective-permute-start | bytes 221192 | tf_op jit(solution)/shard_map/ppermute | solution.py:27
  8.7 6.6 collective-permute-start.5
  13.2 13.4 %collective-permute-start.3 = (bf16[1,2,3,3,1,128]{5,1,3,2,4,0:T(2,128)(2,1)S(1)}, bf16[1,2,3,3,1,128]{5,1,3,2,4,0:T(2,128)(2,1)S(1)}, u32[]{:S(2)}, u32[]{:S(2)}) collective-permute-start(bf16[1,2,3,3,1,128]{5,1,3,2,4,0:T(2,128)(2,1)S(1)} %get-tuple-element.530), channel_id=1, source_target_pairs={{0,1},{1,2},{2,3},{3,4},{4,5},{5,6},{6,7},{7,8},{8,9},{9,10},{10,1... | collective-permute-start | bytes 13832 | tf_op jit(solution)/shard_map/ppermute | solution.py:16
  26.6 0.9 copy-start.1
  27.6 15.6 %collective-permute-start.4 = (bf16[3,2,4,3,12,1,128]{6,4,3,2,5,1,0:T(8,128)(2,1)S(1)}, bf16[3,2,4,3,12,1,128]{6,4,3,2,5,1,0:T(8,128)(2,1)S(1)}, u32[]{:S(2)}, u32[]{:S(2)}) collective-permute-start(bf16[3,2,4,3,12,1,128]{6,4,3,2,5,1,0:T(8,128)(2,1)S(1)} %constant_dynamic-update-slice_fusion), channel_id=1, source_target_pairs={{0,1},{1,2},{2,3},{3,4},{4,5},{5,6},{6,7},{7,8},{8,9},{9,10},{10,1... | collective-permute-start | bytes 663560 | tf_op jit(solution)/shard_map/ppermute | solution.py:26
  29.6 17.6 %collective-permute-start.2 = (bf16[3,2,4,3,12,1,128]{6,4,3,2,5,1,0:T(8,128)(2,1)S(1)}, bf16[3,2,4,3,12,1,128]{6,4,3,2,5,1,0:T(8,128)(2,1)S(1)}, u32[]{:S(2)}, u32[]{:S(2)}) collective-permute-start(bf16[3,2,4,3,12,1,128]{6,4,3,2,5,1,0:T(8,128)(2,1)S(1)} %constant_dynamic-update-slice_fusion), channel_id=1, source_target_pairs={{1,0},{2,1},{3,2},{4,3},{5,4},{6,5},{7,6},{8,7},{9,8},{10,9},{11,1... | collective-permute-start | bytes 663560 | tf_op jit(solution)/shard_map/ppermute | solution.py:27
  47.6 9.1 %collective-permute-start.6 = (bf16[1,2,4,3,12,1,128]{6,4,3,2,5,1,0:T(8,128)(2,1)S(1)}, bf16[1,2,4,3,12,1,128]{6,4,3,2,5,1,0:T(8,128)(2,1)S(1)}, u32[]{:S(2)}, u32[]{:S(2)}) collective-permute-start(bf16[1,2,4,3,12,1,128]{6,4,3,2,5,1,0:T(8,128)(2,1)S(1)} %get-tuple-element.45), channel_id=1, source_target_pairs={{0,128},{128,256},{256,384},{384,0},{1,129},{129,257},{257,385},{3... | collective-permute-start | bytes 221192 | tf_op jit(solution)/shard_map/ppermute | solution.py:26
  49.6 7.3 %collective-permute-start.7 = (bf16[1,2,4,3,12,1,128]{6,4,3,2,5,1,0:T(8,128)(2,1)S(1)}, bf16[1,2,4,3,12,1,128]{6,4,3,2,5,1,0:T(8,128)(2,1)S(1)}, u32[]{:S(2)}, u32[]{:S(2)}) collective-permute-start(bf16[1,2,4,3,12,1,128]{6,4,3,2,5,1,0:T(8,128)(2,1)S(1)} %get-tuple-element.45), channel_id=1, source_target_pairs={{128,0},{256,128},{384,256},{0,384},{129,1},{257,129},{385,257},{1... | collective-permute-start | bytes 221192 | tf_op jit(solution)/shard_map/ppermute | solution.py:27
  57.4 15.9 %collective-permute-start.9 = (bf16[3,2,4,3,12,1,128]{6,4,3,2,5,1,0:T(8,128)(2,1)S(1)}, bf16[3,2,4,3,12,1,128]{6,4,3,2,5,1,0:T(8,128)(2,1)S(1)}, u32[]{:S(2)}, u32[]{:S(2)}) collective-permute-start(bf16[3,2,4,3,12,1,128]{6,4,3,2,5,1,0:T(8,128)(2,1)S(1)} %get-tuple-element.83), channel_id=1, source_target_pairs={{0,1},{1,2},{2,3},{3,4},{4,5},{5,6},{6,7},{7,8},{8,9},{9,10},{10,1... | collective-permute-start | bytes 663560 | tf_op jit(solution)/shard_map/ppermute | solution.py:26
  59.4 17.9 %collective-permute-start.8 = (bf16[3,2,4,3,12,1,128]{6,4,3,2,5,1,0:T(8,128)(2,1)S(1)}, bf16[3,2,4,3,12,1,128]{6,4,3,2,5,1,0:T(8,128)(2,1)S(1)}, u32[]{:S(2)}, u32[]{:S(2)}) collective-permute-start(bf16[3,2,4,3,12,1,128]{6,4,3,2,5,1,0:T(8,128)(2,1)S(1)} %get-tuple-element.83), channel_id=1, source_target_pairs={{1,0},{2,1},{3,2},{4,3},{5,4},{6,5},{7,6},{8,7},{9,8},{10,9},{11,1... | collective-permute-start | bytes 663560 | tf_op jit(solution)/shard_map/ppermute | solution.py:27
  77.9 9.1 %collective-permute-start.10 = (bf16[1,2,4,3,12,1,128]{6,4,1,3,2,5,0:T(8,128)(2,1)S(1)}, bf16[1,2,4,3,12,1,128]{6,4,1,3,2,5,0:T(8,128)(2,1)S(1)}, u32[]{:S(2)}, u32[]{:S(2)}) collective-permute-start(bf16[1,2,4,3,12,1,128]{6,4,1,3,2,5,0:T(8,128)(2,1)S(1)} %fusion.8), channel_id=1, source_target_pairs={{0,128},{128,256},{256,384},{384,0},{1,129},{129,257},{257,385},{3... | collective-permute-start | bytes 221192 | tf_op jit(solution)/shard_map/ppermute | solution.py:26
  79.8 7.3 %collective-permute-start.11 = (bf16[1,2,4,3,12,1,128]{6,4,1,3,2,5,0:T(8,128)(2,1)S(1)}, bf16[1,2,4,3,12,1,128]{6,4,1,3,2,5,0:T(8,128)(2,1)S(1)}, u32[]{:S(2)}, u32[]{:S(2)}) collective-permute-start(bf16[1,2,4,3,12,1,128]{6,4,1,3,2,5,0:T(8,128)(2,1)S(1)} %fusion.8), channel_id=1, source_target_pairs={{128,0},{256,128},{384,256},{0,384},{129,1},{257,129},{385,257},{1... | collective-permute-start | bytes 221192 | tf_op jit(solution)/shard_map/ppermute | solution.py:27
  87.7 15.1 %collective-permute-start.13 = (bf16[3,2,4,3,12,1,128]{6,4,3,2,5,1,0:T(8,128)(2,1)S(1)}, bf16[3,2,4,3,12,1,128]{6,4,3,2,5,1,0:T(8,128)(2,1)S(1)}, u32[]{:S(2)}, u32[]{:S(2)}) collective-permute-start(bf16[3,2,4,3,12,1,128]{6,4,3,2,5,1,0:T(8,128)(2,1)S(1)} %copy.354), channel_id=1, source_target_pairs={{0,1},{1,2},{2,3},{3,4},{4,5},{5,6},{6,7},{7,8},{8,9},{9,10},{10,1... | collective-permute-start | bytes 663560 | tf_op jit(solution)/shard_map/ppermute | solution.py:26
  89.6 17.1 %collective-permute-start.12 = (bf16[3,2,4,3,12,1,128]{6,4,3,2,5,1,0:T(8,128)(2,1)S(1)}, bf16[3,2,4,3,12,1,128]{6,4,3,2,5,1,0:T(8,128)(2,1)S(1)}, u32[]{:S(2)}, u32[]{:S(2)}) collective-permute-start(bf16[3,2,4,3,12,1,128]{6,4,3,2,5,1,0:T(8,128)(2,1)S(1)} %copy.354), channel_id=1, source_target_pairs={{1,0},{2,1},{3,2},{4,3},{5,4},{6,5},{7,6},{8,7},{9,8},{10,9},{11,1... | collective-permute-start | bytes 663560 | tf_op jit(solution)/shard_map/ppermute | solution.py:27
  107.6 607.9 %copy-start.3 = (f32[1,2,1,128]{3,2,1,0:T(1,128)S(1)}, f32[1,2,1,128]{3,2,1,0:T(1,128)}, u32[]{:S(2)}) copy-start(f32[1,2,1,128]{3,2,1,0:T(1,128)} %param.7) | copy-start | bytes 3076
where the time goes:
time: 719 us; the launch traced here: 718 us
  blocking collectives  608 us (85%)
  starting transfers between devices  57.8 us (8%)
  waiting for transfers between devices  36.3 us (5%)
  other arithmetic  8.04 us (1%)
    psum x1, blocking collectives, local(): totals = lax.psum(partial_value, 'space')  608 us
    ppermute x6, starting transfers between devices, with_halo(): after = lax.ppermute(leading, axis, down)  39.9 us
  transfers between devices with their start and end apart: 14, of which 9 were waited for; matrix products, arithmetic and copies ran while one was open for 1% of the time, Pallas kernels for 0%

commit v1 on v0

--- a/solution.py
+++ b/solution.py
@@ -1,9 +1,13 @@
 import jax
 import jax.numpy as jnp
 from jax import lax
+from jax.sharding import Mesh
 from jax.sharding import PartitionSpec as P
 
 LX = 8
+TM = ("y_hi", "core")
+SPACE = ("x", "z", "y_lo")
+PLANE = ("x", "y_lo")
 
 
 highest = lax.Precision.HIGHEST
@@ -129,6 +133,21 @@
     return (forward[0] + backward[0], forward[1] + backward[1])
 
 
+def exchange(value, axes):
+    return lax.all_to_all(value, axes, 0, 0, tiled=True)
+
+
+def all_reduce(partial_value):
+    plane = lax.axis_size(PLANE)
+    depth = lax.axis_size("z")
+    flat = partial_value.reshape(plane, -1, 128)
+    mine = exchange(flat, PLANE).sum(0)
+    copies = jnp.broadcast_to(mine, (depth, *mine.shape))
+    mine = exchange(copies, "z").sum(0)
+    copies = jnp.broadcast_to(mine, (plane, *mine.shape))
+    return exchange(copies, PLANE).reshape(partial_value.shape)
+
+
 def contract(matrices, values):
 
     def product(left, right):
@@ -140,12 +159,12 @@
 
 
 def local(sources, gauge_links, eigenvectors, elementals):
-    tm_last = lax.axis_size("tm") - 1
-    tm_index = lax.axis_index("tm")
+    tm_last = lax.axis_size(TM) - 1
+    tm_index = lax.axis_index(TM)
     local_t = sources.shape[0]
     link_here = [split_parts(gauge_links[direction]) for direction in range(4)]
-    below_t = from_behind(gauge_links[3], "tm", 1)
-    below_z = from_behind(gauge_links[2], "space", 1)
+    below_t = from_behind(gauge_links[3], TM, 1)
+    below_z = from_behind(gauge_links[2], SPACE, 1)
     link_t_back = split_parts(jnp.concatenate([below_t, gauge_links[3][:-1]], 0))
     link_z_back = split_parts(jnp.concatenate([below_z, gauge_links[2][:, :, :, :, :-1, :]], 4))
     tpos = jnp.arange(local_t).reshape(-1, 1, 1, 1, 1, 1, 1)
@@ -163,7 +182,7 @@
             behind[apply_direction] = plane_shift(
                 plus_chi(apply_direction, pair, link_here[apply_direction]), apply_direction, -1, LX
             )
-        padded = with_halo(current, (("tm", 0), ("space", 5)), 1)
+        padded = with_halo(current, ((TM, 0), (SPACE, 5)), 1)
         along_t = padded[:, :, :, :, :, 1:-1, :].astype(jnp.float32)
         along_z = padded[1:-1]
         ahead[3] = minus_chi(3, split_parts(ahead_sign * along_t[2:]))
@@ -190,23 +209,24 @@
         "tkrczp,toracszp->toask", eigenvectors, stacked, preferred_element_type=jnp.float32
     )
     modes_dev = elementals.shape[2]
-    totals = lax.psum(partial_value, "space")
-    projected = lax.dynamic_slice_in_dim(totals, lax.axis_index("space") * modes_dev, modes_dev, 4)
+    totals = all_reduce(partial_value)
+    projected = lax.dynamic_slice_in_dim(totals, lax.axis_index(SPACE) * modes_dev, modes_dev, 4)
     contracted = contract(elementals, totals)
     return (projected, contracted)
 
 
 def solution(mesh):
     placed = (
-        P("tm", None, None, None, None, "space", None),
-        P(None, "tm", None, None, None, "space", None),
-        P("tm", None, None, None, "space", None),
-        P("tm", None, "space", None),
+        P(TM, None, None, None, None, SPACE, None),
+        P(None, TM, None, None, None, SPACE, None),
+        P(TM, None, None, None, SPACE, None),
+        P(TM, None, SPACE, None),
     )
+    fine = Mesh(mesh.devices.reshape(2, 2, 4, 16, 2), (*TM, *SPACE))
     return jax.shard_map(
         local,
-        mesh=mesh,
+        mesh=fine,
         in_specs=placed,
-        out_specs=(P("tm", None, None, None, "space"), P("tm", None, None, None, "space")),
+        out_specs=(P(TM, None, None, None, SPACE), P(TM, None, None, None, SPACE)),
         check_vma=False,
     )

time: 719 us -> 152 us (0.21)
  the two profiles are of different devices: /device:TPU:16 before, /device:TPU:8 now
where the time goes in v1:
time: 152 us; the launch traced here: 151 us
  starting transfers between devices  59.6 us (39%)
  waiting for transfers between devices  34.6 us (23%)
  blocking collectives  28.1 us (18%)
  other arithmetic  20.4 us (13%)
  between operations  3.53 us (2%)
  local copies, waits for them, and re-layouts  3.42 us (2%)
  matrix products  1.59 us (1%)
    ppermute x6, starting transfers between devices, with_halo(): after = lax.ppermute(leading, axis, down)  36.5 us
    all_to_all x2, blocking collectives, exchange(): return lax.all_to_all(value, axes, 0, 0, tiled=True)  28.1 us
    ppermute x6, waiting for transfers between devices, with_halo(): after = lax.ppermute(leading, axis, down)  14.2 us
    ppermute x6, starting transfers between devices, with_halo(): before = lax.ppermute(last, axis, up)  13 us
    ppermute x6, waiting for transfers between devices, with_halo(): before = lax.ppermute(last, axis, up)  10.1 us
    ppermute x2, starting transfers between devices, from_behind(): return lax.ppermute(value, axis, pairs)  5.69 us
    ppermute x2, waiting for transfers between devices, from_behind(): return lax.ppermute(value, axis, pairs)  5.27 us
    all_to_all x1, waiting for transfers between devices, exchange(): return lax.all_to_all(value, axes, 0, 0, tiled=True)  5.09 us
  transfers between devices with their start and end apart: 15, of which 8 were waited for; matrix products, arithmetic and copies ran while one was open for 8% of the time, Pallas kernels for 0%

profile of v1, /device:TPU:8, one launch (start us, length us, event | category | flops | bytes accessed | tf_op | source)
XLA Modules:
  0.0 151.2 jit_solution(14394883824204038208)
XLA Ops:
  0.6 2.1 %collective-permute-start = (bf16[1,2,4,3,12,1,128]{6,2,5,4,3,1,0:T(4,128)(2,1)}, bf16[1,2,4,3,12,1,128]{6,2,5,4,3,1,0:T(4,128)(2,1)S(1)}, u32[]{:S(2)}, u32[]{:S(2)}) collective-permute-start(bf16[1,2,4,3,12,1,128]{6,2,5,4,3,1,0:T(4,128)(2,1)} %param.4), channel_id=1, source_target_pairs={{0,128},{128,256},{256,384},{384,0},{1,129},{129,257},{257,385},{3... | collective-permute-start | bytes 221192 | tf_op jit(solution)/shard_map/ppermute | solution.py:30
  2.7 5.1 %collective-permute-start.1 = (bf16[1,2,4,3,12,1,128]{6,2,5,4,3,1,0:T(4,128)(2,1)}, bf16[1,2,4,3,12,1,128]{6,2,5,4,3,1,0:T(4,128)(2,1)S(1)}, u32[]{:S(2)}, u32[]{:S(2)}) collective-permute-start(bf16[1,2,4,3,12,1,128]{6,2,5,4,3,1,0:T(4,128)(2,1)} %param.4), channel_id=1, source_target_pairs={{128,0},{256,128},{384,256},{0,384},{129,1},{257,129},{385,257},{1... | collective-permute-start | bytes 221192 | tf_op jit(solution)/shard_map/ppermute | solution.py:31
  8.6 1.9 %collective-permute-start.5 = (bf16[1,2,3,3,1,128]{5,1,3,2,4,0:T(2,128)(2,1)S(1)}, bf16[1,2,3,3,1,128]{5,1,3,2,4,0:T(2,128)(2,1)S(1)}, u32[]{:S(2)}, u32[]{:S(2)}) collective-permute-start(bf16[1,2,3,3,1,128]{5,1,3,2,4,0:T(2,128)(2,1)S(1)} %get-tuple-element.486), channel_id=1, source_target_pairs={{0,128},{128,256},{256,384},{384,0},{1,129},{129,257},{257,385},{3... | collective-permute-start | bytes 13832 | tf_op jit(solution)/shard_map/ppermute | solution.py:20
  10.6 3.8 %collective-permute-start.3 = (bf16[1,2,3,3,1,128]{5,1,3,2,4,0:T(2,128)(2,1)S(1)}, bf16[1,2,3,3,1,128]{5,1,3,2,4,0:T(2,128)(2,1)S(1)}, u32[]{:S(2)}, u32[]{:S(2)}) collective-permute-start(bf16[1,2,3,3,1,128]{5,1,3,2,4,0:T(2,128)(2,1)S(1)} %get-tuple-element.491), channel_id=1, source_target_pairs={{0,1},{1,2},{2,3},{3,4},{4,5},{5,6},{6,7},{7,8},{8,9},{9,10},{10,1... | collective-permute-start | bytes 13832 | tf_op jit(solution)/shard_map/ppermute | solution.py:20
  15.1 4.8 %collective-permute-done.3 = bf16[1,2,3,3,1,128]{5,1,3,2,4,0:T(2,128)(2,1)S(1)} collective-permute-done((bf16[1,2,3,3,1,128]{5,1,3,2,4,0:T(2,128)(2,1)S(1)}, bf16[1,2,3,3,1,128]{5,1,3,2,4,0:T(2,128)(2,1)S(1)}, u32[]{:S(2)}, u32[]{:S(2)}) %collective-permute-start.3) | collective-permute-done | bytes 4640 | tf_op jit(solution)/shard_map/ppermute | solution.py:20
  23.7 1.9 %collective-permute-start.4 = (bf16[3,2,4,3,12,1,128]{6,2,4,3,5,1,0:T(4,128)(2,1)S(1)}, bf16[3,2,4,3,12,1,128]{6,2,4,3,5,1,0:T(4,128)(2,1)S(1)}, u32[]{:S(2)}, u32[]{:S(2)}) collective-permute-start(bf16[3,2,4,3,12,1,128]{6,2,4,3,5,1,0:T(4,128)(2,1)S(1)} %bitcast.2677), channel_id=1, source_target_pairs={{0,1},{1,2},{2,3},{3,4},{4,5},{5,6},{6,7},{7,8},{8,9},{9,10},{10,1... | collective-permute-start | bytes 663560 | tf_op jit(solution)/shard_map/ppermute | solution.py:30
  25.6 9.3 %collective-permute-start.2 = (bf16[3,2,4,3,12,1,128]{6,2,4,3,5,1,0:T(4,128)(2,1)S(1)}, bf16[3,2,4,3,12,1,128]{6,2,4,3,5,1,0:T(4,128)(2,1)S(1)}, u32[]{:S(2)}, u32[]{:S(2)}) collective-permute-start(bf16[3,2,4,3,12,1,128]{6,2,4,3,5,1,0:T(4,128)(2,1)S(1)} %bitcast.2678), channel_id=1, source_target_pairs={{1,0},{2,1},{3,2},{4,3},{5,4},{6,5},{7,6},{8,7},{9,8},{10,9},{11,1... | collective-permute-start | bytes 663560 | tf_op jit(solution)/shard_map/ppermute | solution.py:31
  37.2 7.6 %collective-permute-done.2 = bf16[3,2,4,3,12,1,128]{6,2,4,3,5,1,0:T(4,128)(2,1)S(1)} collective-permute-done((bf16[3,2,4,3,12,1,128]{6,2,4,3,5,1,0:T(4,128)(2,1)S(1)}, bf16[3,2,4,3,12,1,128]{6,2,4,3,5,1,0:T(4,128)(2,1)S(1)}, u32[]{:S(2)}, u32[]{:S(2)}) %collective-permute-start.2) | collective-permute-done | bytes 221216 | tf_op jit(solution)/shard_map/ppermute | solution.py:31
  47.0 2.6 %collective-permute-start.6 = (bf16[1,2,4,3,12,1,128]{6,2,4,3,5,1,0:T(4,128)(2,1)S(1)}, bf16[1,2,4,3,12,1,128]{6,2,4,3,5,1,0:T(4,128)(2,1)S(1)}, u32[]{:S(2)}, u32[]{:S(2)}) collective-permute-start(bf16[1,2,4,3,12,1,128]{6,2,4,3,5,1,0:T(4,128)(2,1)S(1)} %get-tuple-element.56), channel_id=1, source_target_pairs={{0,128},{128,256},{256,384},{384,0},{1,129},{129,257},{257,385},{3... | collective-permute-start | bytes 221192 | tf_op jit(solution)/shard_map/ppermute | solution.py:30
  49.6 4.7 %collective-permute-start.7 = (bf16[1,2,4,3,12,1,128]{6,2,4,3,5,1,0:T(4,128)(2,1)S(1)}, bf16[1,2,4,3,12,1,128]{6,2,4,3,5,1,0:T(4,128)(2,1)S(1)}, u32[]{:S(2)}, u32[]{:S(2)}) collective-permute-start(bf16[1,2,4,3,12,1,128]{6,2,4,3,5,1,0:T(4,128)(2,1)S(1)} %get-tuple-element.56), channel_id=1, source_target_pairs={{128,0},{256,128},{384,256},{0,384},{129,1},{257,129},{385,257},{1... | collective-permute-start | bytes 221192 | tf_op jit(solution)/shard_map/ppermute | solution.py:31
  59.2 4.4 %collective-permute-start.8 = (bf16[3,2,4,3,12,1,128]{6,2,4,3,5,1,0:T(4,128)(2,1)S(1)}, bf16[3,2,4,3,12,1,128]{6,2,4,3,5,1,0:T(4,128)(2,1)S(1)}, u32[]{:S(2)}, u32[]{:S(2)}) collective-permute-start(bf16[3,2,4,3,12,1,128]{6,2,4,3,5,1,0:T(4,128)(2,1)S(1)} %get-tuple-element.89), channel_id=1, source_target_pairs={{1,0},{2,1},{3,2},{4,3},{5,4},{6,5},{7,6},{8,7},{9,8},{10,9},{11,1... | collective-permute-start | bytes 663560 | tf_op jit(solution)/shard_map/ppermute | solution.py:31
  63.6 2.4 %collective-permute-start.9 = (bf16[3,2,4,3,12,1,128]{6,2,4,3,5,1,0:T(4,128)(2,1)S(1)}, bf16[3,2,4,3,12,1,128]{6,2,4,3,5,1,0:T(4,128)(2,1)S(1)}, u32[]{:S(2)}, u32[]{:S(2)}) collective-permute-start(bf16[3,2,4,3,12,1,128]{6,2,4,3,5,1,0:T(4,128)(2,1)S(1)} %get-tuple-element.89), channel_id=1, source_target_pairs={{0,1},{1,2},{2,3},{3,4},{4,5},{5,6},{6,7},{7,8},{8,9},{9,10},{10,1... | collective-permute-start | bytes 663560 | tf_op jit(solution)/shard_map/ppermute | solution.py:30
  66.2 3.6 %collective-permute-done.8 = bf16[3,2,4,3,12,1,128]{6,2,4,3,5,1,0:T(4,128)(2,1)S(1)} collective-permute-done((bf16[3,2,4,3,12,1,128]{6,2,4,3,5,1,0:T(4,128)(2,1)S(1)}, bf16[3,2,4,3,12,1,128]{6,2,4,3,5,1,0:T(4,128)(2,1)S(1)}, u32[]{:S(2)}, u32[]{:S(2)}) %collective-permute-start.8) | collective-permute-done | bytes 221216 | tf_op jit(solution)/shard_map/ppermute | solution.py:31
  70.3 6.4 %collective-permute-done.9 = bf16[3,2,4,3,12,1,128]{6,2,4,3,5,1,0:T(4,128)(2,1)S(1)} collective-permute-done((bf16[3,2,4,3,12,1,128]{6,2,4,3,5,1,0:T(4,128)(2,1)S(1)}, bf16[3,2,4,3,12,1,128]{6,2,4,3,5,1,0:T(4,128)(2,1)S(1)}, u32[]{:S(2)}, u32[]{:S(2)}) %collective-permute-start.9) | collective-permute-done | bytes 221216 | tf_op jit(solution)/shard_map/ppermute | solution.py:30
  78.4 1.9 %collective-permute-start.10 = (bf16[1,2,4,3,12,1,128]{6,2,4,3,5,1,0:T(4,128)(2,1)S(1)}, bf16[1,2,4,3,12,1,128]{6,2,4,3,5,1,0:T(4,128)(2,1)S(1)}, u32[]{:S(2)}, u32[]{:S(2)}) collective-permute-start(bf16[1,2,4,3,12,1,128]{6,2,4,3,5,1,0:T(4,128)(2,1)S(1)} %get-tuple-element.33), channel_id=1, source_target_pairs={{0,128},{128,256},{256,384},{384,0},{1,129},{129,257},{257,385},{3... | collective-permute-start | bytes 221192 | tf_op jit(solution)/shard_map/ppermute | solution.py:30
  80.3 5.1 %collective-permute-start.11 = (bf16[1,2,4,3,12,1,128]{6,2,4,3,5,1,0:T(4,128)(2,1)S(1)}, bf16[1,2,4,3,12,1,128]{6,2,4,3,5,1,0:T(4,128)(2,1)S(1)}, u32[]{:S(2)}, u32[]{:S(2)}) collective-permute-start(bf16[1,2,4,3,12,1,128]{6,2,4,3,5,1,0:T(4,128)(2,1)S(1)} %get-tuple-element.33), channel_id=1, source_target_pairs={{128,0},{256,128},{384,256},{0,384},{129,1},{257,129},{385,257},{1... | collective-permute-start | bytes 221192 | tf_op jit(solution)/shard_map/ppermute | solution.py:31
  90.5 7.9 %collective-permute-start.12 = (bf16[3,2,4,3,12,1,128]{6,2,4,3,5,1,0:T(4,128)(2,1)S(1)}, bf16[3,2,4,3,12,1,128]{6,2,4,3,5,1,0:T(4,128)(2,1)S(1)}, u32[]{:S(2)}, u32[]{:S(2)}) collective-permute-start(bf16[3,2,4,3,12,1,128]{6,2,4,3,5,1,0:T(4,128)(2,1)S(1)} %get-tuple-element.87), channel_id=1, source_target_pairs={{1,0},{2,1},{3,2},{4,3},{5,4},{6,5},{7,6},{8,7},{9,8},{10,9},{11,1... | collective-permute-start | bytes 663560 | tf_op jit(solution)/shard_map/ppermute | solution.py:31
  98.3 2.1 %collective-permute-start.13 = (bf16[3,2,4,3,12,1,128]{6,2,4,3,5,1,0:T(4,128)(2,1)S(1)}, bf16[3,2,4,3,12,1,128]{6,2,4,3,5,1,0:T(4,128)(2,1)S(1)}, u32[]{:S(2)}, u32[]{:S(2)}) collective-permute-start(bf16[3,2,4,3,12,1,128]{6,2,4,3,5,1,0:T(4,128)(2,1)S(1)} %get-tuple-element.87), channel_id=1, source_target_pairs={{0,1},{1,2},{2,3},{3,4},{4,5},{5,6},{6,7},{7,8},{8,9},{9,10},{10,1... | collective-permute-start | bytes 663560 | tf_op jit(solution)/shard_map/ppermute | solution.py:30
  100.8 3.0 %collective-permute-done.12 = bf16[3,2,4,3,12,1,128]{6,2,4,3,5,1,0:T(4,128)(2,1)S(1)} collective-permute-done((bf16[3,2,4,3,12,1,128]{6,2,4,3,5,1,0:T(4,128)(2,1)S(1)}, bf16[3,2,4,3,12,1,128]{6,2,4,3,5,1,0:T(4,128)(2,1)S(1)}, u32[]{:S(2)}, u32[]{:S(2)}) %collective-permute-start.12) | collective-permute-done | bytes 221216 | tf_op jit(solution)/shard_map/ppermute | solution.py:31
  104.3 3.6 %collective-permute-done.13 = bf16[3,2,4,3,12,1,128]{6,2,4,3,5,1,0:T(4,128)(2,1)S(1)} collective-permute-done((bf16[3,2,4,3,12,1,128]{6,2,4,3,5,1,0:T(4,128)(2,1)S(1)}, bf16[3,2,4,3,12,1,128]{6,2,4,3,5,1,0:T(4,128)(2,1)S(1)}, u32[]{:S(2)}, u32[]{:S(2)}) %collective-permute-start.13) | collective-permute-done | bytes 221216 | tf_op jit(solution)/shard_map/ppermute | solution.py:30
  110.1 11.9 %all_to_all.15 = f32[8,12,128]{2,1,0:T(8,128)S(1)} all-to-all(f32[8,12,128]{2,1,0:T(8,128)S(1)} %convolution_bitcast_fusion), channel_id=1, replica_groups=mesh['y_hi'=2,'core'=2,'x'=4,'z'=16,'y_lo'=2] {'x','y_lo'}, dimensions={0} | all-to-all | bytes 98304 | tf_op jit(solution)/shard_map/all_to_all | solution.py:137
  122.1 16.2 %all_to_all.16 = f32[16,12,128]{2,1,0:T(8,128)S(1)} all-to-all(f32[16,12,128]{2,1,0:T(8,128)S(1)} %broadcast_in_dim.33), channel_id=1, replica_groups=mesh['y_hi'=2,'core'=2,'x'=4,'z'=16,'y_lo'=2] {'z'}, dimensions={0} | all-to-all | bytes 196608 | tf_op jit(solution)/shard_map/all_to_all | solution.py:137
  138.9 4.4 %all-to-all-start.2 = ((f32[8,12,128]{2,1,0:T(8,128)}), f32[8,12,128]{2,1,0:T(8,128)S(1)}, u32[]{:S(2)}, u32[]{:S(2)}) async-start(f32[8,12,128]{2,1,0:T(8,128)} %broadcast_in_dim.34), calls=%async_computation.2 | async-start | bytes 131072 | tf_op jit(solution)/shard_map/all_to_all | solution.py:137
  143.3 5.1 %all-to-all-done.2 = f32[8,12,128]{2,1,0:T(8,128)S(1)} async-done(((f32[8,12,128]{2,1,0:T(8,128)}), f32[8,12,128]{2,1,0:T(8,128)S(1)}, u32[]{:S(2)}, u32[]{:S(2)}) %all-to-all-start.2) | async-done | bytes 49184 | tf_op jit(solution)/shard_map/all_to_all | solution.py:137
  (419 shorter events, 25.9 us)
Async XLA Ops:
  0.6 109.2 %copy-start = (bf16[1,128,2,3,1,128]{5,2,4,3,1,0:T(2,128)(2,1)S(1)}, bf16[1,128,2,3,1,128]{5,2,4,3,1,0:T(2,128)(2,1)}, u32[]{:S(2)}) copy-start(bf16[1,128,2,3,1,128]{5,2,4,3,1,0:T(2,128)(2,1)} %param.6) | copy-start | bytes 589828
  0.6 19.3 %collective-permute-start = (bf16[1,2,4,3,12,1,128]{6,2,5,4,3,1,0:T(4,128)(2,1)}, bf16[1,2,4,3,12,1,128]{6,2,5,4,3,1,0:T(4,128)(2,1)S(1)}, u32[]{:S(2)}, u32[]{:S(2)}) collective-permute-start(bf16[1,2,4,3,12,1,128]{6,2,5,4,3,1,0:T(4,128)(2,1)} %param.4), channel_id=1, source_target_pairs={{0,128},{128,256},{256,384},{384,0},{1,129},{129,257},{257,385},{3... | collective-permute-start | bytes 221192 | tf_op jit(solution)/shard_map/ppermute | solution.py:30
  2.7 18.1 %collective-permute-start.1 = (bf16[1,2,4,3,12,1,128]{6,2,5,4,3,1,0:T(4,128)(2,1)}, bf16[1,2,4,3,12,1,128]{6,2,5,4,3,1,0:T(4,128)(2,1)S(1)}, u32[]{:S(2)}, u32[]{:S(2)}) collective-permute-start(bf16[1,2,4,3,12,1,128]{6,2,5,4,3,1,0:T(4,128)(2,1)} %param.4), channel_id=1, source_target_pairs={{128,0},{256,128},{384,256},{0,384},{129,1},{257,129},{385,257},{1... | collective-permute-start | bytes 221192 | tf_op jit(solution)/shard_map/ppermute | solution.py:31
  8.6 6.4 %collective-permute-start.5 = (bf16[1,2,3,3,1,128]{5,1,3,2,4,0:T(2,128)(2,1)S(1)}, bf16[1,2,3,3,1,128]{5,1,3,2,4,0:T(2,128)(2,1)S(1)}, u32[]{:S(2)}, u32[]{:S(2)}) collective-permute-start(bf16[1,2,3,3,1,128]{5,1,3,2,4,0:T(2,128)(2,1)S(1)} %get-tuple-element.486), channel_id=1, source_target_pairs={{0,128},{128,256},{256,384},{384,0},{1,129},{129,257},{257,385},{3... | collective-permute-start | bytes 13832 | tf_op jit(solution)/shard_map/ppermute | solution.py:20
  10.6 9.3 %collective-permute-start.3 = (bf16[1,2,3,3,1,128]{5,1,3,2,4,0:T(2,128)(2,1)S(1)}, bf16[1,2,3,3,1,128]{5,1,3,2,4,0:T(2,128)(2,1)S(1)}, u32[]{:S(2)}, u32[]{:S(2)}) collective-permute-start(bf16[1,2,3,3,1,128]{5,1,3,2,4,0:T(2,128)(2,1)S(1)} %get-tuple-element.491), channel_id=1, source_target_pairs={{0,1},{1,2},{2,3},{3,4},{4,5},{5,6},{6,7},{7,8},{8,9},{9,10},{10,1... | collective-permute-start | bytes 13832 | tf_op jit(solution)/shard_map/ppermute | solution.py:20
  19.9 0.9 copy-start.1
  23.7 21.8 %collective-permute-start.4 = (bf16[3,2,4,3,12,1,128]{6,2,4,3,5,1,0:T(4,128)(2,1)S(1)}, bf16[3,2,4,3,12,1,128]{6,2,4,3,5,1,0:T(4,128)(2,1)S(1)}, u32[]{:S(2)}, u32[]{:S(2)}) collective-permute-start(bf16[3,2,4,3,12,1,128]{6,2,4,3,5,1,0:T(4,128)(2,1)S(1)} %bitcast.2677), channel_id=1, source_target_pairs={{0,1},{1,2},{2,3},{3,4},{4,5},{5,6},{6,7},{7,8},{8,9},{9,10},{10,1... | collective-permute-start | bytes 663560 | tf_op jit(solution)/shard_map/ppermute | solution.py:30
  25.6 19.3 %collective-permute-start.2 = (bf16[3,2,4,3,12,1,128]{6,2,4,3,5,1,0:T(4,128)(2,1)S(1)}, bf16[3,2,4,3,12,1,128]{6,2,4,3,5,1,0:T(4,128)(2,1)S(1)}, u32[]{:S(2)}, u32[]{:S(2)}) collective-permute-start(bf16[3,2,4,3,12,1,128]{6,2,4,3,5,1,0:T(4,128)(2,1)S(1)} %bitcast.2678), channel_id=1, source_target_pairs={{1,0},{2,1},{3,2},{4,3},{5,4},{6,5},{7,6},{8,7},{9,8},{10,9},{11,1... | collective-permute-start | bytes 663560 | tf_op jit(solution)/shard_map/ppermute | solution.py:31
  47.0 11.0 %collective-permute-start.6 = (bf16[1,2,4,3,12,1,128]{6,2,4,3,5,1,0:T(4,128)(2,1)S(1)}, bf16[1,2,4,3,12,1,128]{6,2,4,3,5,1,0:T(4,128)(2,1)S(1)}, u32[]{:S(2)}, u32[]{:S(2)}) collective-permute-start(bf16[1,2,4,3,12,1,128]{6,2,4,3,5,1,0:T(4,128)(2,1)S(1)} %get-tuple-element.56), channel_id=1, source_target_pairs={{0,128},{128,256},{256,384},{384,0},{1,129},{129,257},{257,385},{3... | collective-permute-start | bytes 221192 | tf_op jit(solution)/shard_map/ppermute | solution.py:30
  49.6 8.4 %collective-permute-start.7 = (bf16[1,2,4,3,12,1,128]{6,2,4,3,5,1,0:T(4,128)(2,1)S(1)}, bf16[1,2,4,3,12,1,128]{6,2,4,3,5,1,0:T(4,128)(2,1)S(1)}, u32[]{:S(2)}, u32[]{:S(2)}) collective-permute-start(bf16[1,2,4,3,12,1,128]{6,2,4,3,5,1,0:T(4,128)(2,1)S(1)} %get-tuple-element.56), channel_id=1, source_target_pairs={{128,0},{256,128},{384,256},{0,384},{129,1},{257,129},{385,257},{1... | collective-permute-start | bytes 221192 | tf_op jit(solution)/shard_map/ppermute | solution.py:31
  59.2 10.7 %collective-permute-start.8 = (bf16[3,2,4,3,12,1,128]{6,2,4,3,5,1,0:T(4,128)(2,1)S(1)}, bf16[3,2,4,3,12,1,128]{6,2,4,3,5,1,0:T(4,128)(2,1)S(1)}, u32[]{:S(2)}, u32[]{:S(2)}) collective-permute-start(bf16[3,2,4,3,12,1,128]{6,2,4,3,5,1,0:T(4,128)(2,1)S(1)} %get-tuple-element.89), channel_id=1, source_target_pairs={{1,0},{2,1},{3,2},{4,3},{5,4},{6,5},{7,6},{8,7},{9,8},{10,9},{11,1... | collective-permute-start | bytes 663560 | tf_op jit(solution)/shard_map/ppermute | solution.py:31
  63.6 13.2 %collective-permute-start.9 = (bf16[3,2,4,3,12,1,128]{6,2,4,3,5,1,0:T(4,128)(2,1)S(1)}, bf16[3,2,4,3,12,1,128]{6,2,4,3,5,1,0:T(4,128)(2,1)S(1)}, u32[]{:S(2)}, u32[]{:S(2)}) collective-permute-start(bf16[3,2,4,3,12,1,128]{6,2,4,3,5,1,0:T(4,128)(2,1)S(1)} %get-tuple-element.89), channel_id=1, source_target_pairs={{0,1},{1,2},{2,3},{3,4},{4,5},{5,6},{6,7},{7,8},{8,9},{9,10},{10,1... | collective-permute-start | bytes 663560 | tf_op jit(solution)/shard_map/ppermute | solution.py:30
  78.4 10.9 %collective-permute-start.10 = (bf16[1,2,4,3,12,1,128]{6,2,4,3,5,1,0:T(4,128)(2,1)S(1)}, bf16[1,2,4,3,12,1,128]{6,2,4,3,5,1,0:T(4,128)(2,1)S(1)}, u32[]{:S(2)}, u32[]{:S(2)}) collective-permute-start(bf16[1,2,4,3,12,1,128]{6,2,4,3,5,1,0:T(4,128)(2,1)S(1)} %get-tuple-element.33), channel_id=1, source_target_pairs={{0,128},{128,256},{256,384},{384,0},{1,129},{129,257},{257,385},{3... | collective-permute-start | bytes 221192 | tf_op jit(solution)/shard_map/ppermute | solution.py:30
  80.3 9.0 %collective-permute-start.11 = (bf16[1,2,4,3,12,1,128]{6,2,4,3,5,1,0:T(4,128)(2,1)S(1)}, bf16[1,2,4,3,12,1,128]{6,2,4,3,5,1,0:T(4,128)(2,1)S(1)}, u32[]{:S(2)}, u32[]{:S(2)}) collective-permute-start(bf16[1,2,4,3,12,1,128]{6,2,4,3,5,1,0:T(4,128)(2,1)S(1)} %get-tuple-element.33), channel_id=1, source_target_pairs={{128,0},{256,128},{384,256},{0,384},{129,1},{257,129},{385,257},{1... | collective-permute-start | bytes 221192 | tf_op jit(solution)/shard_map/ppermute | solution.py:31
  90.5 13.3 %collective-permute-start.12 = (bf16[3,2,4,3,12,1,128]{6,2,4,3,5,1,0:T(4,128)(2,1)S(1)}, bf16[3,2,4,3,12,1,128]{6,2,4,3,5,1,0:T(4,128)(2,1)S(1)}, u32[]{:S(2)}, u32[]{:S(2)}) collective-permute-start(bf16[3,2,4,3,12,1,128]{6,2,4,3,5,1,0:T(4,128)(2,1)S(1)} %get-tuple-element.87), channel_id=1, source_target_pairs={{1,0},{2,1},{3,2},{4,3},{5,4},{6,5},{7,6},{8,7},{9,8},{10,9},{11,1... | collective-permute-start | bytes 663560 | tf_op jit(solution)/shard_map/ppermute | solution.py:31
  98.3 9.6 %collective-permute-start.13 = (bf16[3,2,4,3,12,1,128]{6,2,4,3,5,1,0:T(4,128)(2,1)S(1)}, bf16[3,2,4,3,12,1,128]{6,2,4,3,5,1,0:T(4,128)(2,1)S(1)}, u32[]{:S(2)}, u32[]{:S(2)}) collective-permute-start(bf16[3,2,4,3,12,1,128]{6,2,4,3,5,1,0:T(4,128)(2,1)S(1)} %get-tuple-element.87), channel_id=1, source_target_pairs={{0,1},{1,2},{2,3},{3,4},{4,5},{5,6},{6,7},{7,8},{8,9},{9,10},{10,1... | collective-permute-start | bytes 663560 | tf_op jit(solution)/shard_map/ppermute | solution.py:30
  138.9 9.5 %all-to-all-start.2 = ((f32[8,12,128]{2,1,0:T(8,128)}), f32[8,12,128]{2,1,0:T(8,128)S(1)}, u32[]{:S(2)}, u32[]{:S(2)}) async-start(f32[8,12,128]{2,1,0:T(8,128)} %broadcast_in_dim.34), calls=%async_computation.2 | async-start | bytes 131072 | tf_op jit(solution)/shard_map/all_to_all | solution.py:137
  143.3 5.1 %copy-start.2 = (f32[1,2,1,128]{3,2,1,0:T(1,128)S(1)}, f32[1,2,1,128]{3,2,1,0:T(1,128)}, u32[]{:S(2)}) copy-start(f32[1,2,1,128]{3,2,1,0:T(1,128)} %param.7) | copy-start | bytes 3076

commit v2 on v1

v2 whole, which is shorter than its diff:
```python
import functools

import jax
import jax.numpy as jnp
from jax import lax
from jax.experimental import pallas as pl
from jax.experimental.pallas import tpu as pltpu
from jax.sharding import Mesh
from jax.sharding import PartitionSpec as P

HOPPING = 0.125
TM = ("y_hi", "core")
SPACE = ("x", "z", "y_lo")
PLANE = ("x", "y_lo")
POSITION = ("x", "z")
BLOCK = ("y_lo", "y_hi", "core")
LX = 8
FIELD = 48
LINK = 72
ROWS = FIELD + LINK
SITES = 128
F32 = jnp.float32
BF16 = jnp.bfloat16


def exchange(value, axes):
    return lax.all_to_all(value, axes, 0, 0, tiled=True)


def from_behind(value, axes, steps):
    count = lax.axis_size(axes)
    return lax.ppermute(value, axes, [(i, (i + steps) % count) for i in range(count)])


def local_call(kernel, outs, scratch, flops):
    return pl.pallas_call(
        kernel,
        out_shape=outs,
        scratch_shapes=scratch,
        compiler_params=pltpu.CompilerParams(vmem_limit_bytes=16 << 20),
        cost_estimate=pl.CostEstimate(flops=flops, bytes_accessed=1 << 20, transcendentals=0),
    )


def pack_kernel(source_ref, link_ref, out_ref, rows, links):
    for entry in range(36):
        links[2 * entry : 2 * entry + 2] = link_ref[entry].astype(F32)
    shared = links[...]
    for target in range(8):
        for part in range(2):
            for color in range(3):
                for which in range(2):
                    at = part * 24 + color * 8 + which * 4
                    if target < 6:
                        piece = source_ref[part, color, 2 * target + which].astype(F32)
                    else:
                        piece = jnp.zeros((4, SITES), F32)
                    rows[target, at : at + 4] = piece
        rows[target, FIELD:] = shared
    out_ref[...] = rows[...].astype(BF16)


def signed_add(base, sign, value):
    if base is None:
        return value if sign > 0 else -value
    return base + value if sign > 0 else base - value


def block_terms(direction, first, second):
    if direction == 0:
        return (((1, second[1]), (-1, second[0])), ((1, first[1]), (-1, first[0])))
    if direction == 1:
        return (((-1, second[0]), (-1, second[1])), ((1, first[0]), (1, first[1])))
    if direction == 2:
        return (((1, first[1]), (-1, first[0])), ((-1, second[1]), (1, second[0])))
    return (((1, first[0]), (1, first[1])), ((1, second[0]), (1, second[1])))


def half_of(field, direction, sign):
    half = []
    for color in range(3):
        up = [(field(0, color, a), field(1, color, a)) for a in range(4)]
        terms = block_terms(direction, up[2], up[3])
        half.append(
            [
                tuple(
                    signed_add(up[a][part], sign * terms[a][part][0], terms[a][part][1])
                    for part in range(2)
                )
                for a in range(2)
            ]
        )
    return half


def color_apply(link, direction, half, dagger):
    out = []
    for row in range(3):
        acc = [[None, None], [None, None]]
        for col in range(3):
            i, j = (col, row) if dagger else (row, col)
            re, im = link(direction, i, j, 0), link(direction, i, j, 1)
            flip = -1 if dagger else 1
            for a in range(2):
                vec_re, vec_im = half[col][a]
                acc[a][0] = signed_add(acc[a][0], 1, re * vec_re)
                acc[a][0] = signed_add(acc[a][0], -flip, im * vec_im)
                acc[a][1] = signed_add(acc[a][1], 1, re * vec_im)
                acc[a][1] = signed_add(acc[a][1], flip, im * vec_re)
        out.append([tuple(acc[a]) for a in range(2)])
    return out


def shift(value, direction, ahead):
    if direction == 3:
        return pltpu.roll(value, 6 if ahead else 2, 0)
    if direction == 1:
        return pltpu.roll(value, SITES - LX if ahead else LX, 1)
    column = lax.broadcasted_iota(jnp.int32, value.shape, 1) % LX
    if ahead:
        return jnp.where(
            column == LX - 1, pltpu.roll(value, LX - 1, 1), pltpu.roll(value, SITES - 1, 1)
        )
    return jnp.where(column == 0, pltpu.roll(value, SITES - (LX - 1), 1), pltpu.roll(value, 1, 1))


def map_half(function, half):
    return [[tuple(function(v) for v in pair) for pair in spins] for spins in half]


def accumulate(total, direction, ahead, behind):
    for color in range(3):
        both = []
        for a in range(2):
            for part in range(2):
                key = (part, color, a)
                value = ahead[color][a][part] + behind[color][a][part]
                total[key] = value if key not in total else total[key] + value
            both.append(tuple(ahead[color][a][part] - behind[color][a][part] for part in range(2)))
        terms = block_terms(direction, both[0], both[1])
        outer = -1 if direction == 3 else 1
        for a in range(2):
            for part in range(2):
                key = (part, color, a + 2)
                sign, value = terms[a][part]
                total[key] = signed_add(total.get(key), outer * sign, value)


def hop(field, link, ahead_z, behind_z):
    total = {}
    for direction in (0, 1, 3):
        ahead = map_half(
            lambda v, d=direction: shift(v, d, True), half_of(field, direction, -1)
        )
        behind = color_apply(link, direction, half_of(field, direction, 1), True)
        behind = map_half(lambda v, d=direction: shift(v, d, False), behind)
        accumulate(total, direction, color_apply(link, direction, ahead, False), behind)
    accumulate(total, 2, color_apply(link, 2, ahead_z(), False), behind_z())
    return total


def comp(part, color, spin):
    return color * 8 + part * 4 + spin


def slot(direction, row, col, part):
    return direction * 18 + row * 6 + col * 2 + part


def field_at(ref, layer):
    return lambda part, color, spin: ref[layer, comp(part, color, spin)]


def link_at(ref, layer):
    return lambda direction, row, col, part: ref[layer, slot(direction, row, col, part)]


def put_half(ref, half):
    for color in range(3):
        for a in range(2):
            for part in range(2):
                ref[color * 4 + a * 2 + part] = half[color][a][part].astype(BF16)


def get_half(ref):
    return [
        [tuple(ref[color * 4 + a * 2 + part].astype(F32) for part in range(2)) for a in range(2)]
        for color in range(3)
    ]


def first_kernel(
    below_ref, own_ref, above_ref, base_ref, link_ref, out_ref, low_ref, high_ref, wide, src, phi, links
):
    for at, ref in enumerate((below_ref, own_ref, above_ref)):
        wide[at * 8 * ROWS : (at + 1) * 8 * ROWS] = ref[...].reshape(8 * ROWS, SITES).astype(F32)
    slices = lax.broadcasted_iota(jnp.int32, (4, SITES), 0)
    turn = jnp.where(slices == 3, -1.0, 1.0)

    def assemble(layer, carry):
        start = layer * 4 * ROWS
        for color in range(3):
            for part in range(2):
                for spin in range(4):
                    for which in range(2):
                        row = start + part * 24 + color * 8 + which * 4 + spin
                        src[layer, comp(part, color, spin), pl.ds(which, 4, stride=2)] = wide[
                            pl.ds(row, 4, stride=ROWS)
                        ]
        for entry in range(LINK):
            value = wide[pl.ds(start + FIELD + entry, 4, stride=ROWS)]
            if entry >= 54:
                value = value * turn
            for which in range(2):
                links[layer, entry, pl.ds(which, 4, stride=2)] = value
        return carry

    lax.fori_loop(0, 6, assemble, 0)

    def sweep(from_ref, to_ref, layer, target):
        def ahead_z():
            return half_of(field_at(from_ref, layer + 1), 2, -1)

        def behind_z():
            half = half_of(field_at(from_ref, layer - 1), 2, 1)
            return color_apply(link_at(links, layer - 1), 2, half, True)

        total = hop(field_at(from_ref, layer), link_at(links, layer), ahead_z, behind_z)
        for (part, color, spin), value in total.items():
            at = comp(part, color, spin)
            to_ref[target, at] = src[layer, at] + HOPPING * value

    def one(layer, carry):
        sweep(src, phi, layer, layer)
        return carry

    lax.fori_loop(1, 5, one, 0)

    def two(layer, carry):
        sweep(phi, out_ref, layer, layer - 2)
        return carry

    lax.fori_loop(2, 4, two, 0)
    base_ref[...] = src[2:4]
    link_ref[...] = links[2:4]
    put_half(low_ref, half_of(field_at(out_ref, 0), 2, -1))
    high = half_of(field_at(out_ref, 1), 2, 1)
    put_half(high_ref, color_apply(link_at(links, 3), 2, high, True))


def second_kernel(base_ref, link_ref, phi_ref, low_ref, high_ref, out_ref, done):
    for layer in range(2):
        if layer == 0:

            def ahead_z():
                return half_of(field_at(phi_ref, 1), 2, -1)

            def behind_z():
                return get_half(high_ref)
        else:

            def ahead_z():
                return get_half(low_ref)

            def behind_z():
                half = half_of(field_at(phi_ref, 0), 2, 1)
                return color_apply(link_at(link_ref, 0), 2, half, True)

        total = hop(field_at(phi_ref, layer), link_at(link_ref, layer), ahead_z, behind_z)
        for (part, color, spin), value in total.items():
            at = comp(part, color, spin)
            done[(layer * 24 + at) * 8 : (layer * 24 + at + 1) * 8] = (
                base_ref[layer, at] + HOPPING * value
            )
    for layer in range(2):
        for time in range(4):
            for color in range(3):
                start = (layer * 24 + color * 8) * 8 + 2 * time
                pair = [done[pl.ds(start + which, 8, stride=8)] for which in range(2)]
                out_ref[layer * 4 + time, color * 16 : color * 16 + 16] = jnp.concatenate(
                    pair, 0
                ).astype(BF16)


def project_kernel(phi_ref, vector_ref, out_ref):
    totals = [None, None]
    for color in range(3):
        rows = phi_ref[:, color * 16 : color * 16 + 16].reshape(8 * 16, SITES)
        for part in range(2):
            value = lax.dot_general(
                rows,
                vector_ref[color, part],
                (((1,), (1,)), ((), ())),
                preferred_element_type=F32,
            )
            totals[part] = value if totals[part] is None else totals[part] + value
    crossed = pltpu.roll(totals[1].reshape(16, 8, 128), 4, 1)
    upper = lax.broadcasted_iota(jnp.int32, crossed.shape, 1) < 4
    mixed = totals[0].reshape(16, 8, 128) + jnp.where(upper, crossed, -crossed)
    out_ref[...] = mixed.reshape(8, 16, 128)


def all_reduce(partial_value):
    plane = lax.axis_size(PLANE)
    depth = lax.axis_size("z")
    mine = exchange(partial_value, PLANE).sum(0)
    copies = jnp.broadcast_to(mine, (depth, *mine.shape))
    mine = exchange(copies, "z").sum(0)
    copies = jnp.broadcast_to(mine, (plane, *mine.shape))
    return exchange(copies, PLANE)


def spinors(sources, gauge_links):
    moved = sources[0, :, :, :, :, 0].transpose(0, 2, 3, 1, 4)
    entries = gauge_links[:, 0, :, :, :, 0].transpose(0, 2, 3, 1, 4).reshape(36, 2, SITES)
    packed = local_call(
        pack_kernel,
        jax.ShapeDtypeStruct((8, ROWS, SITES), BF16),
        [pltpu.VMEM((8, ROWS, SITES), F32), pltpu.VMEM((LINK, SITES), F32)],
        1 << 17,
    )(moved, entries)
    own = exchange(packed, BLOCK)
    below = from_behind(own, POSITION, 1)
    above = from_behind(own, POSITION, -1)
    vectors = (8, SITES)
    base, links, phi, low, high = local_call(
        first_kernel,
        (
            jax.ShapeDtypeStruct((2, 24, *vectors), F32),
            jax.ShapeDtypeStruct((2, LINK, *vectors), F32),
            jax.ShapeDtypeStruct((2, 24, *vectors), F32),
            jax.ShapeDtypeStruct((12, *vectors), BF16),
            jax.ShapeDtypeStruct((12, *vectors), BF16),
        ),
        [
            pltpu.VMEM((3 * 8 * ROWS, SITES), F32),
            pltpu.VMEM((6, 24, *vectors), F32),
            pltpu.VMEM((6, 24, *vectors), F32),
            pltpu.VMEM((6, LINK, *vectors), F32),
        ],
        1 << 24,
    )(below, own, above)
    high = from_behind(high, POSITION, 1)
    low = from_behind(low, POSITION, -1)
    done = local_call(
        second_kernel,
        jax.ShapeDtypeStruct((8, FIELD, SITES), BF16),
        [pltpu.VMEM((2 * 24 * 8, SITES), F32)],
        1 << 23,
    )(base, links, phi, low, high)
    return exchange(done, BLOCK)


def contract(matrices, values):
    product = functools.partial(jnp.einsum, "xl,sral->sra", precision=lax.Precision.HIGHEST)
    by_re, by_im = product(matrices[0], values), product(matrices[1], values)
    real_part = by_re[:, 0] - by_im[:, 1]
    imag_part = by_re[:, 1] + by_im[:, 0]
    return jnp.stack([real_part, imag_part], 1)


def placed_out(values):
    return values.transpose(1, 2, 0)[None, :, :, :, None]


def local(sources, gauge_links, eigenvectors, elementals):
    vectors = eigenvectors[0, :, :, :, 0].transpose(2, 1, 0, 3)
    finals = spinors(sources, gauge_links)
    partial_value = local_call(
        project_kernel, jax.ShapeDtypeStruct((8, 16, 128), F32), [], 1 << 25
    )(finals, vectors)
    totals = all_reduce(partial_value)[:6].reshape(12, 2, 4, 128)
    mine = lax.dynamic_slice_in_dim(totals, lax.axis_index(SPACE), 1, 3)[..., 0]
    return placed_out(mine), placed_out(contract(elementals[0], totals))


def solution(mesh):
    fine = Mesh(mesh.devices.reshape(2, 2, 4, 16, 2), (*TM, *SPACE))
    placed = (
        P(TM, None, None, None, None, SPACE, None),
        P(None, TM, None, None, None, SPACE, None),
        P(TM, None, None, None, SPACE, None),
        P(TM, None, SPACE, None),
    )
    result = P(TM, None, None, None, SPACE)
    return jax.shard_map(
        local, mesh=fine, in_specs=placed, out_specs=(result, result), check_vma=False
    )
```

time: 152 us -> 102 us (0.67)
  starting transfers between devices: 59.6 us -> 31.7 us
  other arithmetic: 20.4 us -> 0.63 us
  waiting for transfers between devices: 34.6 us -> 20.9 us
  blocking collectives: 28.1 us -> 39.5 us
  Pallas kernels: 0 us -> 3.35 us
  between operations: 3.53 us -> 0.73 us
    ppermute x14 -> x4, starting transfers between devices: 55.1 us -> 21.7 us  [from_behind(): lax.ppermute(value, axes, [(i, (i + steps) % count) for i in range(count)])]
    ppermute x14 -> x4, waiting for transfers between devices: 29.5 us -> 11.8 us  [from_behind(): lax.ppermute(value, axes, [(i, (i + steps) % count) for i in range(count)])]
    another operation x224 -> x0, other arithmetic: 12.3 us -> none  [the longest x70 4.32 us: stored(): return jnp.stack([pair[0], pair[1]], 1).astype(jnp.bfloat16)]
    all_to_all x2 -> x3, blocking collectives: 28.1 us -> 39.5 us  [exchange(): return lax.all_to_all(value, axes, 0, 0, tiled=True)]
    all_to_all x1 -> x2, starting transfers between devices: 4.45 us -> 10 us  [exchange(): return lax.all_to_all(value, axes, 0, 0, tiled=True)]
    all_to_all x1 -> x2, waiting for transfers between devices: 5.09 us -> 9.15 us  [exchange(): return lax.all_to_all(value, axes, 0, 0, tiled=True)]
    pallas_call x0 -> x4, Pallas kernels: none -> 3.35 us  [the longest x1 1.99 us: spinors(): local_call(first_kernel, (jax.ShapeDtypeStruct((2, 24, *vectors), F32), j...]
    convert_element_type x38 -> x0, other arithmetic: 3.11 us -> none  [the longest x34 2.59 us: split_parts(): widened = values.astype(jnp.float32)]
  transfers between devices with their start and end apart: 15 -> 6, of which waited for: 8 -> 5; matrix products, arithmetic and copies ran while one was open for 8% -> 0% of each run, Pallas kernels for 0% -> 0%
where the time goes in v2:
time: 102 us
  blocking collectives  39.5 us (39%)
  starting transfers between devices  31.7 us (31%)
  waiting for transfers between devices  20.9 us (20%)
  local copies, waits for them, and re-layouts  3.78 us (4%)
  Pallas kernels  3.35 us (3%)
  matrix products  1.15 us (1%)
    all_to_all x3, blocking collectives, exchange(): return lax.all_to_all(value, axes, 0, 0, tiled=True)  39.5 us
    ppermute x4, starting transfers between devices, from_behind(): lax.ppermute(value, axes, [(i, (i + steps) % count) for i in range(count)])  21.7 us
    ppermute x4, waiting for transfers between devices, from_behind(): lax.ppermute(value, axes, [(i, (i + steps) % count) for i in range(count)])  11.8 us
    all_to_all x2, starting transfers between devices, exchange(): return lax.all_to_all(value, axes, 0, 0, tiled=True)  10 us
    all_to_all x2, waiting for transfers between devices, exchange(): return lax.all_to_all(value, axes, 0, 0, tiled=True)  9.15 us
    unnamed x9, local copies, waits for them, and re-layouts  2.31 us
  transfers between devices with their start and end apart: 6, of which 5 were waited for; matrix products, arithmetic and copies ran while one was open for 0% of the time, Pallas kernels for 0%

profile of v2, /device:TPU:8, one launch (start us, length us, event | category | flops | bytes accessed | tf_op | source)
XLA Modules:
  0.0 101.8 jit_solution(9962239791953977629)
XLA Ops:
  0.6 0.9 copy-done
  1.5 0.7 copy-done.1
  2.3 13.5 %all_to_all.25.own_ref = bf16[8,120,128]{2,1,0:T(8,128)(2,1)S(1)} all-to-all(bf16[8,120,128]{2,1,0:T(8,128)(2,1)S(1)} %shard_map.59), channel_id=1, replica_groups=mesh['y_hi'=2,'core'=2,'x'=4,'z'=16,'y_lo'=2] {'y_lo','y_hi','core'}, dimensions={0} | all-to-all | bytes 491520 | tf_op jit(solution)/shard_map/all_to_all | solution.py:27
  15.7 1.9 %collective-permute-start = (bf16[8,120,128]{2,1,0:T(8,128)(2,1)S(1)}, bf16[8,120,128]{2,1,0:T(8,128)(2,1)S(1)}, u32[]{:S(2)}, u32[]{:S(2)}) collective-permute-start(bf16[8,120,128]{2,1,0:T(8,128)(2,1)S(1)} %all_to_all.25.own_ref), channel_id=1, source_target_pairs={{0,2},{2,4},{4,6},{6,8},{8,10},{10,12},{12,14},{14,16},{16,18},{18... | collective-permute-start | bytes 737288 | tf_op jit(solution)/shard_map/ppermute | solution.py:32
  17.7 10.1 %collective-permute-start.1 = (bf16[8,120,128]{2,1,0:T(8,128)(2,1)S(1)}, bf16[8,120,128]{2,1,0:T(8,128)(2,1)S(1)}, u32[]{:S(2)}, u32[]{:S(2)}) collective-permute-start(bf16[8,120,128]{2,1,0:T(8,128)(2,1)S(1)} %all_to_all.25.own_ref), channel_id=1, source_target_pairs={{0,126},{2,0},{4,2},{6,4},{8,6},{10,8},{12,10},{14,12},{16,14},{18... | collective-permute-start | bytes 737288 | tf_op jit(solution)/shard_map/ppermute | solution.py:32
  27.8 3.5 %collective-permute-done.below_ref = bf16[8,120,128]{2,1,0:T(8,128)(2,1)S(1)} collective-permute-done((bf16[8,120,128]{2,1,0:T(8,128)(2,1)S(1)}, bf16[8,120,128]{2,1,0:T(8,128)(2,1)S(1)}, u32[]{:S(2)}, u32[]{:S(2)}) %collective-permute-start) | collective-permute-done | bytes 245792 | tf_op jit(solution)/shard_map/ppermute | solution.py:32
  31.3 1.2 %collective-permute-done.1.above_ref = bf16[8,120,128]{2,1,0:T(8,128)(2,1)S(1)} collective-permute-done((bf16[8,120,128]{2,1,0:T(8,128)(2,1)S(1)}, bf16[8,120,128]{2,1,0:T(8,128)(2,1)S(1)}, u32[]{:S(2)}, u32[]{:S(2)}) %collective-permute-start.1) | collective-permute-done | bytes 245792 | tf_op jit(solution)/shard_map/ppermute | solution.py:32
  32.5 2.0 %shard_map.60 = (f32[2,24,8,128]{3,2,1,0:T(8,128)S(1)}, f32[2,72,8,128]{3,2,1,0:T(8,128)S(1)}, f32[2,24,8,128]{3,2,1,0:T(8,128)S(1)}, bf16[12,8,128]{2,1,0:T(8,128)(2,1)S(1)}, bf16[12,8,128]{2,1,0:T(8,128)(2,1)S(1)}) custom-call(bf16[8,120,128]{2,1,0:T(8,128)(2,1)S(1)} %collective-permute-done.below_ref, bf16[8,120,128]{2,1,0:T(8,128)(2,1)S(1)} %all_to_all.25.own_ref, ...), custom_call_target="tpu_custom_call" | custom-call | flops 16777216 | bytes 1048576 | tf_op jit(solution)/shard_map/pallas_call | solution.py:326
  34.5 7.7 %collective-permute-start.2 = (bf16[12,8,128]{2,1,0:T(8,128)(2,1)S(1)}, bf16[12,8,128]{2,1,0:T(8,128)(2,1)S(1)}, u32[]{:S(2)}, u32[]{:S(2)}) collective-permute-start(bf16[12,8,128]{2,1,0:T(8,128)(2,1)S(1)} %get-tuple-element.10), channel_id=1, source_target_pairs={{0,126},{2,0},{4,2},{6,4},{8,6},{10,8},{12,10},{14,12},{16,14},{18... | collective-permute-start | bytes 73736 | tf_op jit(solution)/shard_map/ppermute | solution.py:32
  42.2 1.9 %collective-permute-start.3 = (bf16[12,8,128]{2,1,0:T(8,128)(2,1)S(1)}, bf16[12,8,128]{2,1,0:T(8,128)(2,1)S(1)}, u32[]{:S(2)}, u32[]{:S(2)}) collective-permute-start(bf16[12,8,128]{2,1,0:T(8,128)(2,1)S(1)} %get-tuple-element.11), channel_id=1, source_target_pairs={{0,2},{2,4},{4,6},{6,8},{8,10},{10,12},{12,14},{14,16},{16,18},{18... | collective-permute-start | bytes 73736 | tf_op jit(solution)/shard_map/ppermute | solution.py:32
  44.1 7.1 %collective-permute-done.3.high_ref = bf16[12,8,128]{2,1,0:T(8,128)(2,1)S(1)} collective-permute-done((bf16[12,8,128]{2,1,0:T(8,128)(2,1)S(1)}, bf16[12,8,128]{2,1,0:T(8,128)(2,1)S(1)}, u32[]{:S(2)}, u32[]{:S(2)}) %collective-permute-start.3) | collective-permute-done | bytes 24608 | tf_op jit(solution)/shard_map/ppermute | solution.py:32
  51.2 1.1 %shard_map.61 = bf16[8,48,128]{2,1,0:T(8,128)(2,1)} custom-call(f32[2,24,8,128]{3,2,1,0:T(8,128)S(1)} %get-tuple-element.7.base_ref, f32[2,72,8,128]{3,2,1,0:T(8,128)S(1)} %get-tuple-element.8.link_ref, f32[2,24,8,128]{3,2,1,0:T(8,128)S(1)} %get-tuple-element.9.phi_ref, bf16[12,8,128]{2,1,0:T(8,128)(2,1)S(1)} %collective-permute-done.2.low_ref, ...), custom_call_target="tpu_custom_call" | custom-call | flops 8388608 | bytes 1048576 | tf_op jit(solution)/shard_map/pallas_call | solution.py:345
  52.3 5.6 %all-to-all-start.1 = ((bf16[8,48,128]{2,1,0:T(8,128)(2,1)}), bf16[8,48,128]{2,1,0:T(8,128)(2,1)S(1)}, u32[]{:S(2)}, u32[]{:S(2)}) async-start(bf16[8,48,128]{2,1,0:T(8,128)(2,1)} %shard_map.61), calls=%async_computation.1 | async-start | bytes 196608 | tf_op jit(solution)/shard_map/all_to_all | solution.py:27
  57.9 4.1 %all-to-all-done.1.phi_ref = bf16[8,48,128]{2,1,0:T(8,128)(2,1)S(1)} async-done(((bf16[8,48,128]{2,1,0:T(8,128)(2,1)}), bf16[8,48,128]{2,1,0:T(8,128)(2,1)S(1)}, u32[]{:S(2)}, u32[]{:S(2)}) %all-to-all-start.1) | async-done | bytes 98336 | tf_op jit(solution)/shard_map/all_to_all | solution.py:27
  62.2 9.0 %all_to_all.26 = f32[8,16,128]{2,1,0:T(8,128)S(1)} all-to-all(f32[8,16,128]{2,1,0:T(8,128)S(1)} %shard_map.62), channel_id=1, replica_groups=mesh['y_hi'=2,'core'=2,'x'=4,'z'=16,'y_lo'=2] {'x','y_lo'}, dimensions={0} | all-to-all | bytes 131072 | tf_op jit(solution)/shard_map/all_to_all | solution.py:27
  71.2 17.1 %all_to_all.27 = f32[16,16,128]{2,1,0:T(8,128)S(1)} all-to-all(f32[16,16,128]{2,1,0:T(8,128)S(1)} %broadcast_in_dim.12), channel_id=1, replica_groups=mesh['y_hi'=2,'core'=2,'x'=4,'z'=16,'y_lo'=2] {'z'}, dimensions={0} | all-to-all | bytes 262144 | tf_op jit(solution)/shard_map/all_to_all | solution.py:27
  88.3 0.6 broadcast_in_dim.13
  89.0 4.4 %all-to-all-start.4 = ((f32[8,16,128]{2,1,0:T(8,128)}), f32[8,16,128]{2,1,0:T(8,128)S(1)}, u32[]{:S(2)}, u32[]{:S(2)}) async-start(f32[8,16,128]{2,1,0:T(8,128)} %broadcast_in_dim.13), calls=%async_computation.4 | async-start | bytes 131072 | tf_op jit(solution)/shard_map/all_to_all | solution.py:27
  93.4 5.1 %all-to-all-done.4 = f32[8,16,128]{2,1,0:T(8,128)S(1)} async-done(((f32[8,16,128]{2,1,0:T(8,128)}), f32[8,16,128]{2,1,0:T(8,128)S(1)}, u32[]{:S(2)}, u32[]{:S(2)}) %all-to-all-start.4) | async-done | bytes 65568 | tf_op jit(solution)/shard_map/all_to_all | solution.py:27
  98.5 0.7 copy-done.3
  99.2 0.6 fusion.2
  99.8 0.6 fusion
  100.4 0.7 copy.14
  101.2 0.6 pad_maximum_fusion
  (15 shorter events, 0.5 us)
Async XLA Ops:
  0.6 0.9 copy-start
  1.5 0.7 copy-start.1
  15.7 15.5 %collective-permute-start = (bf16[8,120,128]{2,1,0:T(8,128)(2,1)S(1)}, bf16[8,120,128]{2,1,0:T(8,128)(2,1)S(1)}, u32[]{:S(2)}, u32[]{:S(2)}) collective-permute-start(bf16[8,120,128]{2,1,0:T(8,128)(2,1)S(1)} %all_to_all.25.own_ref), channel_id=1, source_target_pairs={{0,2},{2,4},{4,6},{6,8},{8,10},{10,12},{12,14},{14,16},{16,18},{18... | collective-permute-start | bytes 737288 | tf_op jit(solution)/shard_map/ppermute | solution.py:32
  17.7 14.8 %collective-permute-start.1 = (bf16[8,120,128]{2,1,0:T(8,128)(2,1)S(1)}, bf16[8,120,128]{2,1,0:T(8,128)(2,1)S(1)}, u32[]{:S(2)}, u32[]{:S(2)}) collective-permute-start(bf16[8,120,128]{2,1,0:T(8,128)(2,1)S(1)} %all_to_all.25.own_ref), channel_id=1, source_target_pairs={{0,126},{2,0},{4,2},{6,4},{8,6},{10,8},{12,10},{14,12},{16,14},{18... | collective-permute-start | bytes 737288 | tf_op jit(solution)/shard_map/ppermute | solution.py:32
  34.5 9.6 %collective-permute-start.2 = (bf16[12,8,128]{2,1,0:T(8,128)(2,1)S(1)}, bf16[12,8,128]{2,1,0:T(8,128)(2,1)S(1)}, u32[]{:S(2)}, u32[]{:S(2)}) collective-permute-start(bf16[12,8,128]{2,1,0:T(8,128)(2,1)S(1)} %get-tuple-element.10), channel_id=1, source_target_pairs={{0,126},{2,0},{4,2},{6,4},{8,6},{10,8},{12,10},{14,12},{16,14},{18... | collective-permute-start | bytes 73736 | tf_op jit(solution)/shard_map/ppermute | solution.py:32
  42.2 9.0 %collective-permute-start.3 = (bf16[12,8,128]{2,1,0:T(8,128)(2,1)S(1)}, bf16[12,8,128]{2,1,0:T(8,128)(2,1)S(1)}, u32[]{:S(2)}, u32[]{:S(2)}) collective-permute-start(bf16[12,8,128]{2,1,0:T(8,128)(2,1)S(1)} %get-tuple-element.11), channel_id=1, source_target_pairs={{0,2},{2,4},{4,6},{6,8},{8,10},{10,12},{12,14},{14,16},{16,18},{18... | collective-permute-start | bytes 73736 | tf_op jit(solution)/shard_map/ppermute | solution.py:32
  52.3 5.6 %copy-start.2 = (bf16[1,128,2,3,1,128]{5,2,4,3,1,0:T(2,128)(2,1)S(1)}, bf16[1,128,2,3,1,128]{5,2,4,3,1,0:T(2,128)(2,1)}, u32[]{:S(2)}) copy-start(bf16[1,128,2,3,1,128]{5,2,4,3,1,0:T(2,128)(2,1)} %param.6) | copy-start | bytes 589828
  52.3 9.7 %all-to-all-start.1 = ((bf16[8,48,128]{2,1,0:T(8,128)(2,1)}), bf16[8,48,128]{2,1,0:T(8,128)(2,1)S(1)}, u32[]{:S(2)}, u32[]{:S(2)}) async-start(bf16[8,48,128]{2,1,0:T(8,128)(2,1)} %shard_map.61), calls=%async_computation.1 | async-start | bytes 196608 | tf_op jit(solution)/shard_map/all_to_all | solution.py:27
  89.0 9.5 %all-to-all-start.4 = ((f32[8,16,128]{2,1,0:T(8,128)}), f32[8,16,128]{2,1,0:T(8,128)S(1)}, u32[]{:S(2)}, u32[]{:S(2)}) async-start(f32[8,16,128]{2,1,0:T(8,128)} %broadcast_in_dim.13), calls=%async_computation.4 | async-start | bytes 131072 | tf_op jit(solution)/shard_map/all_to_all | solution.py:27
  98.5 0.7 copy-start.3

commit v3 on v2

--- a/solution.py
+++ b/solution.py
@@ -1,5 +1,3 @@
-import functools
-
 import jax
 import jax.numpy as jnp
 from jax import lax
@@ -32,9 +30,10 @@
     return lax.ppermute(value, axes, [(i, (i + steps) % count) for i in range(count)])
 
 
-def local_call(kernel, outs, scratch, flops):
+def local_call(kernel, outs, scratch, flops, **options):
     return pl.pallas_call(
         kernel,
+        **options,
         out_shape=outs,
         scratch_shapes=scratch,
         compiler_params=pltpu.CompilerParams(vmem_limit_bytes=16 << 20),
@@ -46,6 +45,8 @@
     for entry in range(36):
         links[2 * entry : 2 * entry + 2] = link_ref[entry].astype(F32)
     shared = links[...]
+    for target in range(8):
+        rows[target, FIELD:] = shared
     for target in range(8):
         for part in range(2):
             for color in range(3):
@@ -56,7 +57,6 @@
                     else:
                         piece = jnp.zeros((4, SITES), F32)
                     rows[target, at : at + 4] = piece
-        rows[target, FIELD:] = shared
     out_ref[...] = rows[...].astype(BF16)
 
 
@@ -155,7 +155,7 @@
         behind = color_apply(link, direction, half_of(field, direction, 1), True)
         behind = map_half(lambda v, d=direction: shift(v, d, False), behind)
         accumulate(total, direction, color_apply(link, direction, ahead, False), behind)
-    accumulate(total, 2, color_apply(link, 2, ahead_z(), False), behind_z())
+    accumulate(total, 2, color_apply(link, 2, ahead_z, False), behind_z)
     return total
 
 
@@ -173,105 +173,115 @@
 
 def link_at(ref, layer):
     return lambda direction, row, col, part: ref[layer, slot(direction, row, col, part)]
+
+
+def half_slot(part, color, spin):
+    return color * 4 + spin * 2 + part
 
 
 def put_half(ref, half):
     for color in range(3):
         for a in range(2):
             for part in range(2):
-                ref[color * 4 + a * 2 + part] = half[color][a][part].astype(BF16)
-
-
-def get_half(ref):
+                ref[half_slot(part, color, a)] = half[color][a][part].astype(ref.dtype)
+
+
+def get_half(ref, layer):
     return [
-        [tuple(ref[color * 4 + a * 2 + part].astype(F32) for part in range(2)) for a in range(2)]
+        [tuple(ref[layer, half_slot(part, color, a)] for part in range(2)) for a in range(2)]
         for color in range(3)
     ]
 
 
-def first_kernel(
-    below_ref, own_ref, above_ref, base_ref, link_ref, out_ref, low_ref, high_ref, wide, src, phi, links
-):
-    for at, ref in enumerate((below_ref, own_ref, above_ref)):
-        wide[at * 8 * ROWS : (at + 1) * 8 * ROWS] = ref[...].reshape(8 * ROWS, SITES).astype(F32)
+def assemble(wide, start, src, links, layer):
     slices = lax.broadcasted_iota(jnp.int32, (4, SITES), 0)
     turn = jnp.where(slices == 3, -1.0, 1.0)
-
-    def assemble(layer, carry):
-        start = layer * 4 * ROWS
-        for color in range(3):
-            for part in range(2):
-                for spin in range(4):
-                    for which in range(2):
-                        row = start + part * 24 + color * 8 + which * 4 + spin
-                        src[layer, comp(part, color, spin), pl.ds(which, 4, stride=2)] = wide[
-                            pl.ds(row, 4, stride=ROWS)
-                        ]
-        for entry in range(LINK):
-            value = wide[pl.ds(start + FIELD + entry, 4, stride=ROWS)]
-            if entry >= 54:
-                value = value * turn
-            for which in range(2):
-                links[layer, entry, pl.ds(which, 4, stride=2)] = value
+    for color in range(3):
+        for part in range(2):
+            for spin in range(4):
+                for which in range(2):
+                    row = start + part * 24 + color * 8 + which * 4 + spin
+                    src[layer, comp(part, color, spin), pl.ds(which, 4, stride=2)] = wide[
+                        pl.ds(row, 4, stride=ROWS)
+                    ]
+    for entry in range(LINK):
+        value = wide[pl.ds(start + FIELD + entry, 4, stride=ROWS)]
+        if entry >= 54:
+            value = value * turn
+        for which in range(2):
+            links[layer, entry, pl.ds(which, 4, stride=2)] = value
+
+
+def sent_down(field):
+    return half_of(field, 2, -1)
+
+
+def sent_up(field, link):
+    return color_apply(link, 2, half_of(field, 2, 1), True)
+
+
+def own_kernel(own_ref, matrix_ref, base_ref, link_ref, low_ref, high_ref, kept_ref, wide):
+    kept_ref[...] = matrix_ref[...]
+    wide[...] = own_ref[...].reshape(8 * ROWS, SITES).astype(F32)
+
+    def one(layer, carry):
+        assemble(wide, layer * 4 * ROWS, base_ref, link_ref, layer)
         return carry
 
-    lax.fori_loop(0, 6, assemble, 0)
-
-    def sweep(from_ref, to_ref, layer, target):
-        def ahead_z():
-            return half_of(field_at(from_ref, layer + 1), 2, -1)
-
-        def behind_z():
-            half = half_of(field_at(from_ref, layer - 1), 2, 1)
-            return color_apply(link_at(links, layer - 1), 2, half, True)
-
-        total = hop(field_at(from_ref, layer), link_at(links, layer), ahead_z, behind_z)
-        for (part, color, spin), value in total.items():
-            at = comp(part, color, spin)
-            to_ref[target, at] = src[layer, at] + HOPPING * value
-
-    def one(layer, carry):
-        sweep(src, phi, layer, layer)
+    lax.fori_loop(0, 2, one, 0)
+    put_half(low_ref, sent_down(field_at(base_ref, 0)))
+    put_half(high_ref, sent_up(field_at(base_ref, 1), link_at(link_ref, 1)))
+
+
+def sweep_kernel(
+    below_ref, above_ref, base_ref, link_ref, low_ref, high_ref, out_ref,
+    wide, src, one, two, links, ahead, behind, done,
+):
+    for at, ref in enumerate((below_ref, above_ref)):
+        wide[at * 8 * ROWS : (at + 1) * 8 * ROWS] = ref[...].reshape(8 * ROWS, SITES).astype(F32)
+
+    def gather(layer, carry):
+        assemble(wide, layer * 4 * ROWS, src, links, layer + 2 * (layer // 2))
         return carry
 
-    lax.fori_loop(1, 5, one, 0)
-
-    def two(layer, carry):
-        sweep(phi, out_ref, layer, layer - 2)
-        return carry
-
-    lax.fori_loop(2, 4, two, 0)
-    base_ref[...] = src[2:4]
-    link_ref[...] = links[2:4]
-    put_half(low_ref, half_of(field_at(out_ref, 0), 2, -1))
-    high = half_of(field_at(out_ref, 1), 2, 1)
-    put_half(high_ref, color_apply(link_at(links, 3), 2, high, True))
-
-
-def second_kernel(base_ref, link_ref, phi_ref, low_ref, high_ref, out_ref, done):
-    for layer in range(2):
-        if layer == 0:
-
-            def ahead_z():
-                return half_of(field_at(phi_ref, 1), 2, -1)
-
-            def behind_z():
-                return get_half(high_ref)
-        else:
-
-            def ahead_z():
-                return get_half(low_ref)
-
-            def behind_z():
-                half = half_of(field_at(phi_ref, 0), 2, 1)
-                return color_apply(link_at(link_ref, 0), 2, half, True)
-
-        total = hop(field_at(phi_ref, layer), link_at(link_ref, layer), ahead_z, behind_z)
-        for (part, color, spin), value in total.items():
-            at = comp(part, color, spin)
-            done[(layer * 24 + at) * 8 : (layer * 24 + at + 1) * 8] = (
-                base_ref[layer, at] + HOPPING * value
+    lax.fori_loop(0, 4, gather, 0)
+    src[2:4] = base_ref[...]
+    links[2:4] = link_ref[...]
+    ahead[6] = low_ref[...].astype(F32)
+    behind[0] = high_ref[...].astype(F32)
+
+    def sweep(from_ref, halves, layers, put):
+        def prepare(layer, carry):
+            put_half(ahead.at[layer], sent_down(field_at(from_ref, layer)))
+            put_half(behind.at[layer + 1], sent_up(field_at(from_ref, layer), link_at(links, layer)))
+            return carry
+
+        def step(layer, carry):
+            total = hop(
+                field_at(from_ref, layer),
+                link_at(links, layer),
+                get_half(ahead, layer + 1),
+                get_half(behind, layer),
             )
+            for key, value in total.items():
+                put(layer, comp(*key), src[layer, comp(*key)] + HOPPING * value)
+            return carry
+
+        lax.fori_loop(*halves, prepare, 0)
+        lax.fori_loop(*layers, step, 0)
+
+    def put_one(layer, at, value):
+        one[layer, at] = value
+
+    def put_two(layer, at, value):
+        two[layer, at] = value
+
+    def put_done(layer, at, value):
+        done[pl.ds(pl.multiple_of(((layer - 2) * 24 + at) * 8, 8), 8)] = value
+
+    sweep(src, (0, 6), (0, 6), put_one)
+    sweep(one, (0, 6), (1, 5), put_two)
+    sweep(two, (1, 5), (2, 4), put_done)
     for layer in range(2):
         for time in range(4):
             for color in range(3):
@@ -297,81 +307,122 @@
     crossed = pltpu.roll(totals[1].reshape(16, 8, 128), 4, 1)
     upper = lax.broadcasted_iota(jnp.int32, crossed.shape, 1) < 4
     mixed = totals[0].reshape(16, 8, 128) + jnp.where(upper, crossed, -crossed)
-    out_ref[...] = mixed.reshape(8, 16, 128)
+    out_ref[...] = mixed.reshape(8, 16, 128).astype(BF16)
+
+
+def spread_kernel(value_ref, out_ref):
+    total = value_ref[0].astype(F32)
+    for member in range(1, value_ref.shape[0]):
+        total = total + value_ref[member].astype(F32)
+    total = total.astype(BF16)
+    for member in range(out_ref.shape[0]):
+        out_ref[member] = total
+
+
+def summed(value, copies):
+    shape = jax.ShapeDtypeStruct((copies, *value.shape[1:]), BF16)
+    return local_call(spread_kernel, shape, [], 1 << 16)(value)
 
 
 def all_reduce(partial_value):
     plane = lax.axis_size(PLANE)
     depth = lax.axis_size("z")
-    mine = exchange(partial_value, PLANE).sum(0)
-    copies = jnp.broadcast_to(mine, (depth, *mine.shape))
-    mine = exchange(copies, "z").sum(0)
-    copies = jnp.broadcast_to(mine, (plane, *mine.shape))
+    copies = summed(exchange(partial_value, PLANE), depth)
+    copies = summed(exchange(copies, "z"), plane)
     return exchange(copies, PLANE)
 
 
-def spinors(sources, gauge_links):
+def spinors(sources, gauge_links, matrix):
     moved = sources[0, :, :, :, :, 0].transpose(0, 2, 3, 1, 4)
     entries = gauge_links[:, 0, :, :, :, 0].transpose(0, 2, 3, 1, 4).reshape(36, 2, SITES)
     packed = local_call(
         pack_kernel,
         jax.ShapeDtypeStruct((8, ROWS, SITES), BF16),
-        [pltpu.VMEM((8, ROWS, SITES), F32), pltpu.VMEM((LINK, SITES), F32)],
+        [
+            pltpu.VMEM((8, ROWS, SITES), F32),
+            pltpu.VMEM((LINK, SITES), F32),
+        ],
         1 << 17,
     )(moved, entries)
     own = exchange(packed, BLOCK)
     below = from_behind(own, POSITION, 1)
     above = from_behind(own, POSITION, -1)
     vectors = (8, SITES)
-    base, links, phi, low, high = local_call(
-        first_kernel,
+    base, links, low, high, kept = local_call(
+        own_kernel,
         (
             jax.ShapeDtypeStruct((2, 24, *vectors), F32),
             jax.ShapeDtypeStruct((2, LINK, *vectors), F32),
-            jax.ShapeDtypeStruct((2, 24, *vectors), F32),
             jax.ShapeDtypeStruct((12, *vectors), BF16),
             jax.ShapeDtypeStruct((12, *vectors), BF16),
+            jax.ShapeDtypeStruct(matrix.shape, F32),
         ),
+        [pltpu.VMEM((8 * ROWS, SITES), F32)],
+        1 << 20,
+    )(own, matrix)
+    high = from_behind(high, POSITION, 2)
+    low = from_behind(low, POSITION, -2)
+    done = local_call(
+        sweep_kernel,
+        jax.ShapeDtypeStruct((8, FIELD, SITES), BF16),
         [
-            pltpu.VMEM((3 * 8 * ROWS, SITES), F32),
+            pltpu.VMEM((2 * 8 * ROWS, SITES), F32),
+            pltpu.VMEM((6, 24, *vectors), F32),
             pltpu.VMEM((6, 24, *vectors), F32),
             pltpu.VMEM((6, 24, *vectors), F32),
             pltpu.VMEM((6, LINK, *vectors), F32),
+            pltpu.VMEM((7, 12, *vectors), F32),
+            pltpu.VMEM((7, 12, *vectors), F32),
+            pltpu.VMEM((2 * 24 * 8, SITES), F32),
         ],
         1 << 24,
-    )(below, own, above)
-    high = from_behind(high, POSITION, 1)
-    low = from_behind(low, POSITION, -1)
-    done = local_call(
-        second_kernel,
-        jax.ShapeDtypeStruct((8, FIELD, SITES), BF16),
-        [pltpu.VMEM((2 * 24 * 8, SITES), F32)],
-        1 << 23,
-    )(base, links, phi, low, high)
-    return exchange(done, BLOCK)
-
-
-def contract(matrices, values):
-    product = functools.partial(jnp.einsum, "xl,sral->sra", precision=lax.Precision.HIGHEST)
-    by_re, by_im = product(matrices[0], values), product(matrices[1], values)
-    real_part = by_re[:, 0] - by_im[:, 1]
-    imag_part = by_re[:, 1] + by_im[:, 0]
-    return jnp.stack([real_part, imag_part], 1)
+    )(below, above, base, links, low, high)
+    return exchange(done, BLOCK), kept
+
+
+def finish_kernel(mine_ref, total_ref, matrix_ref, projected_ref, contracted_ref):
+    lane = lax.broadcasted_iota(jnp.int32, (8, 128), 1)
+    row_re = jnp.broadcast_to(matrix_ref[0:1], (8, 128))
+    row_im = jnp.broadcast_to(matrix_ref[1:2], (8, 128))
+    pick = lane == mine_ref[0]
+    own, by_re, by_im = (jnp.zeros((8, 128), F32) for _ in range(3))
+    for pair in range(6):
+        both = total_ref[pair].astype(F32)
+        for which in range(2):
+            value = both[8 * which : 8 * which + 8]
+            here = lane == 2 * pair + which
+            own = jnp.where(here, jnp.sum(jnp.where(pick, value, 0.0), 1, keepdims=True), own)
+            by_re = jnp.where(here, jnp.sum(value * row_re, 1, keepdims=True), by_re)
+            by_im = jnp.where(here, jnp.sum(value * row_im, 1, keepdims=True), by_im)
+    crossed = pltpu.roll(by_im, 4, 0)
+    upper = lax.broadcasted_iota(jnp.int32, (8, 128), 0) < 4
+    contracted = by_re + jnp.where(upper, -crossed, crossed)
+    for row in range(8):
+        projected_ref[row] = own[row : row + 1, :12]
+        contracted_ref[row] = contracted[row : row + 1, :12]
 
 
 def placed_out(values):
-    return values.transpose(1, 2, 0)[None, :, :, :, None]
+    return values.reshape(1, 2, 4, 1, 12).transpose(0, 1, 2, 4, 3)
 
 
 def local(sources, gauge_links, eigenvectors, elementals):
     vectors = eigenvectors[0, :, :, :, 0].transpose(2, 1, 0, 3)
-    finals = spinors(sources, gauge_links)
+    finals, kept = spinors(sources, gauge_links, elementals[0, :, 0])
     partial_value = local_call(
-        project_kernel, jax.ShapeDtypeStruct((8, 16, 128), F32), [], 1 << 25
+        project_kernel, jax.ShapeDtypeStruct((8, 16, 128), BF16), [], 1 << 25
     )(finals, vectors)
-    totals = all_reduce(partial_value)[:6].reshape(12, 2, 4, 128)
-    mine = lax.dynamic_slice_in_dim(totals, lax.axis_index(SPACE), 1, 3)[..., 0]
-    return placed_out(mine), placed_out(contract(elementals[0], totals))
+    totals = all_reduce(partial_value)
+    mine = lax.axis_index(SPACE).astype(jnp.int32).reshape(1)
+    shape = jax.ShapeDtypeStruct((8, 1, 12), F32)
+    projected, contracted = local_call(
+        finish_kernel,
+        (shape, shape),
+        [],
+        1 << 17,
+        in_specs=[pl.BlockSpec(memory_space=pltpu.SMEM)] + [pl.BlockSpec()] * 2,
+    )(mine, totals, kept)
+    return placed_out(projected), placed_out(contracted)
 
 
 def solution(mesh):

time: 102 us -> 93 us (0.912)
  waiting for transfers between devices: 20.9 us -> 16.5 us
  starting transfers between devices: 31.7 us -> 28.7 us
  Pallas kernels: 3.35 us -> 5.82 us
  local copies, waits for them, and re-layouts: 3.78 us -> 1.63 us
  matrix products: 1.15 us -> 0 us
    ppermute x4, waiting for transfers between devices: 11.8 us -> 7.55 us  [from_behind(): lax.ppermute(value, axes, [(i, (i + steps) % count) for i in range(count)])]
    ppermute x4, starting transfers between devices: 21.7 us -> 18.9 us  [from_behind(): lax.ppermute(value, axes, [(i, (i + steps) % count) for i in range(count)])]
    pallas_call x3 -> x6, Pallas kernels: 3.3 us -> 5.77 us  [the longest x1 3.91 us: spinors(): local_call(sweep_kernel, jax.ShapeDtypeStruct((8, FIELD, SITES), BF16), [...]
    dot_general x2 -> x0, matrix products: 1.15 us -> none  [contract(): by_re, by_im = (product(matrices[0], values), product(matrices[1], values))]
  transfers between devices with their start and end apart: 6 -> 6, of which waited for: 5 -> 3; matrix products, arithmetic and copies ran while one was open for 0% -> 0% of each run, Pallas kernels for 0% -> 0%
where the time goes in v3:
time: 93 us; the launch traced here: 92.4 us
  blocking collectives  39.1 us (42%)
  starting transfers between devices  28.7 us (31%)
  waiting for transfers between devices  16.5 us (18%)
  Pallas kernels  5.82 us (6%)
  local copies, waits for them, and re-layouts  1.63 us (2%)
    all_to_all x3, blocking collectives, exchange(): return lax.all_to_all(value, axes, 0, 0, tiled=True)  39.1 us
    ppermute x4, starting transfers between devices, from_behind(): lax.ppermute(value, axes, [(i, (i + steps) % count) for i in range(count)])  18.9 us
    all_to_all x2, starting transfers between devices, exchange(): return lax.all_to_all(value, axes, 0, 0, tiled=True)  9.75 us
    all_to_all x2, waiting for transfers between devices, exchange(): return lax.all_to_all(value, axes, 0, 0, tiled=True)  8.97 us
    ppermute x4, waiting for transfers between devices, from_behind(): lax.ppermute(value, axes, [(i, (i + steps) % count) for i in range(count)])  7.55 us
    pallas_call x1, Pallas kernels, spinors(): local_call(sweep_kernel, jax.ShapeDtypeStruct((8, FIELD, SITES), BF16), [...  3.91 us
  transfers between devices with their start and end apart: 6, of which 3 were waited for; matrix products, arithmetic and copies ran while one was open for 0% of the time, Pallas kernels for 0%

profile of v3, /device:TPU:8, one launch (start us, length us, event | category | flops | bytes accessed | tf_op | source)
XLA Modules:
  0.0 92.4 jit_solution(207019257688538955)
XLA Ops:
  0.6 0.0 copy-start
  0.6 0.9 copy-done
  1.5 0.7 copy-done.1
  2.3 13.5 %all_to_all.25.own_ref = bf16[8,120,128]{2,1,0:T(8,128)(2,1)S(1)} all-to-all(bf16[8,120,128]{2,1,0:T(8,128)(2,1)S(1)} %shard_map.59), channel_id=1, replica_groups=mesh['y_hi'=2,'core'=2,'x'=4,'z'=16,'y_lo'=2] {'y_lo','y_hi','core'}, dimensions={0} | all-to-all | bytes 491520 | tf_op jit(solution)/shard_map/all_to_all | solution.py:25
  15.7 2.0 %collective-permute-start = (bf16[8,120,128]{2,1,0:T(8,128)(2,1)S(1)}, bf16[8,120,128]{2,1,0:T(8,128)(2,1)S(1)}, u32[]{:S(2)}, u32[]{:S(2)}) collective-permute-start(bf16[8,120,128]{2,1,0:T(8,128)(2,1)S(1)} %all_to_all.25.own_ref), channel_id=1, source_target_pairs={{0,2},{2,4},{4,6},{6,8},{8,10},{10,12},{12,14},{14,16},{16,18},{18... | collective-permute-start | bytes 737288 | tf_op jit(solution)/shard_map/ppermute | solution.py:30
  17.8 10.1 %collective-permute-start.1 = (bf16[8,120,128]{2,1,0:T(8,128)(2,1)S(1)}, bf16[8,120,128]{2,1,0:T(8,128)(2,1)S(1)}, u32[]{:S(2)}, u32[]{:S(2)}) collective-permute-start(bf16[8,120,128]{2,1,0:T(8,128)(2,1)S(1)} %all_to_all.25.own_ref), channel_id=1, source_target_pairs={{0,126},{2,0},{4,2},{6,4},{8,6},{10,8},{12,10},{14,12},{16,14},{18... | collective-permute-start | bytes 737288 | tf_op jit(solution)/shard_map/ppermute | solution.py:30
  27.9 0.2 shard_map.60
  28.2 4.4 %collective-permute-start.2 = (bf16[12,8,128]{2,1,0:T(8,128)(2,1)S(1)}, bf16[12,8,128]{2,1,0:T(8,128)(2,1)S(1)}, u32[]{:S(2)}, u32[]{:S(2)}) collective-permute-start(bf16[12,8,128]{2,1,0:T(8,128)(2,1)S(1)} %get-tuple-element.11), channel_id=1, source_target_pairs={{0,124},{2,126},{4,0},{6,2},{8,4},{10,6},{12,8},{14,10},{16,12},{1... | collective-permute-start | bytes 73736 | tf_op jit(solution)/shard_map/ppermute | solution.py:30
  32.6 2.4 %collective-permute-start.3 = (bf16[12,8,128]{2,1,0:T(8,128)(2,1)S(1)}, bf16[12,8,128]{2,1,0:T(8,128)(2,1)S(1)}, u32[]{:S(2)}, u32[]{:S(2)}) collective-permute-start(bf16[12,8,128]{2,1,0:T(8,128)(2,1)S(1)} %get-tuple-element.12), channel_id=1, source_target_pairs={{0,4},{2,6},{4,8},{6,10},{8,12},{10,14},{12,16},{14,18},{16,20},{1... | collective-permute-start | bytes 73736 | tf_op jit(solution)/shard_map/ppermute | solution.py:30
  34.9 0.0 collective-permute-done.2.low_ref
  35.0 7.5 %collective-permute-done.3.high_ref = bf16[12,8,128]{2,1,0:T(8,128)(2,1)S(1)} collective-permute-done((bf16[12,8,128]{2,1,0:T(8,128)(2,1)S(1)}, bf16[12,8,128]{2,1,0:T(8,128)(2,1)S(1)}, u32[]{:S(2)}, u32[]{:S(2)}) %collective-permute-start.3) | collective-permute-done | bytes 24608 | tf_op jit(solution)/shard_map/ppermute | solution.py:30
  42.5 0.0 collective-permute-done.below_ref
  42.5 0.0 collective-permute-done.1.above_ref
  42.5 3.9 %shard_map.61 = bf16[8,48,128]{2,1,0:T(8,128)(2,1)} custom-call(bf16[8,120,128]{2,1,0:T(8,128)(2,1)S(1)} %collective-permute-done.below_ref, bf16[8,120,128]{2,1,0:T(8,128)(2,1)S(1)} %collective-permute-done.1.above_ref, f32[2,24,8,128]{3,2,1,0:T(8,128)S(1)} %get-tuple-element.9.base_ref, f32[2,72,8,128]{3,2,1,0:T(8,128)S(1)} %get-tuple-element.10.link_ref, ...), custom_call_target="tpu_custom_call" | custom-call | flops 16777216 | bytes 1048576 | tf_op jit(solution)/shard_map/pallas_call | solution.py:365
  46.4 5.2 %all-to-all-start.1 = ((bf16[8,48,128]{2,1,0:T(8,128)(2,1)}), bf16[8,48,128]{2,1,0:T(8,128)(2,1)S(1)}, u32[]{:S(2)}, u32[]{:S(2)}) async-start(bf16[8,48,128]{2,1,0:T(8,128)(2,1)} %shard_map.61), calls=%async_computation.1 | async-start | bytes 196608 | tf_op jit(solution)/shard_map/all_to_all | solution.py:25
  51.6 0.0 copy-done.3
  51.6 4.1 %all-to-all-done.1.phi_ref = bf16[8,48,128]{2,1,0:T(8,128)(2,1)S(1)} async-done(((bf16[8,48,128]{2,1,0:T(8,128)(2,1)}), bf16[8,48,128]{2,1,0:T(8,128)(2,1)S(1)}, u32[]{:S(2)}, u32[]{:S(2)}) %all-to-all-start.1) | async-done | bytes 98336 | tf_op jit(solution)/shard_map/all_to_all | solution.py:25
  55.7 0.3 shard_map.62
  56.0 8.8 %all_to_all.26.value_ref = bf16[8,16,128]{2,1,0:T(8,128)(2,1)S(1)} all-to-all(bf16[8,16,128]{2,1,0:T(8,128)(2,1)S(1)} %shard_map.62), channel_id=1, replica_groups=mesh['y_hi'=2,'core'=2,'x'=4,'z'=16,'y_lo'=2] {'x','y_lo'}, dimensions={0} | all-to-all | bytes 65536 | tf_op jit(solution)/shard_map/all_to_all | solution.py:25
  64.8 16.8 %all_to_all.27.value_ref = bf16[16,16,128]{2,1,0:T(8,128)(2,1)S(1)} all-to-all(bf16[16,16,128]{2,1,0:T(8,128)(2,1)S(1)} %shard_map.63), channel_id=1, replica_groups=mesh['y_hi'=2,'core'=2,'x'=4,'z'=16,'y_lo'=2] {'z'}, dimensions={0} | all-to-all | bytes 131072 | tf_op jit(solution)/shard_map/all_to_all | solution.py:25
  81.6 0.6 shard_map.64
  82.2 4.6 %all-to-all-start.4 = ((bf16[8,16,128]{2,1,0:T(8,128)(2,1)}), bf16[8,16,128]{2,1,0:T(8,128)(2,1)S(1)}, u32[]{:S(2)}, u32[]{:S(2)}) async-start(bf16[8,16,128]{2,1,0:T(8,128)(2,1)} %shard_map.64), calls=%async_computation.4 | async-start | bytes 65536 | tf_op jit(solution)/shard_map/all_to_all | solution.py:25
  86.8 4.9 %all-to-all-done.4.total_ref = bf16[8,16,128]{2,1,0:T(8,128)(2,1)S(1)} async-done(((bf16[8,16,128]{2,1,0:T(8,128)(2,1)}), bf16[8,16,128]{2,1,0:T(8,128)(2,1)S(1)}, u32[]{:S(2)}, u32[]{:S(2)}) %all-to-all-start.4) | async-done | bytes 32800 | tf_op jit(solution)/shard_map/all_to_all | solution.py:25
  91.7 0.7 shard_map.65
  (7 shorter events, 0.1 us)
Async XLA Ops:
  0.6 0.9 copy-start
  1.5 0.7 copy-start.1
  15.7 12.2 %copy-start.2 = (f32[1,2,1,128]{3,2,1,0:T(1,128)S(1)}, f32[1,2,1,128]{3,2,1,0:T(1,128)}, u32[]{:S(2)}) copy-start(f32[1,2,1,128]{3,2,1,0:T(1,128)} %param.7) | copy-start | bytes 3076
  15.7 26.8 %collective-permute-start = (bf16[8,120,128]{2,1,0:T(8,128)(2,1)S(1)}, bf16[8,120,128]{2,1,0:T(8,128)(2,1)S(1)}, u32[]{:S(2)}, u32[]{:S(2)}) collective-permute-start(bf16[8,120,128]{2,1,0:T(8,128)(2,1)S(1)} %all_to_all.25.own_ref), channel_id=1, source_target_pairs={{0,2},{2,4},{4,6},{6,8},{8,10},{10,12},{12,14},{14,16},{16,18},{18... | collective-permute-start | bytes 737288 | tf_op jit(solution)/shard_map/ppermute | solution.py:30
  17.8 24.7 %collective-permute-start.1 = (bf16[8,120,128]{2,1,0:T(8,128)(2,1)S(1)}, bf16[8,120,128]{2,1,0:T(8,128)(2,1)S(1)}, u32[]{:S(2)}, u32[]{:S(2)}) collective-permute-start(bf16[8,120,128]{2,1,0:T(8,128)(2,1)S(1)} %all_to_all.25.own_ref), channel_id=1, source_target_pairs={{0,126},{2,0},{4,2},{6,4},{8,6},{10,8},{12,10},{14,12},{16,14},{18... | collective-permute-start | bytes 737288 | tf_op jit(solution)/shard_map/ppermute | solution.py:30
  28.2 6.8 %collective-permute-start.2 = (bf16[12,8,128]{2,1,0:T(8,128)(2,1)S(1)}, bf16[12,8,128]{2,1,0:T(8,128)(2,1)S(1)}, u32[]{:S(2)}, u32[]{:S(2)}) collective-permute-start(bf16[12,8,128]{2,1,0:T(8,128)(2,1)S(1)} %get-tuple-element.11), channel_id=1, source_target_pairs={{0,124},{2,126},{4,0},{6,2},{8,4},{10,6},{12,8},{14,10},{16,12},{1... | collective-permute-start | bytes 73736 | tf_op jit(solution)/shard_map/ppermute | solution.py:30
  32.6 9.9 %collective-permute-start.3 = (bf16[12,8,128]{2,1,0:T(8,128)(2,1)S(1)}, bf16[12,8,128]{2,1,0:T(8,128)(2,1)S(1)}, u32[]{:S(2)}, u32[]{:S(2)}) collective-permute-start(bf16[12,8,128]{2,1,0:T(8,128)(2,1)S(1)} %get-tuple-element.12), channel_id=1, source_target_pairs={{0,4},{2,6},{4,8},{6,10},{8,12},{10,14},{12,16},{14,18},{16,20},{1... | collective-permute-start | bytes 73736 | tf_op jit(solution)/shard_map/ppermute | solution.py:30
  46.4 5.2 %copy-start.3 = (bf16[1,128,2,3,1,128]{5,2,4,3,1,0:T(2,128)(2,1)S(1)}, bf16[1,128,2,3,1,128]{5,2,4,3,1,0:T(2,128)(2,1)}, u32[]{:S(2)}) copy-start(bf16[1,128,2,3,1,128]{5,2,4,3,1,0:T(2,128)(2,1)} %param.6) | copy-start | bytes 589828
  46.4 9.3 %all-to-all-start.1 = ((bf16[8,48,128]{2,1,0:T(8,128)(2,1)}), bf16[8,48,128]{2,1,0:T(8,128)(2,1)S(1)}, u32[]{:S(2)}, u32[]{:S(2)}) async-start(bf16[8,48,128]{2,1,0:T(8,128)(2,1)} %shard_map.61), calls=%async_computation.1 | async-start | bytes 196608 | tf_op jit(solution)/shard_map/all_to_all | solution.py:25
  82.2 9.5 %all-to-all-start.4 = ((bf16[8,16,128]{2,1,0:T(8,128)(2,1)}), bf16[8,16,128]{2,1,0:T(8,128)(2,1)S(1)}, u32[]{:S(2)}, u32[]{:S(2)}) async-start(bf16[8,16,128]{2,1,0:T(8,128)(2,1)} %shard_map.64), calls=%async_computation.4 | async-start | bytes 65536 | tf_op jit(solution)/shard_map/all_to_all | solution.py:25

commit v4 on v3

--- a/solution.py
+++ b/solution.py
@@ -8,10 +8,12 @@
 
 HOPPING = 0.125
 TM = ("y_hi", "core")
-SPACE = ("x", "z", "y_lo")
+SPACE = ("x", "z_hi", "z_lo", "y_lo")
 PLANE = ("x", "y_lo")
-POSITION = ("x", "z")
-BLOCK = ("y_lo", "y_hi", "core")
+DEPTH = ("z_hi", "z_lo")
+POSITION = ("x", *DEPTH)
+BLOCK = ("y_lo", *TM)
+GROUP = ("z_lo", *BLOCK)
 LX = 8
 FIELD = 48
 LINK = 72
@@ -25,9 +27,10 @@
     return lax.all_to_all(value, axes, 0, 0, tiled=True)
 
 
-def from_behind(value, axes, steps):
+def send(value, axes, steps):
     count = lax.axis_size(axes)
-    return lax.ppermute(value, axes, [(i, (i + steps) % count) for i in range(count)])
+    pairs = [(i, (i + steps[1] if i % 2 else i - steps[0]) % count) for i in range(count)]
+    return lax.ppermute(value, axes, pairs)
 
 
 def local_call(kernel, outs, scratch, flops, **options):
@@ -41,7 +44,9 @@
     )
 
 
-def pack_kernel(source_ref, link_ref, out_ref, rows, links):
+def pack_kernel(place_ref, source_ref, link_ref, out_ref, side_ref, mine_ref, rows, links):
+    side_ref[0] = place_ref[0]
+    mine_ref[0] = place_ref[1]
     for entry in range(36):
         links[2 * entry : 2 * entry + 2] = link_ref[entry].astype(F32)
     shared = links[...]
@@ -57,7 +62,9 @@
                     else:
                         piece = jnp.zeros((4, SITES), F32)
                     rows[target, at : at + 4] = piece
-    out_ref[...] = rows[...].astype(BF16)
+    packed = rows[...].astype(BF16)
+    out_ref[:8] = packed
+    out_ref[8:] = packed
 
 
 def signed_add(base, sign, value):
@@ -220,35 +227,59 @@
     return color_apply(link, 2, half_of(field, 2, 1), True)
 
 
-def own_kernel(own_ref, matrix_ref, base_ref, link_ref, low_ref, high_ref, kept_ref, wide):
-    kept_ref[...] = matrix_ref[...]
-    wide[...] = own_ref[...].reshape(8 * ROWS, SITES).astype(F32)
+def own_kernel(side_ref, own_ref, base_ref, link_ref, near_ref, far_ref, wide):
+    wide[...] = own_ref[...].reshape(16 * ROWS, SITES).astype(F32)
+    side = side_ref[0]
 
     def one(layer, carry):
         assemble(wide, layer * 4 * ROWS, base_ref, link_ref, layer)
         return carry
 
-    lax.fori_loop(0, 2, one, 0)
-    put_half(low_ref, sent_down(field_at(base_ref, 0)))
-    put_half(high_ref, sent_up(field_at(base_ref, 1), link_at(link_ref, 1)))
+    lax.fori_loop(0, 4, one, 0)
+    near_ref[: 8 * ROWS] = own_ref[pl.ds(side * 8, 8)].reshape(8 * ROWS, SITES)
+
+    def put(ref, start, below, above):
+        for color in range(3):
+            for a in range(2):
+                at = start + 8 * half_slot(0, color, a)
+                low = jnp.concatenate(below[color][a], 0)
+                high = jnp.concatenate(above[color][a], 0)
+                ref[at : at + 16] = jnp.where(side == 0, low, high).astype(BF16)
+
+    def half_down(layer):
+        return sent_down(field_at(base_ref, layer))
+
+    def half_up(layer):
+        return sent_up(field_at(base_ref, layer), link_at(link_ref, layer))
+
+    put(near_ref, 8 * ROWS, half_down(2), half_up(1))
+    put(far_ref, 0, half_down(0), half_up(3))
+
+
+def keep_kernel(far_ref, matrix_ref, vector_ref, kept_matrix, kept_vector, tie_ref):
+    kept_matrix[...] = matrix_ref[...]
+    kept_vector[...] = vector_ref[...]
+    tie_ref[...] = far_ref[:16]
 
 
 def sweep_kernel(
-    below_ref, above_ref, base_ref, link_ref, low_ref, high_ref, out_ref,
+    side_ref, near_ref, far_ref, base_ref, link_ref, tie_ref, out_ref,
     wide, src, one, two, links, ahead, behind, done,
 ):
-    for at, ref in enumerate((below_ref, above_ref)):
-        wide[at * 8 * ROWS : (at + 1) * 8 * ROWS] = ref[...].reshape(8 * ROWS, SITES).astype(F32)
+    side = side_ref[0]
+    wide[...] = near_ref[: 8 * ROWS].astype(F32)
 
     def gather(layer, carry):
-        assemble(wide, layer * 4 * ROWS, src, links, layer + 2 * (layer // 2))
+        assemble(wide, layer * 4 * ROWS, src, links, layer + 4 * side)
         return carry
 
-    lax.fori_loop(0, 4, gather, 0)
-    src[2:4] = base_ref[...]
-    links[2:4] = link_ref[...]
-    ahead[6] = low_ref[...].astype(F32)
-    behind[0] = high_ref[...].astype(F32)
+    lax.fori_loop(0, 2, gather, 0)
+    src[pl.ds(2 - 2 * side, 4)] = base_ref[...]
+    links[pl.ds(2 - 2 * side, 4)] = link_ref[...]
+    near = near_ref[8 * ROWS :].astype(F32).reshape(12, 8, SITES)
+    far = far_ref[...].astype(F32).reshape(12, 8, SITES)
+    ahead[6] = jnp.where(side == 0, far, near)
+    behind[0] = jnp.where(side == 0, near, far)
 
     def sweep(from_ref, halves, layers, put):
         def prepare(layer, carry):
@@ -326,47 +357,61 @@
 
 def all_reduce(partial_value):
     plane = lax.axis_size(PLANE)
-    depth = lax.axis_size("z")
+    depth = lax.axis_size(DEPTH)
     copies = summed(exchange(partial_value, PLANE), depth)
-    copies = summed(exchange(copies, "z"), plane)
+    copies = summed(exchange(copies, DEPTH), plane)
     return exchange(copies, PLANE)
 
 
-def spinors(sources, gauge_links, matrix):
+def spinors(sources, gauge_links, kept):
     moved = sources[0, :, :, :, :, 0].transpose(0, 2, 3, 1, 4)
     entries = gauge_links[:, 0, :, :, :, 0].transpose(0, 2, 3, 1, 4).reshape(36, 2, SITES)
-    packed = local_call(
+    smem = [pl.BlockSpec(memory_space=pltpu.SMEM)]
+    scalar = jax.ShapeDtypeStruct((1,), jnp.int32)
+    place = jnp.stack([lax.axis_index("z_lo"), lax.axis_index(SPACE)]).astype(jnp.int32)
+    packed, side, mine = local_call(
         pack_kernel,
-        jax.ShapeDtypeStruct((8, ROWS, SITES), BF16),
+        (jax.ShapeDtypeStruct((16, ROWS, SITES), BF16), scalar, scalar),
         [
             pltpu.VMEM((8, ROWS, SITES), F32),
             pltpu.VMEM((LINK, SITES), F32),
         ],
         1 << 17,
-    )(moved, entries)
-    own = exchange(packed, BLOCK)
-    below = from_behind(own, POSITION, 1)
-    above = from_behind(own, POSITION, -1)
+        in_specs=smem + [pl.BlockSpec()] * 2,
+        out_specs=(pl.BlockSpec(), *smem, *smem),
+    )(place, moved, entries)
+    own = exchange(packed, GROUP)
     vectors = (8, SITES)
-    base, links, low, high, kept = local_call(
+    base, links, near, far = local_call(
         own_kernel,
         (
-            jax.ShapeDtypeStruct((2, 24, *vectors), F32),
-            jax.ShapeDtypeStruct((2, LINK, *vectors), F32),
-            jax.ShapeDtypeStruct((12, *vectors), BF16),
-            jax.ShapeDtypeStruct((12, *vectors), BF16),
+            jax.ShapeDtypeStruct((4, 24, *vectors), F32),
+            jax.ShapeDtypeStruct((4, LINK, *vectors), F32),
+            jax.ShapeDtypeStruct((8 * ROWS + 96, SITES), BF16),
+            jax.ShapeDtypeStruct((96, SITES), BF16),
+        ),
+        [pltpu.VMEM((16 * ROWS, SITES), F32)],
+        1 << 20,
+        in_specs=smem + [pl.BlockSpec()],
+    )(side, own)
+    matrix, spectrum = kept
+    *kept, tie = local_call(
+        keep_kernel,
+        (
             jax.ShapeDtypeStruct(matrix.shape, F32),
+            jax.ShapeDtypeStruct(spectrum.shape, BF16),
+            jax.ShapeDtypeStruct((16, SITES), BF16),
         ),
-        [pltpu.VMEM((8 * ROWS, SITES), F32)],
-        1 << 20,
-    )(own, matrix)
-    high = from_behind(high, POSITION, 2)
-    low = from_behind(low, POSITION, -2)
+        [],
+        1 << 18,
+    )(far, matrix, spectrum)
+    near = send(near, POSITION, (1, 1))
+    far = send(far, POSITION, (2, 2))
     done = local_call(
         sweep_kernel,
         jax.ShapeDtypeStruct((8, FIELD, SITES), BF16),
         [
-            pltpu.VMEM((2 * 8 * ROWS, SITES), F32),
+            pltpu.VMEM((8 * ROWS, SITES), F32),
             pltpu.VMEM((6, 24, *vectors), F32),
             pltpu.VMEM((6, 24, *vectors), F32),
             pltpu.VMEM((6, 24, *vectors), F32),
@@ -376,8 +421,9 @@
             pltpu.VMEM((2 * 24 * 8, SITES), F32),
         ],
         1 << 24,
-    )(below, above, base, links, low, high)
-    return exchange(done, BLOCK), kept
+        in_specs=smem + [pl.BlockSpec()] * 5,
+    )(side, near, far, base, links, tie)
+    return exchange(done, BLOCK), mine, kept
 
 
 def finish_kernel(mine_ref, total_ref, matrix_ref, projected_ref, contracted_ref):
@@ -408,12 +454,12 @@
 
 def local(sources, gauge_links, eigenvectors, elementals):
     vectors = eigenvectors[0, :, :, :, 0].transpose(2, 1, 0, 3)
-    finals, kept = spinors(sources, gauge_links, elementals[0, :, 0])
+    kept = (elementals[0, :, 0], vectors)
+    finals, mine, (matrix, vectors) = spinors(sources, gauge_links, kept)
     partial_value = local_call(
         project_kernel, jax.ShapeDtypeStruct((8, 16, 128), BF16), [], 1 << 25
     )(finals, vectors)
     totals = all_reduce(partial_value)
-    mine = lax.axis_index(SPACE).astype(jnp.int32).reshape(1)
     shape = jax.ShapeDtypeStruct((8, 1, 12), F32)
     projected, contracted = local_call(
         finish_kernel,
@@ -421,12 +467,12 @@
         [],
         1 << 17,
         in_specs=[pl.BlockSpec(memory_space=pltpu.SMEM)] + [pl.BlockSpec()] * 2,
-    )(mine, totals, kept)
+    )(mine, totals, matrix)
     return placed_out(projected), placed_out(contracted)
 
 
 def solution(mesh):
-    fine = Mesh(mesh.devices.reshape(2, 2, 4, 16, 2), (*TM, *SPACE))
+    fine = Mesh(mesh.devices.reshape(2, 2, 4, 8, 2, 2), (*TM, *SPACE))
     placed = (
         P(TM, None, None, None, None, SPACE, None),
         P(None, TM, None, None, None, SPACE, None),

time: 93 us -> 91.6 us (0.985)
  blocking collectives: 39.1 us -> 62.4 us
  starting transfers between devices: 28.7 us -> 15.2 us
  waiting for transfers between devices: 16.5 us -> 3.56 us
  Pallas kernels: 5.82 us -> 7.65 us
    all_to_all x3 -> x5, blocking collectives: 39.1 us -> 62.4 us  [exchange(): return lax.all_to_all(value, axes, 0, 0, tiled=True)]
    all_to_all x2 -> x0, starting transfers between devices: 9.75 us -> none  [exchange(): return lax.all_to_all(value, axes, 0, 0, tiled=True)]
    all_to_all x2 -> x0, waiting for transfers between devices: 8.97 us -> none  [exchange(): return lax.all_to_all(value, axes, 0, 0, tiled=True)]
    ppermute x4 -> x2, waiting for transfers between devices: 7.55 us -> 3.56 us  [send(): return lax.ppermute(value, axes, pairs)]
    ppermute x4 -> x2, starting transfers between devices: 18.9 us -> 15.2 us  [send(): return lax.ppermute(value, axes, pairs)]
    pallas_call x2 -> x3, Pallas kernels: 0.29 us -> 2.24 us  [the longest x1 1.13 us: spinors(): local_call(own_kernel, (jax.ShapeDtypeStruct((4, 24, *vectors), F32), jax...]
  transfers between devices with their start and end apart: 6 -> 2, of which waited for: 3 -> 2; matrix products, arithmetic and copies ran while one was open for 0% -> 0% of each run, Pallas kernels for 0% -> 0%
where the time goes in v4:
time: 91.6 us; the launch traced here: 91.2 us
  blocking collectives  62.4 us (68%)
  starting transfers between devices  15.2 us (17%)
  Pallas kernels  7.65 us (8%)
  waiting for transfers between devices  3.56 us (4%)
  local copies, waits for them, and re-layouts  1.64 us (2%)
    all_to_all x5, blocking collectives, exchange(): return lax.all_to_all(value, axes, 0, 0, tiled=True)  62.4 us
    ppermute x2, starting transfers between devices, send(): return lax.ppermute(value, axes, pairs)  15.2 us
    pallas_call x1, Pallas kernels, spinors(): local_call(sweep_kernel, jax.ShapeDtypeStruct((8, FIELD, SITES), BF16), [...  3.77 us
    ppermute x2, waiting for transfers between devices, send(): return lax.ppermute(value, axes, pairs)  3.56 us
  transfers between devices with their start and end apart: 2, of which 2 were waited for; matrix products, arithmetic and copies ran while one was open for 0% of the time, Pallas kernels for 0%

profile of v4, /device:TPU:8, one launch (start us, length us, event | category | flops | bytes accessed | tf_op | source)
XLA Modules:
  0.0 91.2 jit_solution(14260143817358362724)
XLA Ops:
  0.6 0.0 copy-start.2
  0.6 0.1 pad_add_fusion.place_ref
  0.7 0.0 copy-start
  0.7 0.9 copy-done
  1.6 0.0 copy-start.1
  1.6 0.7 copy-done.1
  2.3 0.0 copy-start.3
  2.3 1.1 %shard_map.59 = (bf16[16,120,128]{2,1,0:T(8,128)(2,1)S(1)}, s32[1]{0:T(128)}, s32[1]{0:T(128)}) custom-call(s32[2]{0:T(128)S(1)} %pad_add_fusion.place_ref, bf16[2,3,12,4,128]{4,3,2,1,0:T(4,128)(2,1)S(1)} %bitcast.23, bf16[36,2,128]{2,1,0:T(2,128)(2,1)S(1)} %bitcast.24), custom_call_target="tpu_custom_call" | custom-call | flops 131072 | bytes 1048576 | tf_op jit(solution)/shard_map/pallas_call | solution.py:372
  3.4 15.9 %all_to_all.25.own_ref = bf16[16,120,128]{2,1,0:T(8,128)(2,1)S(1)} all-to-all(bf16[16,120,128]{2,1,0:T(8,128)(2,1)S(1)} %get-tuple-element.16), channel_id=1, replica_groups=mesh['y_hi'=2,'core'=2,'x'=4,'z_hi'=8,'z_lo'=2,'y_lo'=2] {'z_lo','y_lo',..., dimensions={0} | all-to-all | bytes 983040 | tf_op jit(solution)/shard_map/all_to_all | solution.py:27
  19.3 1.1 %shard_map.60 = (f32[4,24,8,128]{3,2,1,0:T(8,128)S(1)}, f32[4,72,8,128]{3,2,1,0:T(8,128)S(1)}, bf16[1056,128]{1,0:T(8,128)(2,1)S(1)}, bf16[96,128]{1,0:T(8,128)(2,1)S(1)}) custom-call(s32[1]{0:T(128)} %get-tuple-element.15.side_ref, bf16[16,120,128]{2,1,0:T(8,128)(2,1)S(1)} %all_to_all.25.own_ref), custom_call_target="tpu_custom_call" | custom-call | flops 1048576 | bytes 1048576 | tf_op jit(solution)/shard_map/pallas_call | solution.py:385
  20.4 11.8 %collective-permute-start = (bf16[1056,128]{1,0:T(8,128)(2,1)S(1)}, bf16[1056,128]{1,0:T(8,128)(2,1)S(1)}, u32[]{:S(2)}, u32[]{:S(2)}) collective-permute-start(bf16[1056,128]{1,0:T(8,128)(2,1)S(1)} %get-tuple-element.17), channel_id=1, source_target_pairs={{0,126},{2,4},{4,2},{6,8},{8,6},{10,12},{12,10},{14,16},{16,14},{1... | collective-permute-start | bytes 811016 | tf_op jit(solution)/shard_map/ppermute | solution.py:33
  32.3 3.4 %collective-permute-start.1 = (bf16[96,128]{1,0:T(8,128)(2,1)S(1)}, bf16[96,128]{1,0:T(8,128)(2,1)S(1)}, u32[]{:S(2)}, u32[]{:S(2)}) collective-permute-start(bf16[96,128]{1,0:T(8,128)(2,1)S(1)} %get-tuple-element.18.far_ref), channel_id=1, source_target_pairs={{0,124},{2,6},{4,0},{6,10},{8,4},{10,14},{12,8},{14,18},{16,12},{1... | collective-permute-start | bytes 73736 | tf_op jit(solution)/shard_map/ppermute | solution.py:33
  35.6 0.0 copy-done.3
  35.7 0.0 copy-done.2
  35.7 3.2 %collective-permute-done.1.far_ref = bf16[96,128]{1,0:T(8,128)(2,1)S(1)} collective-permute-done((bf16[96,128]{1,0:T(8,128)(2,1)S(1)}, bf16[96,128]{1,0:T(8,128)(2,1)S(1)}, u32[]{:S(2)}, u32[]{:S(2)}) %collective-permute-start.1) | collective-permute-done | bytes 24608 | tf_op jit(solution)/shard_map/ppermute | solution.py:33
  38.9 0.4 collective-permute-done.near_ref
  39.3 3.8 %shard_map.62 = bf16[8,48,128]{2,1,0:T(8,128)(2,1)S(1)} custom-call(s32[1]{0:T(128)} %get-tuple-element.15.side_ref, bf16[1056,128]{1,0:T(8,128)(2,1)S(1)} %collective-permute-done.near_ref, bf16[96,128]{1,0:T(8,128)(2,1)S(1)} %collective-permute-done.1.far_ref, f32[4,24,8,128]{3,2,1,0:T(8,128)S(1)} %get-tuple-element.19.base_ref, ...), custom_call_target="tpu_custom_call" | custom-call | flops 16777216 | bytes 1048576 | tf_op jit(solution)/shard_map/pallas_call | solution.py:410
  43.0 7.8 %all_to_all.26.phi_ref = bf16[8,48,128]{2,1,0:T(8,128)(2,1)S(1)} all-to-all(bf16[8,48,128]{2,1,0:T(8,128)(2,1)S(1)} %shard_map.62), channel_id=1, replica_groups=mesh['y_hi'=2,'core'=2,'x'=4,'z_hi'=8,'z_lo'=2,'y_lo'=2] {'y_lo','y_hi',..., dimensions={0} | all-to-all | bytes 196608 | tf_op jit(solution)/shard_map/all_to_all | solution.py:27
  50.8 0.3 shard_map.63
  51.1 8.8 %all_to_all.27.value_ref = bf16[8,16,128]{2,1,0:T(8,128)(2,1)S(1)} all-to-all(bf16[8,16,128]{2,1,0:T(8,128)(2,1)S(1)} %shard_map.63), channel_id=1, replica_groups=mesh['y_hi'=2,'core'=2,'x'=4,'z_hi'=8,'z_lo'=2,'y_lo'=2] {'x','y_lo'}, dimensions={0} | all-to-all | bytes 65536 | tf_op jit(solution)/shard_map/all_to_all | solution.py:27
  59.9 21.4 %all_to_all.28.value_ref = bf16[16,16,128]{2,1,0:T(8,128)(2,1)S(1)} all-to-all(bf16[16,16,128]{2,1,0:T(8,128)(2,1)S(1)} %shard_map.64), channel_id=1, replica_groups=mesh['y_hi'=2,'core'=2,'x'=4,'z_hi'=8,'z_lo'=2,'y_lo'=2] {'z_hi','z_lo'}, dimensions={0} | all-to-all | bytes 131072 | tf_op jit(solution)/shard_map/all_to_all | solution.py:27
  81.3 8.6 %all_to_all.29.total_ref = bf16[8,16,128]{2,1,0:T(8,128)(2,1)S(1)} all-to-all(bf16[8,16,128]{2,1,0:T(8,128)(2,1)S(1)} %shard_map.65), channel_id=1, replica_groups=mesh['y_hi'=2,'core'=2,'x'=4,'z_hi'=8,'z_lo'=2,'y_lo'=2] {'x','y_lo'}, dimensions={0} | all-to-all | bytes 65536 | tf_op jit(solution)/shard_map/all_to_all | solution.py:27
  89.8 1.3 %shard_map.66 = (f32[8,1,12]{2,1,0:T(1,128)}, f32[8,1,12]{2,1,0:T(1,128)}) custom-call(s32[1]{0:T(128)} %get-tuple-element.14.mine_ref, bf16[8,16,128]{2,1,0:T(8,128)(2,1)S(1)} %all_to_all.29.total_ref, f32[2,128]{1,0:T(2,128)S(1)} %get-tuple-element.23.matrix_ref), custom_call_target="tpu_custom_call" | custom-call | flops 131072 | bytes 1048576 | tf_op jit(solution)/shard_map/pallas_call | solution.py:464
  (4 shorter events, 0.1 us)
Async XLA Ops:
  0.6 35.0 %copy-start.2 = (f32[1,2,1,128]{3,2,1,0:T(1,128)S(1)}, f32[1,2,1,128]{3,2,1,0:T(1,128)}, u32[]{:S(2)}) copy-start(f32[1,2,1,128]{3,2,1,0:T(1,128)} %param.7) | copy-start | bytes 3076
  0.7 0.9 copy-start
  1.6 0.7 copy-start.1
  2.3 33.3 %copy-start.3 = (bf16[1,128,2,3,1,128]{5,2,4,3,1,0:T(2,128)(2,1)S(1)}, bf16[1,128,2,3,1,128]{5,2,4,3,1,0:T(2,128)(2,1)}, u32[]{:S(2)}) copy-start(bf16[1,128,2,3,1,128]{5,2,4,3,1,0:T(2,128)(2,1)} %param.6) | copy-start | bytes 589828
  20.4 18.8 %collective-permute-start = (bf16[1056,128]{1,0:T(8,128)(2,1)S(1)}, bf16[1056,128]{1,0:T(8,128)(2,1)S(1)}, u32[]{:S(2)}, u32[]{:S(2)}) collective-permute-start(bf16[1056,128]{1,0:T(8,128)(2,1)S(1)} %get-tuple-element.17), channel_id=1, source_target_pairs={{0,126},{2,4},{4,2},{6,8},{8,6},{10,12},{12,10},{14,16},{16,14},{1... | collective-permute-start | bytes 811016 | tf_op jit(solution)/shard_map/ppermute | solution.py:33
  32.3 6.6 %collective-permute-start.1 = (bf16[96,128]{1,0:T(8,128)(2,1)S(1)}, bf16[96,128]{1,0:T(8,128)(2,1)S(1)}, u32[]{:S(2)}, u32[]{:S(2)}) collective-permute-start(bf16[96,128]{1,0:T(8,128)(2,1)S(1)} %get-tuple-element.18.far_ref), channel_id=1, source_target_pairs={{0,124},{2,6},{4,0},{6,10},{8,4},{10,14},{12,8},{14,18},{16,12},{1... | collective-permute-start | bytes 73736 | tf_op jit(solution)/shard_map/ppermute | solution.py:33

commit v5 on v4

--- a/solution.py
+++ b/solution.py
@@ -44,9 +44,7 @@
     )
 
 
-def pack_kernel(place_ref, source_ref, link_ref, out_ref, side_ref, mine_ref, rows, links):
-    side_ref[0] = place_ref[0]
-    mine_ref[0] = place_ref[1]
+def pack_kernel(source_ref, link_ref, out_ref, rows, links):
     for entry in range(36):
         links[2 * entry : 2 * entry + 2] = link_ref[entry].astype(F32)
     shared = links[...]
@@ -227,9 +225,9 @@
     return color_apply(link, 2, half_of(field, 2, 1), True)
 
 
-def own_kernel(side_ref, own_ref, base_ref, link_ref, near_ref, far_ref, wide):
+def own_kernel(own_ref, base_ref, link_ref, near_ref, far_ref, wide):
     wide[...] = own_ref[...].reshape(16 * ROWS, SITES).astype(F32)
-    side = side_ref[0]
+    side = lax.axis_index("z_lo")
 
     def one(layer, carry):
         assemble(wide, layer * 4 * ROWS, base_ref, link_ref, layer)
@@ -256,63 +254,105 @@
     put(far_ref, 0, half_down(0), half_up(3))
 
 
-def keep_kernel(far_ref, matrix_ref, vector_ref, kept_matrix, kept_vector, tie_ref):
+def sweep_layer(from_ref, src_ref, link_ref, layer, ahead, behind, put):
+    total = hop(field_at(from_ref, layer), link_at(link_ref, layer), ahead, behind)
+    for key, value in total.items():
+        put(comp(*key), src_ref[layer, comp(*key)] + HOPPING * value)
+
+
+def prepare_layer(from_ref, link_ref, layer, ahead_ref, ahead_at, behind_ref, behind_at):
+    put_half(ahead_ref.at[ahead_at], sent_down(field_at(from_ref, layer)))
+    put_half(
+        behind_ref.at[behind_at], sent_up(field_at(from_ref, layer), link_at(link_ref, layer))
+    )
+
+
+def inner_kernel(
+    matrix_ref, vector_ref, base_ref, link_ref,
+    kept_matrix, kept_vector, inner_ref, ahead_ref, behind_ref,
+):
     kept_matrix[...] = matrix_ref[...]
     kept_vector[...] = vector_ref[...]
-    tie_ref[...] = far_ref[:16]
+
+    def prepare(layer, carry):
+        prepare_layer(base_ref, link_ref, layer, ahead_ref, layer, behind_ref, layer)
+        return carry
+
+    def step(layer, carry):
+        def put(at, value):
+            inner_ref[layer - 1, at] = value
+
+        ahead, behind = get_half(ahead_ref, layer + 1), get_half(behind_ref, layer - 1)
+        sweep_layer(base_ref, base_ref, link_ref, layer, ahead, behind, put)
+        return carry
+
+    lax.fori_loop(0, 4, prepare, 0)
+    lax.fori_loop(1, 3, step, 0)
 
 
 def sweep_kernel(
-    side_ref, near_ref, far_ref, base_ref, link_ref, tie_ref, out_ref,
+    near_ref, far_ref, base_ref, link_ref, inner_ref, ahead_ref, behind_ref, out_ref,
     wide, src, one, two, links, ahead, behind, done,
 ):
-    side = side_ref[0]
+    side = lax.axis_index("z_lo")
+    block, halo = 2 - 2 * side, 4 * side
     wide[...] = near_ref[: 8 * ROWS].astype(F32)
-
-    def gather(layer, carry):
-        assemble(wide, layer * 4 * ROWS, src, links, layer + 4 * side)
-        return carry
-
-    lax.fori_loop(0, 2, gather, 0)
-    src[pl.ds(2 - 2 * side, 4)] = base_ref[...]
-    links[pl.ds(2 - 2 * side, 4)] = link_ref[...]
+    src[pl.ds(block, 4)] = base_ref[...]
+    links[pl.ds(block, 4)] = link_ref[...]
+    one[pl.ds(block + 1, 2)] = inner_ref[...]
+    ahead[pl.ds(block, 4)] = ahead_ref[...]
+    behind[pl.ds(block + 1, 4)] = behind_ref[...]
     near = near_ref[8 * ROWS :].astype(F32).reshape(12, 8, SITES)
     far = far_ref[...].astype(F32).reshape(12, 8, SITES)
     ahead[6] = jnp.where(side == 0, far, near)
     behind[0] = jnp.where(side == 0, near, far)
 
-    def sweep(from_ref, halves, layers, put):
-        def prepare(layer, carry):
-            put_half(ahead.at[layer], sent_down(field_at(from_ref, layer)))
-            put_half(behind.at[layer + 1], sent_up(field_at(from_ref, layer), link_at(links, layer)))
-            return carry
-
-        def step(layer, carry):
-            total = hop(
-                field_at(from_ref, layer),
-                link_at(links, layer),
-                get_half(ahead, layer + 1),
-                get_half(behind, layer),
-            )
-            for key, value in total.items():
-                put(layer, comp(*key), src[layer, comp(*key)] + HOPPING * value)
-            return carry
-
-        lax.fori_loop(*halves, prepare, 0)
-        lax.fori_loop(*layers, step, 0)
-
-    def put_one(layer, at, value):
-        one[layer, at] = value
-
-    def put_two(layer, at, value):
-        two[layer, at] = value
-
-    def put_done(layer, at, value):
-        done[pl.ds(pl.multiple_of(((layer - 2) * 24 + at) * 8, 8), 8)] = value
-
-    sweep(src, (0, 6), (0, 6), put_one)
-    sweep(one, (0, 6), (1, 5), put_two)
-    sweep(two, (1, 5), (2, 4), put_done)
+    def gather(at, carry):
+        layer = halo + at
+        assemble(wide, at * 4 * ROWS, src, links, layer)
+        prepare_layer(src, links, layer, ahead, layer, behind, layer + 1)
+        return carry
+
+    def first(at, carry):
+        layer = at + jnp.where(at >= 3 - 2 * side, 2, 0)
+
+        def put(slot_at, value):
+            one[layer, slot_at] = value
+
+        halves = get_half(ahead, layer + 1), get_half(behind, layer)
+        sweep_layer(src, src, links, layer, *halves, put)
+        return carry
+
+    lax.fori_loop(0, 2, gather, 0)
+    lax.fori_loop(0, 4, first, 0)
+
+    def prepare_one(layer, carry):
+        prepare_layer(one, links, layer, ahead, layer, behind, layer + 1)
+        return carry
+
+    def second(layer, carry):
+        def put(at, value):
+            two[layer, at] = value
+
+        sweep_layer(one, src, links, layer, get_half(ahead, layer + 1), get_half(behind, layer), put)
+        return carry
+
+    lax.fori_loop(0, 6, prepare_one, 0)
+    lax.fori_loop(1, 5, second, 0)
+
+    def prepare_two(layer, carry):
+        prepare_layer(two, links, layer, ahead, layer, behind, layer + 1)
+        return carry
+
+    def third(layer, carry):
+        def put(at, value):
+            done[pl.ds(pl.multiple_of(((layer - 2) * 24 + at) * 8, 8), 8)] = value
+
+        sweep_layer(two, src, links, layer, get_half(ahead, layer + 1), get_half(behind, layer), put)
+        return carry
+
+    lax.fori_loop(1, 5, prepare_two, 0)
+    lax.fori_loop(2, 4, third, 0)
     for layer in range(2):
         for time in range(4):
             for color in range(3):
@@ -366,20 +406,15 @@
 def spinors(sources, gauge_links, kept):
     moved = sources[0, :, :, :, :, 0].transpose(0, 2, 3, 1, 4)
     entries = gauge_links[:, 0, :, :, :, 0].transpose(0, 2, 3, 1, 4).reshape(36, 2, SITES)
-    smem = [pl.BlockSpec(memory_space=pltpu.SMEM)]
-    scalar = jax.ShapeDtypeStruct((1,), jnp.int32)
-    place = jnp.stack([lax.axis_index("z_lo"), lax.axis_index(SPACE)]).astype(jnp.int32)
-    packed, side, mine = local_call(
+    packed = local_call(
         pack_kernel,
-        (jax.ShapeDtypeStruct((16, ROWS, SITES), BF16), scalar, scalar),
+        jax.ShapeDtypeStruct((16, ROWS, SITES), BF16),
         [
             pltpu.VMEM((8, ROWS, SITES), F32),
             pltpu.VMEM((LINK, SITES), F32),
         ],
         1 << 17,
-        in_specs=smem + [pl.BlockSpec()] * 2,
-        out_specs=(pl.BlockSpec(), *smem, *smem),
-    )(place, moved, entries)
+    )(moved, entries)
     own = exchange(packed, GROUP)
     vectors = (8, SITES)
     base, links, near, far = local_call(
@@ -392,19 +427,20 @@
         ),
         [pltpu.VMEM((16 * ROWS, SITES), F32)],
         1 << 20,
-        in_specs=smem + [pl.BlockSpec()],
-    )(side, own)
+    )(own)
     matrix, spectrum = kept
-    *kept, tie = local_call(
-        keep_kernel,
+    matrix, spectrum, inner, ahead, behind = local_call(
+        inner_kernel,
         (
             jax.ShapeDtypeStruct(matrix.shape, F32),
             jax.ShapeDtypeStruct(spectrum.shape, BF16),
-            jax.ShapeDtypeStruct((16, SITES), BF16),
+            jax.ShapeDtypeStruct((2, 24, *vectors), F32),
+            jax.ShapeDtypeStruct((4, 12, *vectors), F32),
+            jax.ShapeDtypeStruct((4, 12, *vectors), F32),
         ),
         [],
-        1 << 18,
-    )(far, matrix, spectrum)
+        1 << 22,
+    )(matrix, spectrum, base, links)
     near = send(near, POSITION, (1, 1))
     far = send(far, POSITION, (2, 2))
     done = local_call(
@@ -421,16 +457,15 @@
             pltpu.VMEM((2 * 24 * 8, SITES), F32),
         ],
         1 << 24,
-        in_specs=smem + [pl.BlockSpec()] * 5,
-    )(side, near, far, base, links, tie)
-    return exchange(done, BLOCK), mine, kept
-
-
-def finish_kernel(mine_ref, total_ref, matrix_ref, projected_ref, contracted_ref):
+    )(near, far, base, links, inner, ahead, behind)
+    return exchange(done, BLOCK), matrix, spectrum
+
+
+def finish_kernel(total_ref, matrix_ref, projected_ref, contracted_ref):
     lane = lax.broadcasted_iota(jnp.int32, (8, 128), 1)
     row_re = jnp.broadcast_to(matrix_ref[0:1], (8, 128))
     row_im = jnp.broadcast_to(matrix_ref[1:2], (8, 128))
-    pick = lane == mine_ref[0]
+    pick = lane == lax.axis_index(SPACE)
     own, by_re, by_im = (jnp.zeros((8, 128), F32) for _ in range(3))
     for pair in range(6):
         both = total_ref[pair].astype(F32)
@@ -455,7 +490,7 @@
 def local(sources, gauge_links, eigenvectors, elementals):
     vectors = eigenvectors[0, :, :, :, 0].transpose(2, 1, 0, 3)
     kept = (elementals[0, :, 0], vectors)
-    finals, mine, (matrix, vectors) = spinors(sources, gauge_links, kept)
+    finals, matrix, vectors = spinors(sources, gauge_links, kept)
     partial_value = local_call(
         project_kernel, jax.ShapeDtypeStruct((8, 16, 128), BF16), [], 1 << 25
     )(finals, vectors)
@@ -466,8 +501,7 @@
         (shape, shape),
         [],
         1 << 17,
-        in_specs=[pl.BlockSpec(memory_space=pltpu.SMEM)] + [pl.BlockSpec()] * 2,
-    )(mine, totals, matrix)
+    )(totals, matrix)
     return placed_out(projected), placed_out(contracted)
 
 

time: 91.6 us -> 88.2 us (0.963)
  Pallas kernels: 7.65 us -> 4.76 us
    pallas_call x3, Pallas kernels: 2.45 us -> 1.31 us  [the longest x1 0.72 us: local(): local_call(finish_kernel, (shape, shape), [], 1 << 17)(totals, matrix)]
    pallas_call x1, Pallas kernels: 3.77 us -> 2.66 us  [spinors(): local_call(sweep_kernel, jax.ShapeDtypeStruct((8, FIELD, SITES), BF16), [...]
  transfers between devices with their start and end apart: 2 -> 2, of which waited for: 2 -> 2; matrix products, arithmetic and copies ran while one was open for 0% -> 0% of each run, Pallas kernels for 0% -> 1%
where the time goes in v5:
time: 88.2 us; the launch traced here: 87.8 us
  blocking collectives  62.5 us (71%)
  starting transfers between devices  15.2 us (17%)
  Pallas kernels  4.76 us (5%)
  waiting for transfers between devices  3.04 us (3%)
  local copies, waits for them, and re-layouts  1.63 us (2%)
    all_to_all x5, blocking collectives, exchange(): return lax.all_to_all(value, axes, 0, 0, tiled=True)  62.5 us
    ppermute x2, starting transfers between devices, send(): return lax.ppermute(value, axes, pairs)  15.2 us
    ppermute x2, waiting for transfers between devices, send(): return lax.ppermute(value, axes, pairs)  3.04 us
    pallas_call x1, Pallas kernels, spinors(): local_call(sweep_kernel, jax.ShapeDtypeStruct((8, FIELD, SITES), BF16), [...  2.66 us
  transfers between devices with their start and end apart: 2, of which 2 were waited for; matrix products, arithmetic and copies ran while one was open for 0% of the time, Pallas kernels for 1%

profile of v5, /device:TPU:8, one launch (start us, length us, event | category | flops | bytes accessed | tf_op | source)
XLA Modules:
  0.0 87.8 jit_solution(10926352221633314312)
XLA Ops:
  0.6 0.0 copy-start
  0.6 0.9 copy-done
  1.5 0.0 copy-start.1
  1.5 0.7 copy-done.1
  2.2 0.0 copy-start.3
  2.2 0.0 copy-start.2
  2.2 0.1 shard_map.59
  2.3 16.0 %all_to_all.25.own_ref = bf16[16,120,128]{2,1,0:T(8,128)(2,1)S(1)} all-to-all(bf16[16,120,128]{2,1,0:T(8,128)(2,1)S(1)} %shard_map.59), channel_id=1, replica_groups=mesh['y_hi'=2,'core'=2,'x'=4,'z_hi'=8,'z_lo'=2,'y_lo'=2] {'z_lo','y_lo',..., dimensions={0} | all-to-all | bytes 983040 | tf_op jit(solution)/shard_map/all_to_all | solution.py:27
  18.3 0.5 shard_map.60
  18.8 11.8 %collective-permute-start = (bf16[1056,128]{1,0:T(8,128)(2,1)S(1)}, bf16[1056,128]{1,0:T(8,128)(2,1)S(1)}, u32[]{:S(2)}, u32[]{:S(2)}) collective-permute-start(bf16[1056,128]{1,0:T(8,128)(2,1)S(1)} %get-tuple-element.13), channel_id=1, source_target_pairs={{0,126},{2,4},{4,2},{6,8},{8,6},{10,12},{12,10},{14,16},{16,14},{1... | collective-permute-start | bytes 811016 | tf_op jit(solution)/shard_map/ppermute | solution.py:33
  30.6 3.4 %collective-permute-start.1 = (bf16[96,128]{1,0:T(8,128)(2,1)S(1)}, bf16[96,128]{1,0:T(8,128)(2,1)S(1)}, u32[]{:S(2)}, u32[]{:S(2)}) collective-permute-start(bf16[96,128]{1,0:T(8,128)(2,1)S(1)} %get-tuple-element.14), channel_id=1, source_target_pairs={{0,124},{2,6},{4,0},{6,10},{8,4},{10,14},{12,8},{14,18},{16,12},{1... | collective-permute-start | bytes 73736 | tf_op jit(solution)/shard_map/ppermute | solution.py:33
  34.0 0.0 copy-done.3
  34.0 0.0 copy-done.2
  34.0 0.5 shard_map.61
  34.6 2.7 %collective-permute-done.1.far_ref = bf16[96,128]{1,0:T(8,128)(2,1)S(1)} collective-permute-done((bf16[96,128]{1,0:T(8,128)(2,1)S(1)}, bf16[96,128]{1,0:T(8,128)(2,1)S(1)}, u32[]{:S(2)}, u32[]{:S(2)}) %collective-permute-start.1) | collective-permute-done | bytes 24608 | tf_op jit(solution)/shard_map/ppermute | solution.py:33
  37.2 0.4 collective-permute-done.near_ref
  37.6 2.7 %shard_map.62 = bf16[8,48,128]{2,1,0:T(8,128)(2,1)S(1)} custom-call(bf16[1056,128]{1,0:T(8,128)(2,1)S(1)} %collective-permute-done.near_ref, bf16[96,128]{1,0:T(8,128)(2,1)S(1)} %collective-permute-done.1.far_ref, f32[4,24,8,128]{3,2,1,0:T(8,128)S(1)} %get-tuple-element.15.base_ref, f32[4,72,8,128]{3,2,1,0:T(8,128)S(1)} %get-tuple-element.16.link_ref, ...), custom_call_target="tpu_custom_call" | custom-call | flops 16777216 | bytes 1048576 | tf_op jit(solution)/shard_map/pallas_call | solution.py:446
  40.3 7.8 %all_to_all.26.phi_ref = bf16[8,48,128]{2,1,0:T(8,128)(2,1)S(1)} all-to-all(bf16[8,48,128]{2,1,0:T(8,128)(2,1)S(1)} %shard_map.62), channel_id=1, replica_groups=mesh['y_hi'=2,'core'=2,'x'=4,'z_hi'=8,'z_lo'=2,'y_lo'=2] {'y_lo','y_hi',..., dimensions={0} | all-to-all | bytes 196608 | tf_op jit(solution)/shard_map/all_to_all | solution.py:27
  48.0 0.3 shard_map.63
  48.3 8.8 %all_to_all.27.value_ref = bf16[8,16,128]{2,1,0:T(8,128)(2,1)S(1)} all-to-all(bf16[8,16,128]{2,1,0:T(8,128)(2,1)S(1)} %shard_map.63), channel_id=1, replica_groups=mesh['y_hi'=2,'core'=2,'x'=4,'z_hi'=8,'z_lo'=2,'y_lo'=2] {'x','y_lo'}, dimensions={0} | all-to-all | bytes 65536 | tf_op jit(solution)/shard_map/all_to_all | solution.py:27
  57.1 21.4 %all_to_all.28.value_ref = bf16[16,16,128]{2,1,0:T(8,128)(2,1)S(1)} all-to-all(bf16[16,16,128]{2,1,0:T(8,128)(2,1)S(1)} %shard_map.64), channel_id=1, replica_groups=mesh['y_hi'=2,'core'=2,'x'=4,'z_hi'=8,'z_lo'=2,'y_lo'=2] {'z_hi','z_lo'}, dimensions={0} | all-to-all | bytes 131072 | tf_op jit(solution)/shard_map/all_to_all | solution.py:27
  78.5 8.6 %all_to_all.29.total_ref = bf16[8,16,128]{2,1,0:T(8,128)(2,1)S(1)} all-to-all(bf16[8,16,128]{2,1,0:T(8,128)(2,1)S(1)} %shard_map.65), channel_id=1, replica_groups=mesh['y_hi'=2,'core'=2,'x'=4,'z_hi'=8,'z_lo'=2,'y_lo'=2] {'x','y_lo'}, dimensions={0} | all-to-all | bytes 65536 | tf_op jit(solution)/shard_map/all_to_all | solution.py:27
  87.1 0.7 shard_map.66
  (3 shorter events, 0.1 us)
Async XLA Ops:
  0.6 0.9 %copy-start = (bf16[1,2,4,3,12,1,128]{6,2,5,4,3,1,0:T(4,128)(2,1)S(1)}, bf16[1,2,4,3,12,1,128]{6,2,5,4,3,1,0:T(4,128)(2,1)}, u32[]{:S(2)}) copy-start(bf16[1,2,4,3,12,1,128]{6,2,5,4,3,1,0:T(4,128)(2,1)} %param.4) | copy-start | bytes 221188
  1.5 0.7 copy-start.1
  2.2 31.7 %copy-start.3 = (bf16[1,128,2,3,1,128]{5,2,4,3,1,0:T(2,128)(2,1)S(1)}, bf16[1,128,2,3,1,128]{5,2,4,3,1,0:T(2,128)(2,1)}, u32[]{:S(2)}) copy-start(bf16[1,128,2,3,1,128]{5,2,4,3,1,0:T(2,128)(2,1)} %param.6) | copy-start | bytes 589828
  2.2 31.8 %copy-start.2 = (f32[1,2,1,128]{3,2,1,0:T(1,128)S(1)}, f32[1,2,1,128]{3,2,1,0:T(1,128)}, u32[]{:S(2)}) copy-start(f32[1,2,1,128]{3,2,1,0:T(1,128)} %param.7) | copy-start | bytes 3076
  18.8 18.8 %collective-permute-start = (bf16[1056,128]{1,0:T(8,128)(2,1)S(1)}, bf16[1056,128]{1,0:T(8,128)(2,1)S(1)}, u32[]{:S(2)}, u32[]{:S(2)}) collective-permute-start(bf16[1056,128]{1,0:T(8,128)(2,1)S(1)} %get-tuple-element.13), channel_id=1, source_target_pairs={{0,126},{2,4},{4,2},{6,8},{8,6},{10,12},{12,10},{14,16},{16,14},{1... | collective-permute-start | bytes 811016 | tf_op jit(solution)/shard_map/ppermute | solution.py:33
  30.6 6.6 %collective-permute-start.1 = (bf16[96,128]{1,0:T(8,128)(2,1)S(1)}, bf16[96,128]{1,0:T(8,128)(2,1)S(1)}, u32[]{:S(2)}, u32[]{:S(2)}) collective-permute-start(bf16[96,128]{1,0:T(8,128)(2,1)S(1)} %get-tuple-element.14), channel_id=1, source_target_pairs={{0,124},{2,6},{4,0},{6,10},{8,4},{10,14},{12,8},{14,18},{16,12},{1... | collective-permute-start | bytes 73736 | tf_op jit(solution)/shard_map/ppermute | solution.py:33

commit v6 on v5

--- a/solution.py
+++ b/solution.py
@@ -225,7 +225,7 @@
     return color_apply(link, 2, half_of(field, 2, 1), True)
 
 
-def own_kernel(own_ref, base_ref, link_ref, near_ref, far_ref, wide):
+def own_kernel(own_ref, base_ref, link_ref, near_ref, far_ref, wide, next_ref):
     wide[...] = own_ref[...].reshape(16 * ROWS, SITES).astype(F32)
     side = lax.axis_index("z_lo")
 
@@ -234,7 +234,7 @@
         return carry
 
     lax.fori_loop(0, 4, one, 0)
-    near_ref[: 8 * ROWS] = own_ref[pl.ds(side * 8, 8)].reshape(8 * ROWS, SITES)
+    near_ref[: 4 * ROWS] = own_ref[pl.ds(side * 12, 4)].reshape(4 * ROWS, SITES)
 
     def put(ref, start, below, above):
         for color in range(3):
@@ -250,8 +250,19 @@
     def half_up(layer):
         return sent_up(field_at(base_ref, layer), link_at(link_ref, layer))
 
-    put(near_ref, 8 * ROWS, half_down(2), half_up(1))
     put(far_ref, 0, half_down(0), half_up(3))
+    put(near_ref, 4 * ROWS, half_down(1), half_up(2))
+    second = 1 + side
+
+    def keep(at, value):
+        next_ref[at] = value
+
+    sweep_layer(base_ref, base_ref, link_ref, second, half_down(second + 1), half_up(second - 1), keep)
+
+    def field(part, color, spin):
+        return next_ref[comp(part, color, spin)]
+
+    put(near_ref, 4 * ROWS + 96, sent_down(field), sent_up(field, link_at(link_ref, second)))
 
 
 def sweep_layer(from_ref, src_ref, link_ref, layer, ahead, behind, put):
@@ -295,26 +306,22 @@
     wide, src, one, two, links, ahead, behind, done,
 ):
     side = lax.axis_index("z_lo")
-    block, halo = 2 - 2 * side, 4 * side
-    wide[...] = near_ref[: 8 * ROWS].astype(F32)
+    block, halo = 2 - 2 * side, 1 + 3 * side
+    wide[...] = near_ref[: 4 * ROWS].astype(F32)
     src[pl.ds(block, 4)] = base_ref[...]
     links[pl.ds(block, 4)] = link_ref[...]
     one[pl.ds(block + 1, 2)] = inner_ref[...]
     ahead[pl.ds(block, 4)] = ahead_ref[...]
     behind[pl.ds(block + 1, 4)] = behind_ref[...]
-    near = near_ref[8 * ROWS :].astype(F32).reshape(12, 8, SITES)
+    near = near_ref[4 * ROWS : 4 * ROWS + 96].astype(F32).reshape(12, 8, SITES)
     far = far_ref[...].astype(F32).reshape(12, 8, SITES)
-    ahead[6] = jnp.where(side == 0, far, near)
-    behind[0] = jnp.where(side == 0, near, far)
-
-    def gather(at, carry):
-        layer = halo + at
-        assemble(wide, at * 4 * ROWS, src, links, layer)
-        prepare_layer(src, links, layer, ahead, layer, behind, layer + 1)
-        return carry
+    ahead[6 - side] = jnp.where(side == 0, far, near)
+    behind[1 - side] = jnp.where(side == 0, near, far)
+    assemble(wide, 0, src, links, halo)
+    prepare_layer(src, links, halo, ahead, halo, behind, halo + 1)
 
     def first(at, carry):
-        layer = at + jnp.where(at >= 3 - 2 * side, 2, 0)
+        layer = at + 1 - side + jnp.where(at >= 2 - side, 2, 0)
 
         def put(slot_at, value):
             one[layer, slot_at] = value
@@ -323,11 +330,14 @@
         sweep_layer(src, src, links, layer, *halves, put)
         return carry
 
-    lax.fori_loop(0, 2, gather, 0)
-    lax.fori_loop(0, 4, first, 0)
+    lax.fori_loop(0, 3, first, 0)
+
+    def prepare(from_ref, layer):
+        put_half(ahead.at[layer + 2], sent_down(field_at(from_ref, layer + 2)))
+        put_half(behind.at[layer + 1], sent_up(field_at(from_ref, layer), link_at(links, layer)))
 
     def prepare_one(layer, carry):
-        prepare_layer(one, links, layer, ahead, layer, behind, layer + 1)
+        prepare(one, layer)
         return carry
 
     def second(layer, carry):
@@ -337,11 +347,21 @@
         sweep_layer(one, src, links, layer, get_half(ahead, layer + 1), get_half(behind, layer), put)
         return carry
 
-    lax.fori_loop(0, 6, prepare_one, 0)
+    lax.fori_loop(0, 4, prepare_one, 0)
+    near = near_ref[4 * ROWS + 96 :].astype(F32).reshape(12, 8, SITES)
+
+    @pl.when(side == 0)
+    def _():
+        behind[1] = near
+
+    @pl.when(side == 1)
+    def _():
+        ahead[5] = near
+
     lax.fori_loop(1, 5, second, 0)
 
     def prepare_two(layer, carry):
-        prepare_layer(two, links, layer, ahead, layer, behind, layer + 1)
+        prepare(two, layer)
         return carry
 
     def third(layer, carry):
@@ -351,7 +371,7 @@
         sweep_layer(two, src, links, layer, get_half(ahead, layer + 1), get_half(behind, layer), put)
         return carry
 
-    lax.fori_loop(1, 5, prepare_two, 0)
+    lax.fori_loop(1, 3, prepare_two, 0)
     lax.fori_loop(2, 4, third, 0)
     for layer in range(2):
         for time in range(4):
@@ -422,10 +442,10 @@
         (
             jax.ShapeDtypeStruct((4, 24, *vectors), F32),
             jax.ShapeDtypeStruct((4, LINK, *vectors), F32),
-            jax.ShapeDtypeStruct((8 * ROWS + 96, SITES), BF16),
+            jax.ShapeDtypeStruct((4 * ROWS + 192, SITES), BF16),
             jax.ShapeDtypeStruct((96, SITES), BF16),
         ),
-        [pltpu.VMEM((16 * ROWS, SITES), F32)],
+        [pltpu.VMEM((16 * ROWS, SITES), F32), pltpu.VMEM((24, *vectors), F32)],
         1 << 20,
     )(own)
     matrix, spectrum = kept
@@ -447,7 +467,7 @@
         sweep_kernel,
         jax.ShapeDtypeStruct((8, FIELD, SITES), BF16),
         [
-            pltpu.VMEM((8 * ROWS, SITES), F32),
+            pltpu.VMEM((4 * ROWS, SITES), F32),
             pltpu.VMEM((6, 24, *vectors), F32),
             pltpu.VMEM((6, 24, *vectors), F32),
             pltpu.VMEM((6, 24, *vectors), F32),

time: 88.2 us -> 86.4 us (0.980)
  blocking collectives: 62.5 us -> 61.2 us
    all_to_all x5, blocking collectives: 62.5 us -> 61.2 us  [exchange(): return lax.all_to_all(value, axes, 0, 0, tiled=True)]
  transfers between devices with their start and end apart: 2 -> 2, of which waited for: 2 -> 1; matrix products, arithmetic and copies ran while one was open for 0% -> 0% of each run, Pallas kernels for 1% -> 1%
where the time goes in v6:
time: 86.4 us; the launch traced here: 85.9 us
  blocking collectives  61.2 us (71%)
  starting transfers between devices  15.2 us (18%)
  Pallas kernels  4.57 us (5%)
  waiting for transfers between devices  2.65 us (3%)
  local copies, waits for them, and re-layouts  1.63 us (2%)
    all_to_all x5, blocking collectives, exchange(): return lax.all_to_all(value, axes, 0, 0, tiled=True)  61.2 us
    ppermute x2, starting transfers between devices, send(): return lax.ppermute(value, axes, pairs)  15.2 us
    ppermute x2, waiting for transfers between devices, send(): return lax.ppermute(value, axes, pairs)  2.65 us
    pallas_call x1, Pallas kernels, spinors(): local_call(sweep_kernel, jax.ShapeDtypeStruct((8, FIELD, SITES), BF16), [...  2.24 us
  transfers between devices with their start and end apart: 2, of which 1 were waited for; matrix products, arithmetic and copies ran while one was open for 0% of the time, Pallas kernels for 1%

profile of v6, /device:TPU:8, one launch (start us, length us, event | category | flops | bytes accessed | tf_op | source)
XLA Modules:
  0.0 85.9 jit_solution(11269171411718693926)
XLA Ops:
  0.6 0.0 copy-start
  0.6 0.9 %copy-done = bf16[1,2,4,3,12,1,128]{6,2,5,4,3,1,0:T(4,128)(2,1)S(1)} copy-done((bf16[1,2,4,3,12,1,128]{6,2,5,4,3,1,0:T(4,128)(2,1)S(1)}, bf16[1,2,4,3,12,1,128]{6,2,5,4,3,1,0:T(4,128)(2,1)}, u32[]{:S(2)}) %copy-start) | copy-done | bytes 73752
  1.5 0.0 copy-start.1
  1.5 0.7 copy-done.1
  2.2 0.0 copy-start.3
  2.2 0.0 copy-start.2
  2.2 0.1 shard_map.59
  2.3 16.0 %all_to_all.25.own_ref = bf16[16,120,128]{2,1,0:T(8,128)(2,1)S(1)} all-to-all(bf16[16,120,128]{2,1,0:T(8,128)(2,1)S(1)} %shard_map.59), channel_id=1, replica_groups=mesh['y_hi'=2,'core'=2,'x'=4,'z_hi'=8,'z_lo'=2,'y_lo'=2] {'z_lo','y_lo',..., dimensions={0} | all-to-all | bytes 983040 | tf_op jit(solution)/shard_map/all_to_all | solution.py:27
  18.3 0.7 shard_map.60
  19.0 11.8 %collective-permute-start = (bf16[672,128]{1,0:T(8,128)(2,1)S(1)}, bf16[672,128]{1,0:T(8,128)(2,1)S(1)}, u32[]{:S(2)}, u32[]{:S(2)}) collective-permute-start(bf16[672,128]{1,0:T(8,128)(2,1)S(1)} %get-tuple-element.13), channel_id=1, source_target_pairs={{0,126},{2,4},{4,2},{6,8},{8,6},{10,12},{12,10},{14,16},{16,14},{1... | collective-permute-start | bytes 516104 | tf_op jit(solution)/shard_map/ppermute | solution.py:33
  30.8 3.4 %collective-permute-start.1 = (bf16[96,128]{1,0:T(8,128)(2,1)S(1)}, bf16[96,128]{1,0:T(8,128)(2,1)S(1)}, u32[]{:S(2)}, u32[]{:S(2)}) collective-permute-start(bf16[96,128]{1,0:T(8,128)(2,1)S(1)} %get-tuple-element.14), channel_id=1, source_target_pairs={{0,124},{2,6},{4,0},{6,10},{8,4},{10,14},{12,8},{14,18},{16,12},{1... | collective-permute-start | bytes 73736 | tf_op jit(solution)/shard_map/ppermute | solution.py:33
  34.2 0.0 copy-done.3
  34.3 0.0 copy-done.2
  34.3 0.5 shard_map.61
  34.8 2.7 %collective-permute-done.1.far_ref = bf16[96,128]{1,0:T(8,128)(2,1)S(1)} collective-permute-done((bf16[96,128]{1,0:T(8,128)(2,1)S(1)}, bf16[96,128]{1,0:T(8,128)(2,1)S(1)}, u32[]{:S(2)}, u32[]{:S(2)}) %collective-permute-start.1) | collective-permute-done | bytes 24608 | tf_op jit(solution)/shard_map/ppermute | solution.py:33
  37.5 0.0 collective-permute-done.near_ref
  37.5 2.2 %shard_map.62 = bf16[8,48,128]{2,1,0:T(8,128)(2,1)S(1)} custom-call(bf16[672,128]{1,0:T(8,128)(2,1)S(1)} %collective-permute-done.near_ref, bf16[96,128]{1,0:T(8,128)(2,1)S(1)} %collective-permute-done.1.far_ref, f32[4,24,8,128]{3,2,1,0:T(8,128)S(1)} %get-tuple-element.15.base_ref, f32[4,72,8,128]{3,2,1,0:T(8,128)S(1)} %get-tuple-element.16.link_ref, ...), custom_call_target="tpu_custom_call" | custom-call | flops 16777216 | bytes 1048576 | tf_op jit(solution)/shard_map/pallas_call | solution.py:466
  39.7 8.0 %all_to_all.26.phi_ref = bf16[8,48,128]{2,1,0:T(8,128)(2,1)S(1)} all-to-all(bf16[8,48,128]{2,1,0:T(8,128)(2,1)S(1)} %shard_map.62), channel_id=1, replica_groups=mesh['y_hi'=2,'core'=2,'x'=4,'z_hi'=8,'z_lo'=2,'y_lo'=2] {'y_lo','y_hi',..., dimensions={0} | all-to-all | bytes 196608 | tf_op jit(solution)/shard_map/all_to_all | solution.py:27
  47.7 0.3 shard_map.63
  47.9 8.8 %all_to_all.27.value_ref = bf16[8,16,128]{2,1,0:T(8,128)(2,1)S(1)} all-to-all(bf16[8,16,128]{2,1,0:T(8,128)(2,1)S(1)} %shard_map.63), channel_id=1, replica_groups=mesh['y_hi'=2,'core'=2,'x'=4,'z_hi'=8,'z_lo'=2,'y_lo'=2] {'x','y_lo'}, dimensions={0} | all-to-all | bytes 65536 | tf_op jit(solution)/shard_map/all_to_all | solution.py:27
  56.7 19.9 %all_to_all.28.value_ref = bf16[16,16,128]{2,1,0:T(8,128)(2,1)S(1)} all-to-all(bf16[16,16,128]{2,1,0:T(8,128)(2,1)S(1)} %shard_map.64), channel_id=1, replica_groups=mesh['y_hi'=2,'core'=2,'x'=4,'z_hi'=8,'z_lo'=2,'y_lo'=2] {'z_hi','z_lo'}, dimensions={0} | all-to-all | bytes 131072 | tf_op jit(solution)/shard_map/all_to_all | solution.py:27
  76.6 8.6 %all_to_all.29.total_ref = bf16[8,16,128]{2,1,0:T(8,128)(2,1)S(1)} all-to-all(bf16[8,16,128]{2,1,0:T(8,128)(2,1)S(1)} %shard_map.65), channel_id=1, replica_groups=mesh['y_hi'=2,'core'=2,'x'=4,'z_hi'=8,'z_lo'=2,'y_lo'=2] {'x','y_lo'}, dimensions={0} | all-to-all | bytes 65536 | tf_op jit(solution)/shard_map/all_to_all | solution.py:27
  85.2 0.7 shard_map.66
  (3 shorter events, 0.1 us)
Async XLA Ops:
  0.6 0.9 %copy-start = (bf16[1,2,4,3,12,1,128]{6,2,5,4,3,1,0:T(4,128)(2,1)S(1)}, bf16[1,2,4,3,12,1,128]{6,2,5,4,3,1,0:T(4,128)(2,1)}, u32[]{:S(2)}) copy-start(bf16[1,2,4,3,12,1,128]{6,2,5,4,3,1,0:T(4,128)(2,1)} %param.4) | copy-start | bytes 221188
  1.5 0.7 copy-start.1
  2.2 32.0 %copy-start.3 = (bf16[1,128,2,3,1,128]{5,2,4,3,1,0:T(2,128)(2,1)S(1)}, bf16[1,128,2,3,1,128]{5,2,4,3,1,0:T(2,128)(2,1)}, u32[]{:S(2)}) copy-start(bf16[1,128,2,3,1,128]{5,2,4,3,1,0:T(2,128)(2,1)} %param.6) | copy-start | bytes 589828
  2.2 32.0 %copy-start.2 = (f32[1,2,1,128]{3,2,1,0:T(1,128)S(1)}, f32[1,2,1,128]{3,2,1,0:T(1,128)}, u32[]{:S(2)}) copy-start(f32[1,2,1,128]{3,2,1,0:T(1,128)} %param.7) | copy-start | bytes 3076
  19.0 18.4 %collective-permute-start = (bf16[672,128]{1,0:T(8,128)(2,1)S(1)}, bf16[672,128]{1,0:T(8,128)(2,1)S(1)}, u32[]{:S(2)}, u32[]{:S(2)}) collective-permute-start(bf16[672,128]{1,0:T(8,128)(2,1)S(1)} %get-tuple-element.13), channel_id=1, source_target_pairs={{0,126},{2,4},{4,2},{6,8},{8,6},{10,12},{12,10},{14,16},{16,14},{1... | collective-permute-start | bytes 516104 | tf_op jit(solution)/shard_map/ppermute | solution.py:33
  30.8 6.6 %collective-permute-start.1 = (bf16[96,128]{1,0:T(8,128)(2,1)S(1)}, bf16[96,128]{1,0:T(8,128)(2,1)S(1)}, u32[]{:S(2)}, u32[]{:S(2)}) collective-permute-start(bf16[96,128]{1,0:T(8,128)(2,1)S(1)} %get-tuple-element.14), channel_id=1, source_target_pairs={{0,124},{2,6},{4,0},{6,10},{8,4},{10,14},{12,8},{14,18},{16,12},{1... | collective-permute-start | bytes 73736 | tf_op jit(solution)/shard_map/ppermute | solution.py:33

commit v7 on v6

--- a/solution.py
+++ b/solution.py
@@ -44,7 +44,11 @@
     )
 
 
-def pack_kernel(source_ref, link_ref, out_ref, rows, links):
+def clear_kernel(out_ref):
+    out_ref[...] = jnp.zeros(out_ref.shape, F32)
+
+
+def pack_kernel(clear_ref, source_ref, link_ref, out_ref, rows, links):
     for entry in range(36):
         links[2 * entry : 2 * entry + 2] = link_ref[entry].astype(F32)
     shared = links[...]
@@ -58,7 +62,7 @@
                     if target < 6:
                         piece = source_ref[part, color, 2 * target + which].astype(F32)
                     else:
-                        piece = jnp.zeros((4, SITES), F32)
+                        piece = clear_ref[:4]
                     rows[target, at : at + 4] = piece
     packed = rows[...].astype(BF16)
     out_ref[:8] = packed
@@ -398,7 +402,10 @@
     crossed = pltpu.roll(totals[1].reshape(16, 8, 128), 4, 1)
     upper = lax.broadcasted_iota(jnp.int32, crossed.shape, 1) < 4
     mixed = totals[0].reshape(16, 8, 128) + jnp.where(upper, crossed, -crossed)
-    out_ref[...] = mixed.reshape(8, 16, 128).astype(BF16)
+    for source in range(12):
+        for part in range(2):
+            member, at = divmod(2 * source + part, 3)
+            out_ref[member, at] = mixed[source, 4 * part : 4 * part + 4].astype(BF16)
 
 
 def spread_kernel(value_ref, out_ref):
@@ -426,6 +433,7 @@
 def spinors(sources, gauge_links, kept):
     moved = sources[0, :, :, :, :, 0].transpose(0, 2, 3, 1, 4)
     entries = gauge_links[:, 0, :, :, :, 0].transpose(0, 2, 3, 1, 4).reshape(36, 2, SITES)
+    clear = local_call(clear_kernel, jax.ShapeDtypeStruct((8, SITES), F32), [], 1 << 32)()
     packed = local_call(
         pack_kernel,
         jax.ShapeDtypeStruct((16, ROWS, SITES), BF16),
@@ -434,7 +442,7 @@
             pltpu.VMEM((LINK, SITES), F32),
         ],
         1 << 17,
-    )(moved, entries)
+    )(clear, moved, entries)
     own = exchange(packed, GROUP)
     vectors = (8, SITES)
     base, links, near, far = local_call(
@@ -481,20 +489,20 @@
     return exchange(done, BLOCK), matrix, spectrum
 
 
-def finish_kernel(total_ref, matrix_ref, projected_ref, contracted_ref):
+def finish_kernel(total_ref, matrix_ref, projected_ref, contracted_ref, rows):
+    for piece in range(24):
+        rows[4 * piece : 4 * piece + 4] = total_ref[piece // 3, piece % 3].astype(F32)
     lane = lax.broadcasted_iota(jnp.int32, (8, 128), 1)
     row_re = jnp.broadcast_to(matrix_ref[0:1], (8, 128))
     row_im = jnp.broadcast_to(matrix_ref[1:2], (8, 128))
     pick = lane == lax.axis_index(SPACE)
     own, by_re, by_im = (jnp.zeros((8, 128), F32) for _ in range(3))
-    for pair in range(6):
-        both = total_ref[pair].astype(F32)
-        for which in range(2):
-            value = both[8 * which : 8 * which + 8]
-            here = lane == 2 * pair + which
-            own = jnp.where(here, jnp.sum(jnp.where(pick, value, 0.0), 1, keepdims=True), own)
-            by_re = jnp.where(here, jnp.sum(value * row_re, 1, keepdims=True), by_re)
-            by_im = jnp.where(here, jnp.sum(value * row_im, 1, keepdims=True), by_im)
+    for source in range(12):
+        value = rows[8 * source : 8 * source + 8]
+        here = lane == source
+        own = jnp.where(here, jnp.sum(jnp.where(pick, value, 0.0), 1, keepdims=True), own)
+        by_re = jnp.where(here, jnp.sum(value * row_re, 1, keepdims=True), by_re)
+        by_im = jnp.where(here, jnp.sum(value * row_im, 1, keepdims=True), by_im)
     crossed = pltpu.roll(by_im, 4, 0)
     upper = lax.broadcasted_iota(jnp.int32, (8, 128), 0) < 4
     contracted = by_re + jnp.where(upper, -crossed, crossed)
@@ -512,14 +520,14 @@
     kept = (elementals[0, :, 0], vectors)
     finals, matrix, vectors = spinors(sources, gauge_links, kept)
     partial_value = local_call(
-        project_kernel, jax.ShapeDtypeStruct((8, 16, 128), BF16), [], 1 << 25
+        project_kernel, jax.ShapeDtypeStruct((8, 3, 4, 128), BF16), [], 1 << 25
     )(finals, vectors)
     totals = all_reduce(partial_value)
     shape = jax.ShapeDtypeStruct((8, 1, 12), F32)
     projected, contracted = local_call(
         finish_kernel,
         (shape, shape),
-        [],
+        [pltpu.VMEM((96, 128), F32)],
         1 << 17,
     )(totals, matrix)
     return placed_out(projected), placed_out(contracted)

time: 86.4 us -> 85.2 us (0.986)
  no operation moved by 1% of the time
where the time goes in v7:
time: 85.2 us; the launch traced here: 84.9 us
  blocking collectives  60.8 us (71%)
  starting transfers between devices  15.2 us (18%)
  Pallas kernels  4.58 us (5%)
  waiting for transfers between devices  2.65 us (3%)
  local copies, waits for them, and re-layouts  0.9 us (1%)
    all_to_all x5, blocking collectives, exchange(): return lax.all_to_all(value, axes, 0, 0, tiled=True)  60.8 us
    ppermute x2, starting transfers between devices, send(): return lax.ppermute(value, axes, pairs)  15.2 us
    ppermute x2, waiting for transfers between devices, send(): return lax.ppermute(value, axes, pairs)  2.65 us
    pallas_call x1, Pallas kernels, spinors(): local_call(sweep_kernel, jax.ShapeDtypeStruct((8, FIELD, SITES), BF16), [...  2.24 us
  transfers between devices with their start and end apart: 2, of which 1 were waited for; matrix products, arithmetic and copies ran while one was open for 0% of the time, Pallas kernels for 1%

profile of v7, /device:TPU:8, one launch (start us, length us, event | category | flops | bytes accessed | tf_op | source)
XLA Modules:
  0.0 84.9 jit_solution(8409703044245624498)
XLA Ops:
  0.6 0.0 copy-start.1
  0.6 0.0 copy-start
  0.7 0.0 copy-start.3
  0.7 0.7 copy-done.1
  1.4 0.2 copy-done
  1.5 0.0 copy-start.2
  1.5 0.1 shard_map.60
  1.6 15.9 %all_to_all.25.own_ref = bf16[16,120,128]{2,1,0:T(8,128)(2,1)S(1)} all-to-all(bf16[16,120,128]{2,1,0:T(8,128)(2,1)S(1)} %shard_map.60), channel_id=1, replica_groups=mesh['y_hi'=2,'core'=2,'x'=4,'z_hi'=8,'z_lo'=2,'y_lo'=2] {'z_lo','y_lo',..., dimensions={0} | all-to-all | bytes 983040 | tf_op jit(solution)/shard_map/all_to_all | solution.py:27
  17.5 0.7 shard_map.61
  18.2 11.8 %collective-permute-start = (bf16[672,128]{1,0:T(8,128)(2,1)S(1)}, bf16[672,128]{1,0:T(8,128)(2,1)S(1)}, u32[]{:S(2)}, u32[]{:S(2)}) collective-permute-start(bf16[672,128]{1,0:T(8,128)(2,1)S(1)} %get-tuple-element.13), channel_id=1, source_target_pairs={{0,126},{2,4},{4,2},{6,8},{8,6},{10,12},{12,10},{14,16},{16,14},{1... | collective-permute-start | bytes 516104 | tf_op jit(solution)/shard_map/ppermute | solution.py:33
  30.0 3.4 %collective-permute-start.1 = (bf16[96,128]{1,0:T(8,128)(2,1)S(1)}, bf16[96,128]{1,0:T(8,128)(2,1)S(1)}, u32[]{:S(2)}, u32[]{:S(2)}) collective-permute-start(bf16[96,128]{1,0:T(8,128)(2,1)S(1)} %get-tuple-element.14), channel_id=1, source_target_pairs={{0,124},{2,6},{4,0},{6,10},{8,4},{10,14},{12,8},{14,18},{16,12},{1... | collective-permute-start | bytes 73736 | tf_op jit(solution)/shard_map/ppermute | solution.py:33
  33.4 0.0 copy-done.3
  33.4 0.0 copy-done.2
  33.4 0.5 shard_map.62
  34.0 2.7 %collective-permute-done.1.far_ref = bf16[96,128]{1,0:T(8,128)(2,1)S(1)} collective-permute-done((bf16[96,128]{1,0:T(8,128)(2,1)S(1)}, bf16[96,128]{1,0:T(8,128)(2,1)S(1)}, u32[]{:S(2)}, u32[]{:S(2)}) %collective-permute-start.1) | collective-permute-done | bytes 24608 | tf_op jit(solution)/shard_map/ppermute | solution.py:33
  36.6 0.0 collective-permute-done.near_ref
  36.6 2.2 %shard_map.63 = bf16[8,48,128]{2,1,0:T(8,128)(2,1)S(1)} custom-call(bf16[672,128]{1,0:T(8,128)(2,1)S(1)} %collective-permute-done.near_ref, bf16[96,128]{1,0:T(8,128)(2,1)S(1)} %collective-permute-done.1.far_ref, f32[4,24,8,128]{3,2,1,0:T(8,128)S(1)} %get-tuple-element.15.base_ref, f32[4,72,8,128]{3,2,1,0:T(8,128)S(1)} %get-tuple-element.16.link_ref, ...), custom_call_target="tpu_custom_call" | custom-call | flops 16777216 | bytes 1048576 | tf_op jit(solution)/shard_map/pallas_call | solution.py:474
  38.9 8.0 %all_to_all.26.phi_ref = bf16[8,48,128]{2,1,0:T(8,128)(2,1)S(1)} all-to-all(bf16[8,48,128]{2,1,0:T(8,128)(2,1)S(1)} %shard_map.63), channel_id=1, replica_groups=mesh['y_hi'=2,'core'=2,'x'=4,'z_hi'=8,'z_lo'=2,'y_lo'=2] {'y_lo','y_hi',..., dimensions={0} | all-to-all | bytes 196608 | tf_op jit(solution)/shard_map/all_to_all | solution.py:27
  46.8 0.3 shard_map.64
  47.1 8.7 %all_to_all.27.value_ref = bf16[8,3,4,128]{3,2,1,0:T(4,128)(2,1)S(1)} all-to-all(bf16[8,3,4,128]{3,2,1,0:T(4,128)(2,1)S(1)} %shard_map.64), channel_id=1, replica_groups=mesh['y_hi'=2,'core'=2,'x'=4,'z_hi'=8,'z_lo'=2,'y_lo'=2] {'x','y_lo'}, dimensions={0} | all-to-all | bytes 49152 | tf_op jit(solution)/shard_map/all_to_all | solution.py:27
  55.8 19.7 %all_to_all.28.value_ref = bf16[16,3,4,128]{3,2,1,0:T(4,128)(2,1)S(1)} all-to-all(bf16[16,3,4,128]{3,2,1,0:T(4,128)(2,1)S(1)} %shard_map.65), channel_id=1, replica_groups=mesh['y_hi'=2,'core'=2,'x'=4,'z_hi'=8,'z_lo'=2,'y_lo'=2] {'z_hi','z_lo'}, dimensions={0} | all-to-all | bytes 98304 | tf_op jit(solution)/shard_map/all_to_all | solution.py:27
  75.6 8.6 %all_to_all.29.total_ref = bf16[8,3,4,128]{3,2,1,0:T(4,128)(2,1)S(1)} all-to-all(bf16[8,3,4,128]{3,2,1,0:T(4,128)(2,1)S(1)} %shard_map.66), channel_id=1, replica_groups=mesh['y_hi'=2,'core'=2,'x'=4,'z_hi'=8,'z_lo'=2,'y_lo'=2] {'x','y_lo'}, dimensions={0} | all-to-all | bytes 49152 | tf_op jit(solution)/shard_map/all_to_all | solution.py:27
  84.2 0.7 shard_map.67
  (4 shorter events, 0.1 us)
Async XLA Ops:
  0.6 0.7 copy-start.1
  0.6 0.9 %copy-start = (bf16[1,2,4,3,12,1,128]{6,2,5,4,3,1,0:T(4,128)(2,1)S(1)}, bf16[1,2,4,3,12,1,128]{6,2,5,4,3,1,0:T(4,128)(2,1)}, u32[]{:S(2)}) copy-start(bf16[1,2,4,3,12,1,128]{6,2,5,4,3,1,0:T(4,128)(2,1)} %param.4) | copy-start | bytes 221188
  0.7 32.7 %copy-start.3 = (bf16[1,128,2,3,1,128]{5,2,4,3,1,0:T(2,128)(2,1)S(1)}, bf16[1,128,2,3,1,128]{5,2,4,3,1,0:T(2,128)(2,1)}, u32[]{:S(2)}) copy-start(bf16[1,128,2,3,1,128]{5,2,4,3,1,0:T(2,128)(2,1)} %param.6) | copy-start | bytes 589828
  1.5 31.9 %copy-start.2 = (f32[1,2,1,128]{3,2,1,0:T(1,128)S(1)}, f32[1,2,1,128]{3,2,1,0:T(1,128)}, u32[]{:S(2)}) copy-start(f32[1,2,1,128]{3,2,1,0:T(1,128)} %param.7) | copy-start | bytes 3076
  18.2 18.4 %collective-permute-start = (bf16[672,128]{1,0:T(8,128)(2,1)S(1)}, bf16[672,128]{1,0:T(8,128)(2,1)S(1)}, u32[]{:S(2)}, u32[]{:S(2)}) collective-permute-start(bf16[672,128]{1,0:T(8,128)(2,1)S(1)} %get-tuple-element.13), channel_id=1, source_target_pairs={{0,126},{2,4},{4,2},{6,8},{8,6},{10,12},{12,10},{14,16},{16,14},{1... | collective-permute-start | bytes 516104 | tf_op jit(solution)/shard_map/ppermute | solution.py:33
  30.0 6.6 %collective-permute-start.1 = (bf16[96,128]{1,0:T(8,128)(2,1)S(1)}, bf16[96,128]{1,0:T(8,128)(2,1)S(1)}, u32[]{:S(2)}, u32[]{:S(2)}) collective-permute-start(bf16[96,128]{1,0:T(8,128)(2,1)S(1)} %get-tuple-element.14), channel_id=1, source_target_pairs={{0,124},{2,6},{4,0},{6,10},{8,4},{10,14},{12,8},{14,18},{16,12},{1... | collective-permute-start | bytes 73736 | tf_op jit(solution)/shard_map/ppermute | solution.py:33

commit v8 on v7

--- a/solution.py
+++ b/solution.py
@@ -27,9 +27,9 @@
     return lax.all_to_all(value, axes, 0, 0, tiled=True)
 
 
-def send(value, axes, steps):
+def send(value, axes):
     count = lax.axis_size(axes)
-    pairs = [(i, (i + steps[1] if i % 2 else i - steps[0]) % count) for i in range(count)]
+    pairs = [(i, (i + 1 if i % 2 else i - 1) % count) for i in range(count)]
     return lax.ppermute(value, axes, pairs)
 
 
@@ -229,7 +229,7 @@
     return color_apply(link, 2, half_of(field, 2, 1), True)
 
 
-def own_kernel(own_ref, base_ref, link_ref, near_ref, far_ref, wide, next_ref):
+def own_kernel(own_ref, base_ref, link_ref, near_ref, wide, next_ref):
     wide[...] = own_ref[...].reshape(16 * ROWS, SITES).astype(F32)
     side = lax.axis_index("z_lo")
 
@@ -254,7 +254,6 @@
     def half_up(layer):
         return sent_up(field_at(base_ref, layer), link_at(link_ref, layer))
 
-    put(far_ref, 0, half_down(0), half_up(3))
     put(near_ref, 4 * ROWS, half_down(1), half_up(2))
     second = 1 + side
 
@@ -306,7 +305,7 @@
 
 
 def sweep_kernel(
-    near_ref, far_ref, base_ref, link_ref, inner_ref, ahead_ref, behind_ref, out_ref,
+    near_ref, base_ref, link_ref, inner_ref, ahead_ref, behind_ref, out_ref,
     wide, src, one, two, links, ahead, behind, done,
 ):
     side = lax.axis_index("z_lo")
@@ -318,14 +317,22 @@
     ahead[pl.ds(block, 4)] = ahead_ref[...]
     behind[pl.ds(block + 1, 4)] = behind_ref[...]
     near = near_ref[4 * ROWS : 4 * ROWS + 96].astype(F32).reshape(12, 8, SITES)
-    far = far_ref[...].astype(F32).reshape(12, 8, SITES)
-    ahead[6 - side] = jnp.where(side == 0, far, near)
-    behind[1 - side] = jnp.where(side == 0, near, far)
+
+    def place_near(value):
+        @pl.when(side == 0)
+        def _():
+            behind[1] = value
+
+        @pl.when(side == 1)
+        def _():
+            ahead[5] = value
+
+    place_near(near)
     assemble(wide, 0, src, links, halo)
     prepare_layer(src, links, halo, ahead, halo, behind, halo + 1)
 
     def first(at, carry):
-        layer = at + 1 - side + jnp.where(at >= 2 - side, 2, 0)
+        layer = at + 1 + 2 * side
 
         def put(slot_at, value):
             one[layer, slot_at] = value
@@ -334,50 +341,63 @@
         sweep_layer(src, src, links, layer, *halves, put)
         return carry
 
-    lax.fori_loop(0, 3, first, 0)
-
-    def prepare(from_ref, layer):
-        put_half(ahead.at[layer + 2], sent_down(field_at(from_ref, layer + 2)))
-        put_half(behind.at[layer + 1], sent_up(field_at(from_ref, layer), link_at(links, layer)))
+    lax.fori_loop(0, 2, first, 0)
 
     def prepare_one(layer, carry):
-        prepare(one, layer)
-        return carry
-
-    def second(layer, carry):
-        def put(at, value):
-            two[layer, at] = value
+        put_half(ahead.at[layer + 1], sent_down(field_at(one, layer + 1)))
+        put_half(behind.at[layer + 1], sent_up(field_at(one, layer), link_at(links, layer)))
+        return carry
+
+    def second(at, carry):
+        layer = at + 1 + side
+
+        def put(slot_at, value):
+            two[layer, slot_at] = value
 
         sweep_layer(one, src, links, layer, get_half(ahead, layer + 1), get_half(behind, layer), put)
         return carry
 
-    lax.fori_loop(0, 4, prepare_one, 0)
-    near = near_ref[4 * ROWS + 96 :].astype(F32).reshape(12, 8, SITES)
+    lax.fori_loop(1, 4, prepare_one, 0)
+    place_near(near_ref[4 * ROWS + 96 :].astype(F32).reshape(12, 8, SITES))
+    lax.fori_loop(0, 3, second, 0)
+    put_half(ahead.at[3], sent_down(field_at(two, 3)))
+    put_half(behind.at[3], sent_up(field_at(two, 2), link_at(links, 2)))
+    nothing = jnp.zeros((12, 8, SITES), F32)
+
+    def put_done(at, slot_at, value):
+        done[pl.ds(pl.multiple_of((at * 24 + slot_at) * 8, 8), 8)] = value
+
+    def put_cross(down, up):
+        total = {}
+        accumulate(total, 2, down, up)
+        for key, value in total.items():
+            put_done(2 - side, comp(*key), HOPPING * value)
+
+    none = [[(nothing[0], nothing[0])] * 2] * 3
 
     @pl.when(side == 0)
     def _():
-        behind[1] = near
+        put_half(behind.at[2], sent_up(field_at(two, 1), link_at(links, 1)))
+        ahead[4] = nothing
+        put_cross(none, sent_up(field_at(two, 3), link_at(links, 3)))
 
     @pl.when(side == 1)
     def _():
-        ahead[5] = near
-
-    lax.fori_loop(1, 5, second, 0)
-
-    def prepare_two(layer, carry):
-        prepare(two, layer)
-        return carry
+        put_half(ahead.at[4], sent_down(field_at(two, 4)))
+        behind[2] = nothing
+        put_cross(color_apply(link_at(links, 1), 2, sent_down(field_at(two, 2)), False), none)
 
     def third(layer, carry):
         def put(at, value):
-            done[pl.ds(pl.multiple_of(((layer - 2) * 24 + at) * 8, 8), 8)] = value
+            put_done(layer - 2 + 2 * side, at, value)
 
         sweep_layer(two, src, links, layer, get_half(ahead, layer + 1), get_half(behind, layer), put)
         return carry
 
-    lax.fori_loop(1, 3, prepare_two, 0)
     lax.fori_loop(2, 4, third, 0)
-    for layer in range(2):
+    for at in range(24):
+        put_done(3 - 3 * side, at, nothing[0])
+    for layer in range(4):
         for time in range(4):
             for color in range(3):
                 start = (layer * 24 + color * 8) * 8 + 2 * time
@@ -390,7 +410,8 @@
 def project_kernel(phi_ref, vector_ref, out_ref):
     totals = [None, None]
     for color in range(3):
-        rows = phi_ref[:, color * 16 : color * 16 + 16].reshape(8 * 16, SITES)
+        parts = phi_ref[:, color * 16 : color * 16 + 16].reshape(2, 8 * 16, SITES)
+        rows = (parts[0].astype(F32) + parts[1].astype(F32)).astype(BF16)
         for part in range(2):
             value = lax.dot_general(
                 rows,
@@ -445,13 +466,12 @@
     )(clear, moved, entries)
     own = exchange(packed, GROUP)
     vectors = (8, SITES)
-    base, links, near, far = local_call(
+    base, links, near = local_call(
         own_kernel,
         (
             jax.ShapeDtypeStruct((4, 24, *vectors), F32),
             jax.ShapeDtypeStruct((4, LINK, *vectors), F32),
             jax.ShapeDtypeStruct((4 * ROWS + 192, SITES), BF16),
-            jax.ShapeDtypeStruct((96, SITES), BF16),
         ),
         [pltpu.VMEM((16 * ROWS, SITES), F32), pltpu.VMEM((24, *vectors), F32)],
         1 << 20,
@@ -469,11 +489,10 @@
         [],
         1 << 22,
     )(matrix, spectrum, base, links)
-    near = send(near, POSITION, (1, 1))
-    far = send(far, POSITION, (2, 2))
+    near = send(near, POSITION)
     done = local_call(
         sweep_kernel,
-        jax.ShapeDtypeStruct((8, FIELD, SITES), BF16),
+        jax.ShapeDtypeStruct((16, FIELD, SITES), BF16),
         [
             pltpu.VMEM((4 * ROWS, SITES), F32),
             pltpu.VMEM((6, 24, *vectors), F32),
@@ -482,11 +501,11 @@
             pltpu.VMEM((6, LINK, *vectors), F32),
             pltpu.VMEM((7, 12, *vectors), F32),
             pltpu.VMEM((7, 12, *vectors), F32),
-            pltpu.VMEM((2 * 24 * 8, SITES), F32),
+            pltpu.VMEM((4 * 24 * 8, SITES), F32),
         ],
         1 << 24,
-    )(near, far, base, links, inner, ahead, behind)
-    return exchange(done, BLOCK), matrix, spectrum
+    )(near, base, links, inner, ahead, behind)
+    return exchange(done, GROUP), matrix, spectrum
 
 
 def finish_kernel(total_ref, matrix_ref, projected_ref, contracted_ref, rows):

time: 85.2 us -> 85.7 us (level)
  starting transfers between devices: 15.2 us -> 11.8 us
  blocking collectives: 60.8 us -> 63.7 us
  waiting for transfers between devices: 2.65 us -> 4.04 us
    ppermute x2 -> x1, starting transfers between devices: 15.2 us -> 11.8 us  [send(): return lax.ppermute(value, axes, pairs)]
    all_to_all x5, blocking collectives: 60.8 us -> 63.7 us  [exchange(): return lax.all_to_all(value, axes, 0, 0, tiled=True)]
    ppermute x2 -> x1, waiting for transfers between devices: 2.65 us -> 4.04 us  [send(): return lax.ppermute(value, axes, pairs)]
  transfers between devices with their start and end apart: 2 -> 1, of which waited for: 1 -> 1; matrix products, arithmetic and copies ran while one was open for 0% -> 0% of each run, Pallas kernels for 1% -> 1%
where the time goes in v8:
time: 85.7 us; the launch traced here: 85.4 us
  blocking collectives  63.7 us (74%)
  starting transfers between devices  11.8 us (14%)
  Pallas kernels  4.2 us (5%)
  waiting for transfers between devices  4.04 us (5%)
  local copies, waits for them, and re-layouts  0.9 us (1%)
    all_to_all x5, blocking collectives, exchange(): return lax.all_to_all(value, axes, 0, 0, tiled=True)  63.7 us
    ppermute x1, starting transfers between devices, send(): return lax.ppermute(value, axes, pairs)  11.8 us
    ppermute x1, waiting for transfers between devices, send(): return lax.ppermute(value, axes, pairs)  4.04 us
    pallas_call x1, Pallas kernels, spinors(): local_call(sweep_kernel, jax.ShapeDtypeStruct((16, FIELD, SITES), BF16),...  1.89 us
  transfers between devices with their start and end apart: 1, of which 1 were waited for; matrix products, arithmetic and copies ran while one was open for 0% of the time, Pallas kernels for 1%

profile of v8, /device:TPU:8, one launch (start us, length us, event | category | flops | bytes accessed | tf_op | source)
XLA Modules:
  0.0 85.4 jit_solution(10693235785147942929)
XLA Ops:
  0.6 0.0 copy-start.1
  0.6 0.0 copy-start
  0.7 0.0 copy-start.3
  0.7 0.7 copy-done.1
  1.4 0.2 copy-done
  1.5 0.0 copy-start.2
  1.5 0.1 shard_map.60
  1.6 15.9 %all_to_all.25.own_ref = bf16[16,120,128]{2,1,0:T(8,128)(2,1)S(1)} all-to-all(bf16[16,120,128]{2,1,0:T(8,128)(2,1)S(1)} %shard_map.60), channel_id=1, replica_groups=mesh['y_hi'=2,'core'=2,'x'=4,'z_hi'=8,'z_lo'=2,'y_lo'=2] {'z_lo','y_lo',..., dimensions={0} | all-to-all | bytes 983040 | tf_op jit(solution)/shard_map/all_to_all | solution.py:27
  17.5 0.7 shard_map.61
  18.2 11.8 %collective-permute-start = (bf16[672,128]{1,0:T(8,128)(2,1)S(1)}, bf16[672,128]{1,0:T(8,128)(2,1)S(1)}, u32[]{:S(2)}, u32[]{:S(2)}) collective-permute-start(bf16[672,128]{1,0:T(8,128)(2,1)S(1)} %get-tuple-element.12), channel_id=1, source_target_pairs={{0,126},{2,4},{4,2},{6,8},{8,6},{10,12},{12,10},{14,16},{16,14},{1... | collective-permute-start | bytes 516104 | tf_op jit(solution)/shard_map/ppermute | solution.py:33
  30.0 0.0 copy-done.3
  30.0 0.0 copy-done.2
  30.0 0.5 shard_map.62
  30.6 4.0 %collective-permute-done.near_ref = bf16[672,128]{1,0:T(8,128)(2,1)S(1)} collective-permute-done((bf16[672,128]{1,0:T(8,128)(2,1)S(1)}, bf16[672,128]{1,0:T(8,128)(2,1)S(1)}, u32[]{:S(2)}, u32[]{:S(2)}) %collective-permute-start) | collective-permute-done | bytes 172064 | tf_op jit(solution)/shard_map/ppermute | solution.py:33
  34.6 1.9 %shard_map.63 = bf16[16,48,128]{2,1,0:T(8,128)(2,1)S(1)} custom-call(bf16[672,128]{1,0:T(8,128)(2,1)S(1)} %collective-permute-done.near_ref, f32[4,24,8,128]{3,2,1,0:T(8,128)S(1)} %get-tuple-element.13.base_ref, f32[4,72,8,128]{3,2,1,0:T(8,128)S(1)} %get-tuple-element.14.link_ref, f32[2,24,8,128]{3,2,1,0:T(8,128)S(1)} %get-tuple-element.15.inner_ref, ...), custom_call_target="tpu_custom_call" | custom-call | flops 16777216 | bytes 1048576 | tf_op jit(solution)/shard_map/pallas_call | solution.py:493
  36.5 8.9 %all_to_all.26.phi_ref = bf16[16,48,128]{2,1,0:T(8,128)(2,1)S(1)} all-to-all(bf16[16,48,128]{2,1,0:T(8,128)(2,1)S(1)} %shard_map.63), channel_id=1, replica_groups=mesh['y_hi'=2,'core'=2,'x'=4,'z_hi'=8,'z_lo'=2,'y_lo'=2] {'z_lo','y_lo',..., dimensions={0} | all-to-all | bytes 393216 | tf_op jit(solution)/shard_map/all_to_all | solution.py:27
  45.4 0.3 shard_map.64
  45.7 9.4 %all_to_all.27.value_ref = bf16[8,3,4,128]{3,2,1,0:T(4,128)(2,1)S(1)} all-to-all(bf16[8,3,4,128]{3,2,1,0:T(4,128)(2,1)S(1)} %shard_map.64), channel_id=1, replica_groups=mesh['y_hi'=2,'core'=2,'x'=4,'z_hi'=8,'z_lo'=2,'y_lo'=2] {'x','y_lo'}, dimensions={0} | all-to-all | bytes 49152 | tf_op jit(solution)/shard_map/all_to_all | solution.py:27
  55.1 20.9 %all_to_all.28.value_ref = bf16[16,3,4,128]{3,2,1,0:T(4,128)(2,1)S(1)} all-to-all(bf16[16,3,4,128]{3,2,1,0:T(4,128)(2,1)S(1)} %shard_map.65), channel_id=1, replica_groups=mesh['y_hi'=2,'core'=2,'x'=4,'z_hi'=8,'z_lo'=2,'y_lo'=2] {'z_hi','z_lo'}, dimensions={0} | all-to-all | bytes 98304 | tf_op jit(solution)/shard_map/all_to_all | solution.py:27
  76.1 8.6 %all_to_all.29.total_ref = bf16[8,3,4,128]{3,2,1,0:T(4,128)(2,1)S(1)} all-to-all(bf16[8,3,4,128]{3,2,1,0:T(4,128)(2,1)S(1)} %shard_map.66), channel_id=1, replica_groups=mesh['y_hi'=2,'core'=2,'x'=4,'z_hi'=8,'z_lo'=2,'y_lo'=2] {'x','y_lo'}, dimensions={0} | all-to-all | bytes 49152 | tf_op jit(solution)/shard_map/all_to_all | solution.py:27
  84.6 0.7 shard_map.67
  (4 shorter events, 0.1 us)
Async XLA Ops:
  0.6 0.7 copy-start.1
  0.6 0.9 %copy-start = (bf16[1,2,4,3,12,1,128]{6,2,5,4,3,1,0:T(4,128)(2,1)S(1)}, bf16[1,2,4,3,12,1,128]{6,2,5,4,3,1,0:T(4,128)(2,1)}, u32[]{:S(2)}) copy-start(bf16[1,2,4,3,12,1,128]{6,2,5,4,3,1,0:T(4,128)(2,1)} %param.4) | copy-start | bytes 221188
  0.7 29.3 %copy-start.3 = (bf16[1,128,2,3,1,128]{5,2,4,3,1,0:T(2,128)(2,1)S(1)}, bf16[1,128,2,3,1,128]{5,2,4,3,1,0:T(2,128)(2,1)}, u32[]{:S(2)}) copy-start(bf16[1,128,2,3,1,128]{5,2,4,3,1,0:T(2,128)(2,1)} %param.6) | copy-start | bytes 589828
  1.5 28.5 %copy-start.2 = (f32[1,2,1,128]{3,2,1,0:T(1,128)S(1)}, f32[1,2,1,128]{3,2,1,0:T(1,128)}, u32[]{:S(2)}) copy-start(f32[1,2,1,128]{3,2,1,0:T(1,128)} %param.7) | copy-start | bytes 3076
  18.2 16.5 %collective-permute-start = (bf16[672,128]{1,0:T(8,128)(2,1)S(1)}, bf16[672,128]{1,0:T(8,128)(2,1)S(1)}, u32[]{:S(2)}, u32[]{:S(2)}) collective-permute-start(bf16[672,128]{1,0:T(8,128)(2,1)S(1)} %get-tuple-element.12), channel_id=1, source_target_pairs={{0,126},{2,4},{4,2},{6,8},{8,6},{10,12},{12,10},{14,16},{16,14},{1... | collective-permute-start | bytes 516104 | tf_op jit(solution)/shard_map/ppermute | solution.py:33

commit v9 on v7

--- a/solution.py
+++ b/solution.py
@@ -12,8 +12,8 @@
 PLANE = ("x", "y_lo")
 DEPTH = ("z_hi", "z_lo")
 POSITION = ("x", *DEPTH)
-BLOCK = ("y_lo", *TM)
-GROUP = ("z_lo", *BLOCK)
+BLOCK = ("y_hi", "core", "y_lo")
+GROUP = ("y_hi", "y_lo", "core", "z_lo")
 LX = 8
 FIELD = 48
 LINK = 72
@@ -42,6 +42,10 @@
         compiler_params=pltpu.CompilerParams(vmem_limit_bytes=16 << 20),
         cost_estimate=pl.CostEstimate(flops=flops, bytes_accessed=1 << 20, transcendentals=0),
     )
+
+
+def member(high, low, core, position):
+    return high * 8 + low * 4 + core * 2 + position
 
 
 def clear_kernel(out_ref):
@@ -64,9 +68,11 @@
                     else:
                         piece = clear_ref[:4]
                     rows[target, at : at + 4] = piece
-    packed = rows[...].astype(BF16)
-    out_ref[:8] = packed
-    out_ref[8:] = packed
+    for target in range(8):
+        packed = rows[target].astype(BF16)
+        high, core, low = target // 4, target // 2 % 2, target % 2
+        for position in range(2):
+            out_ref[member(high, low, core, position)] = packed
 
 
 def signed_add(base, sign, value):
@@ -230,7 +236,12 @@
 
 
 def own_kernel(own_ref, base_ref, link_ref, near_ref, far_ref, wide, next_ref):
-    wide[...] = own_ref[...].reshape(16 * ROWS, SITES).astype(F32)
+    for layer in range(4):
+        for time in range(4):
+            start = (layer * 4 + time) * ROWS
+            wide[start : start + ROWS] = own_ref[
+                member(time // 2, layer % 2, time % 2, layer // 2)
+            ].astype(F32)
     side = lax.axis_index("z_lo")
 
     def one(layer, carry):
@@ -238,7 +249,8 @@
         return carry
 
     lax.fori_loop(0, 4, one, 0)
-    near_ref[: 4 * ROWS] = own_ref[pl.ds(side * 12, 4)].reshape(4 * ROWS, SITES)
+    edge = pl.ds(pl.multiple_of(side * 12 * ROWS, 8), 4 * ROWS)
+    near_ref[: 4 * ROWS] = wide[edge].astype(BF16)
 
     def put(ref, start, below, above):
         for color in range(3):
@@ -382,7 +394,7 @@
             for color in range(3):
                 start = (layer * 24 + color * 8) * 8 + 2 * time
                 pair = [done[pl.ds(start + which, 8, stride=8)] for which in range(2)]
-                out_ref[layer * 4 + time, color * 16 : color * 16 + 16] = jnp.concatenate(
+                out_ref[time * 2 + layer, color * 16 : color * 16 + 16] = jnp.concatenate(
                     pair, 0
                 ).astype(BF16)
 

time: 85.2 us -> 85 us (level)
  starting transfers between devices: 15.2 us -> 14 us
  blocking collectives: 60.8 us -> 61.8 us
    ppermute x2, starting transfers between devices: 15.2 us -> 14 us  [send(): return lax.ppermute(value, axes, pairs)]
    all_to_all x5, blocking collectives: 60.8 us -> 61.8 us  [exchange(): return lax.all_to_all(value, axes, 0, 0, tiled=True)]
where the time goes in v9:
time: 85 us; the launch traced here: 84.6 us
  blocking collectives  61.8 us (73%)
  starting transfers between devices  14 us (16%)
  Pallas kernels  4.59 us (5%)
  waiting for transfers between devices  2.65 us (3%)
  local copies, waits for them, and re-layouts  0.9 us (1%)
    all_to_all x5, blocking collectives, exchange(): return lax.all_to_all(value, axes, 0, 0, tiled=True)  61.8 us
    ppermute x2, starting transfers between devices, send(): return lax.ppermute(value, axes, pairs)  14 us
    ppermute x2, waiting for transfers between devices, send(): return lax.ppermute(value, axes, pairs)  2.65 us
    pallas_call x1, Pallas kernels, spinors(): local_call(sweep_kernel, jax.ShapeDtypeStruct((8, FIELD, SITES), BF16), [...  2.24 us
  transfers between devices with their start and end apart: 2, of which 1 were waited for; matrix products, arithmetic and copies ran while one was open for 0% of the time, Pallas kernels for 1%

profile of v9, /device:TPU:8, one launch (start us, length us, event | category | flops | bytes accessed | tf_op | source)
XLA Modules:
  0.0 84.6 jit_solution(1558688311067479950)
XLA Ops:
  0.6 0.0 copy-start.1
  0.6 0.0 copy-start
  0.7 0.0 copy-start.3
  0.7 0.7 copy-done.1
  1.4 0.2 copy-done
  1.5 0.0 copy-start.2
  1.5 0.1 shard_map.60
  1.6 16.4 %all_to_all.25.own_ref = bf16[16,120,128]{2,1,0:T(8,128)(2,1)S(1)} all-to-all(bf16[16,120,128]{2,1,0:T(8,128)(2,1)S(1)} %shard_map.60), channel_id=1, replica_groups=mesh['y_hi'=2,'core'=2,'x'=4,'z_hi'=8,'z_lo'=2,'y_lo'=2] {'y_hi','y_lo',..., dimensions={0} | all-to-all | bytes 983040 | tf_op jit(solution)/shard_map/all_to_all | solution.py:27
  18.0 0.7 shard_map.61
  18.7 10.6 %collective-permute-start = (bf16[672,128]{1,0:T(8,128)(2,1)S(1)}, bf16[672,128]{1,0:T(8,128)(2,1)S(1)}, u32[]{:S(2)}, u32[]{:S(2)}) collective-permute-start(bf16[672,128]{1,0:T(8,128)(2,1)S(1)} %get-tuple-element.13), channel_id=1, source_target_pairs={{0,126},{2,4},{4,2},{6,8},{8,6},{10,12},{12,10},{14,16},{16,14},{1... | collective-permute-start | bytes 516104 | tf_op jit(solution)/shard_map/ppermute | solution.py:33
  29.3 3.4 %collective-permute-start.1 = (bf16[96,128]{1,0:T(8,128)(2,1)S(1)}, bf16[96,128]{1,0:T(8,128)(2,1)S(1)}, u32[]{:S(2)}, u32[]{:S(2)}) collective-permute-start(bf16[96,128]{1,0:T(8,128)(2,1)S(1)} %get-tuple-element.14), channel_id=1, source_target_pairs={{0,124},{2,6},{4,0},{6,10},{8,4},{10,14},{12,8},{14,18},{16,12},{1... | collective-permute-start | bytes 73736 | tf_op jit(solution)/shard_map/ppermute | solution.py:33
  32.7 0.0 copy-done.3
  32.7 0.0 copy-done.2
  32.7 0.5 shard_map.62
  33.3 2.7 %collective-permute-done.1.far_ref = bf16[96,128]{1,0:T(8,128)(2,1)S(1)} collective-permute-done((bf16[96,128]{1,0:T(8,128)(2,1)S(1)}, bf16[96,128]{1,0:T(8,128)(2,1)S(1)}, u32[]{:S(2)}, u32[]{:S(2)}) %collective-permute-start.1) | collective-permute-done | bytes 24608 | tf_op jit(solution)/shard_map/ppermute | solution.py:33
  35.9 0.0 collective-permute-done.near_ref
  35.9 2.2 %shard_map.63 = bf16[8,48,128]{2,1,0:T(8,128)(2,1)S(1)} custom-call(bf16[672,128]{1,0:T(8,128)(2,1)S(1)} %collective-permute-done.near_ref, bf16[96,128]{1,0:T(8,128)(2,1)S(1)} %collective-permute-done.1.far_ref, f32[4,24,8,128]{3,2,1,0:T(8,128)S(1)} %get-tuple-element.15.base_ref, f32[4,72,8,128]{3,2,1,0:T(8,128)S(1)} %get-tuple-element.16.link_ref, ...), custom_call_target="tpu_custom_call" | custom-call | flops 16777216 | bytes 1048576 | tf_op jit(solution)/shard_map/pallas_call | solution.py:486
  38.2 8.6 %all_to_all.26.phi_ref = bf16[8,48,128]{2,1,0:T(8,128)(2,1)S(1)} all-to-all(bf16[8,48,128]{2,1,0:T(8,128)(2,1)S(1)} %shard_map.63), channel_id=1, replica_groups=mesh['y_hi'=2,'core'=2,'x'=4,'z_hi'=8,'z_lo'=2,'y_lo'=2] {'y_hi','core',..., dimensions={0} | all-to-all | bytes 196608 | tf_op jit(solution)/shard_map/all_to_all | solution.py:27
  46.8 0.3 shard_map.64
  47.0 8.7 %all_to_all.27.value_ref = bf16[8,3,4,128]{3,2,1,0:T(4,128)(2,1)S(1)} all-to-all(bf16[8,3,4,128]{3,2,1,0:T(4,128)(2,1)S(1)} %shard_map.64), channel_id=1, replica_groups=mesh['y_hi'=2,'core'=2,'x'=4,'z_hi'=8,'z_lo'=2,'y_lo'=2] {'x','y_lo'}, dimensions={0} | all-to-all | bytes 49152 | tf_op jit(solution)/shard_map/all_to_all | solution.py:27
  55.7 19.6 %all_to_all.28.value_ref = bf16[16,3,4,128]{3,2,1,0:T(4,128)(2,1)S(1)} all-to-all(bf16[16,3,4,128]{3,2,1,0:T(4,128)(2,1)S(1)} %shard_map.65), channel_id=1, replica_groups=mesh['y_hi'=2,'core'=2,'x'=4,'z_hi'=8,'z_lo'=2,'y_lo'=2] {'z_hi','z_lo'}, dimensions={0} | all-to-all | bytes 98304 | tf_op jit(solution)/shard_map/all_to_all | solution.py:27
  75.3 8.6 %all_to_all.29.total_ref = bf16[8,3,4,128]{3,2,1,0:T(4,128)(2,1)S(1)} all-to-all(bf16[8,3,4,128]{3,2,1,0:T(4,128)(2,1)S(1)} %shard_map.66), channel_id=1, replica_groups=mesh['y_hi'=2,'core'=2,'x'=4,'z_hi'=8,'z_lo'=2,'y_lo'=2] {'x','y_lo'}, dimensions={0} | all-to-all | bytes 49152 | tf_op jit(solution)/shard_map/all_to_all | solution.py:27
  83.9 0.7 shard_map.67
  (4 shorter events, 0.1 us)
Async XLA Ops:
  0.6 0.7 copy-start.1
  0.6 0.9 %copy-start = (bf16[1,2,4,3,12,1,128]{6,2,5,4,3,1,0:T(4,128)(2,1)S(1)}, bf16[1,2,4,3,12,1,128]{6,2,5,4,3,1,0:T(4,128)(2,1)}, u32[]{:S(2)}) copy-start(bf16[1,2,4,3,12,1,128]{6,2,5,4,3,1,0:T(4,128)(2,1)} %param.4) | copy-start | bytes 221188
  0.7 32.0 %copy-start.3 = (bf16[1,128,2,3,1,128]{5,2,4,3,1,0:T(2,128)(2,1)S(1)}, bf16[1,128,2,3,1,128]{5,2,4,3,1,0:T(2,128)(2,1)}, u32[]{:S(2)}) copy-start(bf16[1,128,2,3,1,128]{5,2,4,3,1,0:T(2,128)(2,1)} %param.6) | copy-start | bytes 589828
  1.5 31.2 %copy-start.2 = (f32[1,2,1,128]{3,2,1,0:T(1,128)S(1)}, f32[1,2,1,128]{3,2,1,0:T(1,128)}, u32[]{:S(2)}) copy-start(f32[1,2,1,128]{3,2,1,0:T(1,128)} %param.7) | copy-start | bytes 3076
  18.7 17.2 %collective-permute-start = (bf16[672,128]{1,0:T(8,128)(2,1)S(1)}, bf16[672,128]{1,0:T(8,128)(2,1)S(1)}, u32[]{:S(2)}, u32[]{:S(2)}) collective-permute-start(bf16[672,128]{1,0:T(8,128)(2,1)S(1)} %get-tuple-element.13), channel_id=1, source_target_pairs={{0,126},{2,4},{4,2},{6,8},{8,6},{10,12},{12,10},{14,16},{16,14},{1... | collective-permute-start | bytes 516104 | tf_op jit(solution)/shard_map/ppermute | solution.py:33
  29.3 6.6 %collective-permute-start.1 = (bf16[96,128]{1,0:T(8,128)(2,1)S(1)}, bf16[96,128]{1,0:T(8,128)(2,1)S(1)}, u32[]{:S(2)}, u32[]{:S(2)}) collective-permute-start(bf16[96,128]{1,0:T(8,128)(2,1)S(1)} %get-tuple-element.14), channel_id=1, source_target_pairs={{0,124},{2,6},{4,0},{6,10},{8,4},{10,14},{12,8},{14,18},{16,12},{1... | collective-permute-start | bytes 73736 | tf_op jit(solution)/shard_map/ppermute | solution.py:33

commit v10 on v9

--- a/solution.py
+++ b/solution.py
@@ -10,8 +10,8 @@
 TM = ("y_hi", "core")
 SPACE = ("x", "z_hi", "z_lo", "y_lo")
 PLANE = ("x", "y_lo")
-DEPTH = ("z_hi", "z_lo")
-POSITION = ("x", *DEPTH)
+DEPTH = ("z_lo", "z_hi")
+POSITION = ("x", "z_hi", "z_lo")
 BLOCK = ("y_hi", "core", "y_lo")
 GROUP = ("y_hi", "y_lo", "core", "z_lo")
 LX = 8

time: 85 us -> 85.1 us (level)
  no operation moved by 1% of the time
where the time goes in v10:
time: 85.1 us; the launch traced here: 84.8 us
  blocking collectives  62 us (73%)
  starting transfers between devices  14 us (16%)
  Pallas kernels  4.59 us (5%)
  waiting for transfers between devices  2.65 us (3%)
  local copies, waits for them, and re-layouts  0.9 us (1%)
    all_to_all x5, blocking collectives, exchange(): return lax.all_to_all(value, axes, 0, 0, tiled=True)  62 us
    ppermute x2, starting transfers between devices, send(): return lax.ppermute(value, axes, pairs)  14 us
    ppermute x2, waiting for transfers between devices, send(): return lax.ppermute(value, axes, pairs)  2.65 us
    pallas_call x1, Pallas kernels, spinors(): local_call(sweep_kernel, jax.ShapeDtypeStruct((8, FIELD, SITES), BF16), [...  2.24 us
  transfers between devices with their start and end apart: 2, of which 1 were waited for; matrix products, arithmetic and copies ran while one was open for 0% of the time, Pallas kernels for 1%

profile of v10, /device:TPU:8, one launch (start us, length us, event | category | flops | bytes accessed | tf_op | source)
XLA Modules:
  0.0 84.8 jit_solution(120922466957816560)
XLA Ops:
  0.6 0.0 copy-start.1
  0.6 0.0 copy-start
  0.7 0.0 copy-start.3
  0.7 0.7 copy-done.1
  1.4 0.2 copy-done
  1.5 0.0 copy-start.2
  1.5 0.1 shard_map.60
  1.6 16.4 %all_to_all.25.own_ref = bf16[16,120,128]{2,1,0:T(8,128)(2,1)S(1)} all-to-all(bf16[16,120,128]{2,1,0:T(8,128)(2,1)S(1)} %shard_map.60), channel_id=1, replica_groups=mesh['y_hi'=2,'core'=2,'x'=4,'z_hi'=8,'z_lo'=2,'y_lo'=2] {'y_hi','y_lo',..., dimensions={0} | all-to-all | bytes 983040 | tf_op jit(solution)/shard_map/all_to_all | solution.py:27
  18.0 0.7 shard_map.61
  18.7 10.6 %collective-permute-start = (bf16[672,128]{1,0:T(8,128)(2,1)S(1)}, bf16[672,128]{1,0:T(8,128)(2,1)S(1)}, u32[]{:S(2)}, u32[]{:S(2)}) collective-permute-start(bf16[672,128]{1,0:T(8,128)(2,1)S(1)} %get-tuple-element.13), channel_id=1, source_target_pairs={{0,126},{2,4},{4,2},{6,8},{8,6},{10,12},{12,10},{14,16},{16,14},{1... | collective-permute-start | bytes 516104 | tf_op jit(solution)/shard_map/ppermute | solution.py:33
  29.3 3.4 %collective-permute-start.1 = (bf16[96,128]{1,0:T(8,128)(2,1)S(1)}, bf16[96,128]{1,0:T(8,128)(2,1)S(1)}, u32[]{:S(2)}, u32[]{:S(2)}) collective-permute-start(bf16[96,128]{1,0:T(8,128)(2,1)S(1)} %get-tuple-element.14), channel_id=1, source_target_pairs={{0,124},{2,6},{4,0},{6,10},{8,4},{10,14},{12,8},{14,18},{16,12},{1... | collective-permute-start | bytes 73736 | tf_op jit(solution)/shard_map/ppermute | solution.py:33
  32.7 0.0 copy-done.3
  32.7 0.0 copy-done.2
  32.7 0.5 shard_map.62
  33.3 2.7 %collective-permute-done.1.far_ref = bf16[96,128]{1,0:T(8,128)(2,1)S(1)} collective-permute-done((bf16[96,128]{1,0:T(8,128)(2,1)S(1)}, bf16[96,128]{1,0:T(8,128)(2,1)S(1)}, u32[]{:S(2)}, u32[]{:S(2)}) %collective-permute-start.1) | collective-permute-done | bytes 24608 | tf_op jit(solution)/shard_map/ppermute | solution.py:33
  35.9 0.0 collective-permute-done.near_ref
  35.9 2.2 %shard_map.63 = bf16[8,48,128]{2,1,0:T(8,128)(2,1)S(1)} custom-call(bf16[672,128]{1,0:T(8,128)(2,1)S(1)} %collective-permute-done.near_ref, bf16[96,128]{1,0:T(8,128)(2,1)S(1)} %collective-permute-done.1.far_ref, f32[4,24,8,128]{3,2,1,0:T(8,128)S(1)} %get-tuple-element.15.base_ref, f32[4,72,8,128]{3,2,1,0:T(8,128)S(1)} %get-tuple-element.16.link_ref, ...), custom_call_target="tpu_custom_call" | custom-call | flops 16777216 | bytes 1048576 | tf_op jit(solution)/shard_map/pallas_call | solution.py:486
  38.2 8.6 %all_to_all.26.phi_ref = bf16[8,48,128]{2,1,0:T(8,128)(2,1)S(1)} all-to-all(bf16[8,48,128]{2,1,0:T(8,128)(2,1)S(1)} %shard_map.63), channel_id=1, replica_groups=mesh['y_hi'=2,'core'=2,'x'=4,'z_hi'=8,'z_lo'=2,'y_lo'=2] {'y_hi','core',..., dimensions={0} | all-to-all | bytes 196608 | tf_op jit(solution)/shard_map/all_to_all | solution.py:27
  46.8 0.3 shard_map.64
  47.0 8.7 %all_to_all.27.value_ref = bf16[8,3,4,128]{3,2,1,0:T(4,128)(2,1)S(1)} all-to-all(bf16[8,3,4,128]{3,2,1,0:T(4,128)(2,1)S(1)} %shard_map.64), channel_id=1, replica_groups=mesh['y_hi'=2,'core'=2,'x'=4,'z_hi'=8,'z_lo'=2,'y_lo'=2] {'x','y_lo'}, dimensions={0} | all-to-all | bytes 49152 | tf_op jit(solution)/shard_map/all_to_all | solution.py:27
  55.7 19.7 %all_to_all.28.value_ref = bf16[16,3,4,128]{3,2,1,0:T(4,128)(2,1)S(1)} all-to-all(bf16[16,3,4,128]{3,2,1,0:T(4,128)(2,1)S(1)} %shard_map.65), channel_id=1, replica_groups=mesh['y_hi'=2,'core'=2,'x'=4,'z_hi'=8,'z_lo'=2,'y_lo'=2] {'z_lo','z_hi'}, dimensions={0} | all-to-all | bytes 98304 | tf_op jit(solution)/shard_map/all_to_all | solution.py:27
  75.5 8.6 %all_to_all.29.total_ref = bf16[8,3,4,128]{3,2,1,0:T(4,128)(2,1)S(1)} all-to-all(bf16[8,3,4,128]{3,2,1,0:T(4,128)(2,1)S(1)} %shard_map.66), channel_id=1, replica_groups=mesh['y_hi'=2,'core'=2,'x'=4,'z_hi'=8,'z_lo'=2,'y_lo'=2] {'x','y_lo'}, dimensions={0} | all-to-all | bytes 49152 | tf_op jit(solution)/shard_map/all_to_all | solution.py:27
  84.1 0.7 shard_map.67
  (4 shorter events, 0.1 us)
Async XLA Ops:
  0.6 0.7 copy-start.1
  0.6 0.9 %copy-start = (bf16[1,2,4,3,12,1,128]{6,2,5,4,3,1,0:T(4,128)(2,1)S(1)}, bf16[1,2,4,3,12,1,128]{6,2,5,4,3,1,0:T(4,128)(2,1)}, u32[]{:S(2)}) copy-start(bf16[1,2,4,3,12,1,128]{6,2,5,4,3,1,0:T(4,128)(2,1)} %param.4) | copy-start | bytes 221188
  0.7 32.0 %copy-start.3 = (bf16[1,128,2,3,1,128]{5,2,4,3,1,0:T(2,128)(2,1)S(1)}, bf16[1,128,2,3,1,128]{5,2,4,3,1,0:T(2,128)(2,1)}, u32[]{:S(2)}) copy-start(bf16[1,128,2,3,1,128]{5,2,4,3,1,0:T(2,128)(2,1)} %param.6) | copy-start | bytes 589828
  1.5 31.2 %copy-start.2 = (f32[1,2,1,128]{3,2,1,0:T(1,128)S(1)}, f32[1,2,1,128]{3,2,1,0:T(1,128)}, u32[]{:S(2)}) copy-start(f32[1,2,1,128]{3,2,1,0:T(1,128)} %param.7) | copy-start | bytes 3076
  18.7 17.2 %collective-permute-start = (bf16[672,128]{1,0:T(8,128)(2,1)S(1)}, bf16[672,128]{1,0:T(8,128)(2,1)S(1)}, u32[]{:S(2)}, u32[]{:S(2)}) collective-permute-start(bf16[672,128]{1,0:T(8,128)(2,1)S(1)} %get-tuple-element.13), channel_id=1, source_target_pairs={{0,126},{2,4},{4,2},{6,8},{8,6},{10,12},{12,10},{14,16},{16,14},{1... | collective-permute-start | bytes 516104 | tf_op jit(solution)/shard_map/ppermute | solution.py:33
  29.3 6.6 %collective-permute-start.1 = (bf16[96,128]{1,0:T(8,128)(2,1)S(1)}, bf16[96,128]{1,0:T(8,128)(2,1)S(1)}, u32[]{:S(2)}, u32[]{:S(2)}) collective-permute-start(bf16[96,128]{1,0:T(8,128)(2,1)S(1)} %get-tuple-element.14), channel_id=1, source_target_pairs={{0,124},{2,6},{4,0},{6,10},{8,4},{10,14},{12,8},{14,18},{16,12},{1... | collective-permute-start | bytes 73736 | tf_op jit(solution)/shard_map/ppermute | solution.py:33

commit v11 on v9

--- a/solution.py
+++ b/solution.py
@@ -9,7 +9,7 @@
 HOPPING = 0.125
 TM = ("y_hi", "core")
 SPACE = ("x", "z_hi", "z_lo", "y_lo")
-PLANE = ("x", "y_lo")
+PLANE = ("y_lo", "x")
 DEPTH = ("z_hi", "z_lo")
 POSITION = ("x", *DEPTH)
 BLOCK = ("y_hi", "core", "y_lo")

time: 85 us -> 85.1 us (level)
  the two profiles are of different devices: /device:TPU:8 before, /device:TPU:2 now
where the time goes in v11:
time: 85.1 us; the launch traced here: 84.8 us
  blocking collectives  61.6 us (72%)
  starting transfers between devices  14.3 us (17%)
  Pallas kernels  4.6 us (5%)
  waiting for transfers between devices  2.65 us (3%)
  local copies, waits for them, and re-layouts  0.9 us (1%)
    all_to_all x5, blocking collectives, exchange(): return lax.all_to_all(value, axes, 0, 0, tiled=True)  61.6 us
    ppermute x2, starting transfers between devices, send(): return lax.ppermute(value, axes, pairs)  14.3 us
    ppermute x2, waiting for transfers between devices, send(): return lax.ppermute(value, axes, pairs)  2.65 us
    pallas_call x1, Pallas kernels, spinors(): local_call(sweep_kernel, jax.ShapeDtypeStruct((8, FIELD, SITES), BF16), [...  2.24 us
  transfers between devices with their start and end apart: 2, of which 1 were waited for; matrix products, arithmetic and copies ran while one was open for 0% of the time, Pallas kernels for 1%

profile of v11, /device:TPU:2, one launch (start us, length us, event | category | flops | bytes accessed | tf_op | source)
XLA Modules:
  0.0 84.8 jit_solution(10391787384955177942)
XLA Ops:
  0.6 0.0 copy-start.1
  0.6 0.0 copy-start
  0.7 0.0 copy-start.3
  0.7 0.7 copy-done.1
  1.4 0.2 copy-done
  1.5 0.0 copy-start.2
  1.5 0.1 shard_map.60
  1.6 15.3 %all_to_all.25.own_ref = bf16[16,120,128]{2,1,0:T(8,128)(2,1)S(1)} all-to-all(bf16[16,120,128]{2,1,0:T(8,128)(2,1)S(1)} %shard_map.60), channel_id=1, replica_groups=mesh['y_hi'=2,'core'=2,'x'=4,'z_hi'=8,'z_lo'=2,'y_lo'=2] {'y_hi','y_lo',..., dimensions={0} | all-to-all | bytes 983040 | tf_op jit(solution)/shard_map/all_to_all | solution.py:27
  16.9 0.7 shard_map.61
  17.6 10.9 %collective-permute-start = (bf16[672,128]{1,0:T(8,128)(2,1)S(1)}, bf16[672,128]{1,0:T(8,128)(2,1)S(1)}, u32[]{:S(2)}, u32[]{:S(2)}) collective-permute-start(bf16[672,128]{1,0:T(8,128)(2,1)S(1)} %get-tuple-element.13), channel_id=1, source_target_pairs={{0,126},{2,4},{4,2},{6,8},{8,6},{10,12},{12,10},{14,16},{16,14},{1... | collective-permute-start | bytes 516104 | tf_op jit(solution)/shard_map/ppermute | solution.py:33
  28.5 3.4 %collective-permute-start.1 = (bf16[96,128]{1,0:T(8,128)(2,1)S(1)}, bf16[96,128]{1,0:T(8,128)(2,1)S(1)}, u32[]{:S(2)}, u32[]{:S(2)}) collective-permute-start(bf16[96,128]{1,0:T(8,128)(2,1)S(1)} %get-tuple-element.14), channel_id=1, source_target_pairs={{0,124},{2,6},{4,0},{6,10},{8,4},{10,14},{12,8},{14,18},{16,12},{1... | collective-permute-start | bytes 73736 | tf_op jit(solution)/shard_map/ppermute | solution.py:33
  31.9 0.0 copy-done.3
  31.9 0.0 copy-done.2
  31.9 0.5 shard_map.62
  32.5 2.7 %collective-permute-done.1.far_ref = bf16[96,128]{1,0:T(8,128)(2,1)S(1)} collective-permute-done((bf16[96,128]{1,0:T(8,128)(2,1)S(1)}, bf16[96,128]{1,0:T(8,128)(2,1)S(1)}, u32[]{:S(2)}, u32[]{:S(2)}) %collective-permute-start.1) | collective-permute-done | bytes 24608 | tf_op jit(solution)/shard_map/ppermute | solution.py:33
  35.1 0.0 collective-permute-done.near_ref
  35.1 2.2 %shard_map.63 = bf16[8,48,128]{2,1,0:T(8,128)(2,1)S(1)} custom-call(bf16[672,128]{1,0:T(8,128)(2,1)S(1)} %collective-permute-done.near_ref, bf16[96,128]{1,0:T(8,128)(2,1)S(1)} %collective-permute-done.1.far_ref, f32[4,24,8,128]{3,2,1,0:T(8,128)S(1)} %get-tuple-element.15.base_ref, f32[4,72,8,128]{3,2,1,0:T(8,128)S(1)} %get-tuple-element.16.link_ref, ...), custom_call_target="tpu_custom_call" | custom-call | flops 16777216 | bytes 1048576 | tf_op jit(solution)/shard_map/pallas_call | solution.py:486
  37.4 8.2 %all_to_all.26.phi_ref = bf16[8,48,128]{2,1,0:T(8,128)(2,1)S(1)} all-to-all(bf16[8,48,128]{2,1,0:T(8,128)(2,1)S(1)} %shard_map.63), channel_id=1, replica_groups=mesh['y_hi'=2,'core'=2,'x'=4,'z_hi'=8,'z_lo'=2,'y_lo'=2] {'y_hi','core',..., dimensions={0} | all-to-all | bytes 196608 | tf_op jit(solution)/shard_map/all_to_all | solution.py:27
  45.6 0.3 shard_map.64
  45.8 10.0 %all_to_all.27.value_ref = bf16[8,3,4,128]{3,2,1,0:T(4,128)(2,1)S(1)} all-to-all(bf16[8,3,4,128]{3,2,1,0:T(4,128)(2,1)S(1)} %shard_map.64), channel_id=1, replica_groups=mesh['y_hi'=2,'core'=2,'x'=4,'z_hi'=8,'z_lo'=2,'y_lo'=2] {'y_lo','x'}, dimensions={0} | all-to-all | bytes 49152 | tf_op jit(solution)/shard_map/all_to_all | solution.py:27
  55.8 19.5 %all_to_all.28.value_ref = bf16[16,3,4,128]{3,2,1,0:T(4,128)(2,1)S(1)} all-to-all(bf16[16,3,4,128]{3,2,1,0:T(4,128)(2,1)S(1)} %shard_map.65), channel_id=1, replica_groups=mesh['y_hi'=2,'core'=2,'x'=4,'z_hi'=8,'z_lo'=2,'y_lo'=2] {'z_hi','z_lo'}, dimensions={0} | all-to-all | bytes 98304 | tf_op jit(solution)/shard_map/all_to_all | solution.py:27
  75.4 8.7 %all_to_all.29.total_ref = bf16[8,3,4,128]{3,2,1,0:T(4,128)(2,1)S(1)} all-to-all(bf16[8,3,4,128]{3,2,1,0:T(4,128)(2,1)S(1)} %shard_map.66), channel_id=1, replica_groups=mesh['y_hi'=2,'core'=2,'x'=4,'z_hi'=8,'z_lo'=2,'y_lo'=2] {'y_lo','x'}, dimensions={0} | all-to-all | bytes 49152 | tf_op jit(solution)/shard_map/all_to_all | solution.py:27
  84.0 0.7 shard_map.67
  (4 shorter events, 0.1 us)
Async XLA Ops:
  0.6 0.7 copy-start.1
  0.6 0.9 %copy-start = (bf16[1,2,4,3,12,1,128]{6,2,5,4,3,1,0:T(4,128)(2,1)S(1)}, bf16[1,2,4,3,12,1,128]{6,2,5,4,3,1,0:T(4,128)(2,1)}, u32[]{:S(2)}) copy-start(bf16[1,2,4,3,12,1,128]{6,2,5,4,3,1,0:T(4,128)(2,1)} %param.4) | copy-start | bytes 221188
  0.7 31.2 %copy-start.3 = (bf16[1,128,2,3,1,128]{5,2,4,3,1,0:T(2,128)(2,1)S(1)}, bf16[1,128,2,3,1,128]{5,2,4,3,1,0:T(2,128)(2,1)}, u32[]{:S(2)}) copy-start(bf16[1,128,2,3,1,128]{5,2,4,3,1,0:T(2,128)(2,1)} %param.6) | copy-start | bytes 589828
  1.5 30.4 %copy-start.2 = (f32[1,2,1,128]{3,2,1,0:T(1,128)S(1)}, f32[1,2,1,128]{3,2,1,0:T(1,128)}, u32[]{:S(2)}) copy-start(f32[1,2,1,128]{3,2,1,0:T(1,128)} %param.7) | copy-start | bytes 3076
  17.6 17.6 %collective-permute-start = (bf16[672,128]{1,0:T(8,128)(2,1)S(1)}, bf16[672,128]{1,0:T(8,128)(2,1)S(1)}, u32[]{:S(2)}, u32[]{:S(2)}) collective-permute-start(bf16[672,128]{1,0:T(8,128)(2,1)S(1)} %get-tuple-element.13), channel_id=1, source_target_pairs={{0,126},{2,4},{4,2},{6,8},{8,6},{10,12},{12,10},{14,16},{16,14},{1... | collective-permute-start | bytes 516104 | tf_op jit(solution)/shard_map/ppermute | solution.py:33
  28.5 6.6 %collective-permute-start.1 = (bf16[96,128]{1,0:T(8,128)(2,1)S(1)}, bf16[96,128]{1,0:T(8,128)(2,1)S(1)}, u32[]{:S(2)}, u32[]{:S(2)}) collective-permute-start(bf16[96,128]{1,0:T(8,128)(2,1)S(1)} %get-tuple-element.14), channel_id=1, source_target_pairs={{0,124},{2,6},{4,0},{6,10},{8,4},{10,14},{12,8},{14,18},{16,12},{1... | collective-permute-start | bytes 73736 | tf_op jit(solution)/shard_map/ppermute | solution.py:33
